TPU v7x, 256 devices: a whole 4x4x8 slice. The times are simulated.
256 devices in a mesh: dp: 8 (over z), tensor: 32 (over y, x, core).
Axes of the slice: x: 4, y: 4, z: 8, core: 2. Of those that a mesh axis runs over, the one named last changes fastest.
Arguments:
- hidden: bfloat16 [16384, 1536], P(('dp', 'tensor')), parts along dimension 0, may hold values from -6 to 6
- segment_ids: int32 [16384], P('dp'), parts along dimension 0, may hold values from 0 to 5, never falling along the last dimension, each value on 1 to 1024 neighbouring positions
- routes: int32 [16384, 8], P(('dp', 'tensor')), parts along dimension 0, may hold values from 0 to 39, all different within a row; in each aligned block of 512 rows (0 to 511, 512 to 1023, ...) at most 204 rows name the same one
- route_weights: bfloat16 [16384, 8], P(('dp', 'tensor')), parts along dimension 0, may hold values from 0.099609375 to 1
- attn_gain: float32 [1536], replicated, may hold values from 0.1 to 1.9
- w_qkv: bfloat16 [1536, 2560], P(None, 'tensor')
- w_out: bfloat16 [1536, 1536], P(None, 'tensor'), may hold values from -0.15625 to 0.15625
- ffn_gain: float32 [1536], replicated, may hold values from 0.1 to 1.9
- w_gate_up: bfloat16 [160, 1536, 256], P('tensor'), may hold values from -0.15625 to 0.15625
- w_down: bfloat16 [160, 128, 1536], P('tensor'), may hold values from -0.25 to 0.25
Outputs:
- after_attention: bfloat16 [16384, 1536], P(('dp', 'tensor')), parts along dimension 0
- hidden_out: bfloat16 [16384, 1536], P(('dp', 'tensor')), parts along dimension 0
- kv_cache: bfloat16 [32, 4096, 128], P('tensor', 'dp'), parts along dimension 1
There are 8 independent parts, one for each index of `dp`. A program takes and returns all parts, laid end to end along the dimension named above; an argument that names none is the same for every part. Nothing has to cross between parts.
Inputs may be any that keep to these rules, and one draw needn't show every extreme that they name: `segment_ids`: prompt numbers never fall along the sequence; each prompt has 1 to 1024 tokens, one exactly 1024. `routes`: each token names 8 different experts. In each aligned block of 512 tokens no expert is named by more than 204 tokens, a bound that some block reaches.
All inputs are finite; a program needn't handle non-finite values.
Results may differ from a plain program's by a relative error of at most 0.0075.
Values may be sent and summed in bfloat16 or wider, within the bound.
A program may use at most 128 MiB of HBM per device.

v0:
```python
import math

import jax
import jax.numpy as jnp
from jax import lax
from jax.sharding import PartitionSpec as P

KVH = 8
HD = 64
GQ = 3


attn_scale = 0.015625
residual_scale = 0.22
rope_base = 10000.0
norm_eps = 1e-06
masked_floor = -1e30


def partner(value, axis, apart):
    mask = 2**apart
    pairs = [(source, source ^ mask) for source in range(lax.axis_size(axis))]
    return lax.ppermute(value, axis, pairs)


def rms_norm(row_block, gain_row):
    widened = row_block.astype(jnp.float32)
    mean_square = jnp.mean(widened * widened, axis=-1, keepdims=True)
    return (widened * lax.rsqrt(mean_square + norm_eps) * gain_row).astype(jnp.bfloat16)


def segment_starts(segment_ids):
    places = jnp.arange(segment_ids.shape[0], dtype=jnp.int32)
    earlier = jnp.concatenate([segment_ids[:1] - 1, segment_ids[:-1]])
    boundary = jnp.where(segment_ids != earlier, places, jnp.zeros_like(places))
    return lax.cummax(boundary, axis=0)


def rotate(vectors, positions):
    half_width = vectors.shape[-1] // 2
    freq_steps = jnp.arange(half_width, dtype=jnp.float32)
    frequency = jnp.exp(freq_steps * (-2.0 * math.log(rope_base) / vectors.shape[-1]))
    angles = positions.astype(jnp.float32)[:, None] * frequency[None, :]
    cosine = jnp.cos(angles)[:, None, :]
    sine_part = jnp.sin(angles)[:, None, :]
    first_half = vectors[..., :half_width]
    second_half = vectors[..., half_width:]
    return jnp.concatenate(
        [
            first_half * cosine - second_half * sine_part,
            second_half * cosine + first_half * sine_part,
        ],
        axis=-1,
    )


def gather_levels(parts, level_bits, join_axes, sender):
    index_now = lax.axis_index("tensor")
    for level_bit in level_bits:
        arrived = sender(parts, level_bit)
        is_upper = index_now >> level_bit & 1 == 1
        joined_parts = []
        for own_part, peer_part, join_axis in zip(parts, arrived, join_axes):
            lower_first = jnp.concatenate([own_part, peer_part], join_axis)
            upper_first = jnp.concatenate([peer_part, own_part], join_axis)
            joined_parts.append(jnp.where(is_upper, upper_first, lower_first))
        parts = tuple(joined_parts)
    return parts


def fold_levels(partial_sum, level_bits, sender):
    index_now = lax.axis_index("tensor")
    for level_bit in reversed(level_bits):
        half_rows = partial_sum.shape[0] // 2
        lower_rows = partial_sum[:half_rows]
        upper_rows = partial_sum[half_rows:]
        is_upper = index_now >> level_bit & 1 == 1
        kept_rows = jnp.where(is_upper, upper_rows, lower_rows)
        sent_rows = jnp.where(is_upper, lower_rows, upper_rows)
        partial_sum = kept_rows + sender(sent_rows, level_bit)
    return partial_sum


def project_pairs(row_block, w_pairs, positions):
    head_size = w_pairs.shape[1] // 2
    paired = jnp.dot(row_block, w_pairs, preferred_element_type=jnp.float32)
    rotated = rotate(paired[:, None, :head_size], positions)[:, 0]
    return jnp.concatenate([rotated, paired[:, head_size:]], axis=1).astype(jnp.bfloat16)


def expert_term(inputs, routes, route_weights, gate_up, down_proj, first_expert, capacity):
    row_count = inputs.shape[0]
    model_width = inputs.shape[1]
    expert_count = gate_up.shape[0]
    inner_width = down_proj.shape[1]
    expert_ids = first_expert + jnp.arange(expert_count, dtype=jnp.int32)
    matches = routes[:, None, :] == expert_ids[None, :, None]
    chosen = jnp.any(matches, axis=2)
    shares = jnp.sum(jnp.where(matches, route_weights.astype(jnp.float32)[:, None, :], 0.0), axis=2)
    ranks = jnp.cumsum(chosen.astype(jnp.int32), axis=0) - 1
    targets = jnp.where(chosen, ranks, capacity)
    row_ids = jnp.broadcast_to(
        jnp.arange(row_count, dtype=jnp.int32)[:, None], (row_count, expert_count)
    )
    column_ids = jnp.broadcast_to(
        jnp.arange(expert_count, dtype=jnp.int32)[None, :], (row_count, expert_count)
    )
    slot_table = (
        jnp.full((expert_count, capacity + 1), row_count, jnp.int32)
        .at[column_ids, targets]
        .set(row_ids)[:, :capacity]
    )
    padded_in = jnp.concatenate([inputs, jnp.zeros((1, model_width), inputs.dtype)], axis=0)
    padded_share = jnp.concatenate([shares, jnp.zeros((1, expert_count), jnp.float32)], axis=0)
    picked = padded_in[slot_table]
    slot_share = jnp.take_along_axis(padded_share.T, slot_table, axis=1)
    gate_up_out = jnp.einsum("ecd,edf->ecf", picked, gate_up, preferred_element_type=jnp.float32)
    inner_act = (
        jax.nn.silu(gate_up_out[..., :inner_width]) * gate_up_out[..., inner_width:]
    ).astype(jnp.bfloat16)
    produced = (
        jnp.einsum("ecf,efd->ecd", inner_act, down_proj, preferred_element_type=jnp.float32)
        * slot_share[..., None]
    )
    summed = (
        jnp.zeros((row_count + 1, model_width), jnp.float32)
        .at[slot_table.reshape(-1)]
        .add(produced.reshape(-1, model_width))
    )
    return summed[:row_count]


def on_device(
    hidden, segment_ids, routes, route_weights, attn_gain, w_qkv, w_out, ffn_gain, w_gate_up, w_down
):
    device_count = lax.axis_size("tensor")
    quarters = device_count // KVH
    index_now = lax.axis_index("tensor")
    quarter_index = index_now // KVH
    group_index = index_now % KVH
    group_bits = list(range(KVH.bit_length() - 1))
    quarter_bits = list(range(len(group_bits), device_count.bit_length() - 1))
    seq_len = segment_ids.shape[0]
    rows_quarter = seq_len // quarters
    model_width = hidden.shape[1]
    starts = segment_starts(segment_ids)
    positions = jnp.arange(seq_len, dtype=jnp.int32) - starts
    own_positions = lax.dynamic_slice_in_dim(
        positions, quarter_index * rows_quarter, rows_quarter, 0
    )
    normed = rms_norm(hidden, attn_gain)
    qkv_width = w_qkv.shape[1]
    joined = jnp.concatenate([w_qkv, w_out], axis=1)
    (gathered_cols,) = gather_levels(
        (joined,),
        quarter_bits,
        (1,),
        lambda payload, level_bit: (partner(payload[0], "tensor", level_bit),),
    )
    by_quarter = gathered_cols.reshape(model_width, quarters, joined.shape[1])
    w_group = by_quarter[:, :, :qkv_width].reshape(model_width, quarters * qkv_width)
    w_attn_out = by_quarter[:, :, qkv_width:].reshape(model_width, GQ * HD)
    w_query = w_group[:, : GQ * HD]
    w_pairs = w_group[:, GQ * HD :]
    all_rows = lax.all_gather(normed, "tensor", axis=0, tiled=True)
    own_rows = lax.dynamic_slice_in_dim(all_rows, quarter_index * rows_quarter, rows_quarter, 0)
    key_values = project_pairs(all_rows, w_pairs, positions)
    kv_block = lax.dynamic_slice_in_dim(key_values, quarter_index * rows_quarter, rows_quarter, 0)
    query_proj = jnp.dot(own_rows, w_query, preferred_element_type=jnp.float32).reshape(
        rows_quarter, GQ, HD
    )
    queries_heads = rotate(query_proj, own_positions).astype(jnp.bfloat16).transpose(1, 0, 2)
    block_rows = min(256, rows_quarter)
    key_block = min(512, seq_len)

    def attend(block_number):
        first_row = block_number * block_rows
        block_queries = lax.dynamic_slice_in_dim(queries_heads, first_row, block_rows, 1).reshape(
            GQ * block_rows, HD
        )
        first_place = quarter_index * rows_quarter + first_row
        query_places = first_place + jnp.arange(block_rows, dtype=jnp.int32)
        query_starts = lax.dynamic_slice_in_dim(starts, first_place, block_rows, 0)
        lowest = query_starts[0] // key_block
        highest = (first_place + block_rows - 1) // key_block + 1

        def step_keys(key_number, loop_state):
            row_peak, totals, accumulated = loop_state
            key_offset = key_number * key_block
            block_pairs = lax.dynamic_slice_in_dim(key_values, key_offset, key_block, 0)
            key_places = key_offset + jnp.arange(key_block, dtype=jnp.int32)
            allowed = (key_places[None, :] <= query_places[:, None]) & (
                key_places[None, :] >= query_starts[:, None]
            )
            scores = (
                lax.dot_general(
                    block_queries,
                    block_pairs[:, :HD],
                    (((1,), (1,)), ((), ())),
                    preferred_element_type=jnp.float32,
                )
                * attn_scale
            )
            scores = jnp.where(jnp.tile(allowed, (GQ, 1)), scores, -jnp.inf)
            new_peak = jnp.maximum(row_peak, jnp.max(scores, axis=1))
            weights = jnp.exp(scores - new_peak[:, None])
            factor = jnp.exp(row_peak - new_peak)
            totals = totals * factor + jnp.sum(weights, axis=1)
            accumulated = accumulated * factor[:, None] + jnp.dot(
                weights.astype(jnp.bfloat16),
                block_pairs[:, HD:],
                preferred_element_type=jnp.float32,
            )
            return (new_peak, totals, accumulated)

        start_state = (
            jnp.full((GQ * block_rows,), masked_floor, jnp.float32),
            jnp.zeros((GQ * block_rows,), jnp.float32),
            jnp.zeros((GQ * block_rows, HD), jnp.float32),
        )
        row_peak, totals, accumulated = lax.fori_loop(lowest, highest, step_keys, start_state)
        mixed = (accumulated / totals[:, None]).astype(jnp.bfloat16).reshape(GQ, block_rows, HD)
        return mixed.transpose(1, 0, 2).reshape(block_rows, GQ * HD)

    attended = lax.map(attend, jnp.arange(rows_quarter // block_rows, dtype=jnp.int32)).reshape(
        rows_quarter, GQ * HD
    )
    partial_proj = lax.dot_general(
        attended, w_attn_out, (((1,), (1,)), ((), ())), preferred_element_type=jnp.float32
    )
    projection = fold_levels(
        partial_proj,
        group_bits,
        lambda sent_rows, level_bit: partner(
            sent_rows.astype(jnp.bfloat16), "tensor", level_bit
        ).astype(sent_rows.dtype),
    )
    after_attention = (hidden.astype(jnp.float32) + residual_scale * projection).astype(
        jnp.bfloat16
    )
    expert_in = rms_norm(after_attention, ffn_gain)
    local_experts = w_gate_up.shape[0]
    capacity = 2 * rows_quarter // 5
    rows_all, routes_all, shares_all = (
        lax.all_gather(expert_in, "tensor", axis=0, tiled=True),
        lax.all_gather(routes, "tensor", axis=0, tiled=True),
        lax.all_gather(route_weights, "tensor", axis=0, tiled=True),
    )
    expert_part = expert_term(
        rows_all,
        routes_all,
        shares_all,
        w_gate_up,
        w_down,
        group_index * local_experts,
        quarters * capacity,
    )
    expert_sum = lax.psum_scatter(
        expert_part.astype(jnp.bfloat16), "tensor", scatter_dimension=0, tiled=True
    ).astype(jnp.float32)
    hidden_out = (after_attention.astype(jnp.float32) + residual_scale * expert_sum).astype(
        jnp.bfloat16
    )
    return (after_attention, hidden_out, kv_block[None])


def solution(mesh):
    placed = (
        P(("dp", "tensor"), None),
        P("dp"),
        P(("dp", "tensor"), None),
        P(("dp", "tensor"), None),
        P(),
        P(None, "tensor"),
        P(None, "tensor"),
        P(),
        P("tensor", None, None),
        P("tensor", None, None),
    )
    return jax.shard_map(
        on_device,
        mesh=mesh,
        in_specs=placed,
        out_specs=(P(("dp", "tensor"), None), P(("dp", "tensor"), None), P("tensor", "dp", None)),
        check_vma=False,
    )
```

profile of v0, /device:TPU:24, one launch (start us, length us, event | category | flops | bytes accessed | tf_op | source)
XLA Modules:
  0.0 499.1 jit_solution(2245536383037473471)
XLA Ops:
  15.3 6.9 %collective-permute-done = bf16[1536,128]{0,1:T(8,128)(2,1)S(1)} collective-permute-done((bf16[1536,128]{0,1:T(8,128)(2,1)S(1)}, bf16[1536,128]{0,1:T(8,128)(2,1)S(1)}, u32[]{:S(2)}, u32[]{:S(2)}) %collective-permute-start) | collective-permute-done | bytes 393248 | tf_op jit(solution)/shard_map/ppermute | solution.py:23
  26.8 20.0 %collective-permute-done.1 = bf16[1536,256]{0,1:T(8,128)(2,1)S(1)} collective-permute-done((bf16[1536,256]{0,1:T(8,128)(2,1)S(1)}, bf16[1536,256]{0,1:T(8,128)(2,1)S(1)}, u32[]{:S(2)}, u32[]{:S(2)}) %collective-permute-start.1) | collective-permute-done | bytes 786464 | tf_op jit(solution)/shard_map/ppermute | solution.py:23
  48.0 30.0 %all-gather.5.cloned.1.call-done = bf16[2048,1536]{1,0:T(8,128)(2,1)} async-done(((bf16[64,1536]{1,0:T(8,128)(2,1)}), bf16[2048,1536]{1,0:T(8,128)(2,1)}) %all-gather.5.cloned.1.call-update) | async-done | bytes 6291472 | tf_op jit(solution)/shard_map/all_gather | solution.py:165
  78.0 4.9 fusion.25
  82.9 2.1 fusion.12
  89.3 2.1 copy.61
  93.0 18.6 %while.59 = (s32[]{:T(128)}, bf16[2,256,192]{1,2,0:T(8,128)(2,1)}, s32[2]{0:T(128)S(1)}, s32[]{:T(128)}, s32[2048]{0:T(1024)S(1)}, /*index=5*/bf16[3,512,64]{2,1...) while((s32[]{:T(128)}, bf16[2,256,192]{1,2,0:T(8,128)(2,1)}, ...), condition=%wide.region_8.9_spmd, body=%wide.region_3.8_spmd.sunk | while | flops 104007976 | bytes 10327068 | solution.py:225
  97.4 4.0 while.60
  106.7 4.0 while.60
  116.0 2.0 collective-permute-start.2
  118.0 19.4 %collective-permute-done.2 = bf16[256,1536]{1,0:T(8,128)(2,1)} collective-permute-done((bf16[256,1536]{1,0:T(8,128)(2,1)S(1)}, bf16[256,1536]{1,0:T(8,128)(2,1)}, u32[]{:S(2)}, u32[]{:S(2)}) %collective-permute-start.2) | collective-permute-done | bytes 786464 | tf_op jit(solution)/shard_map/ppermute | solution.py:23
  137.4 2.5 convert_add_fusion
  141.1 10.4 %collective-permute-done.3 = bf16[128,1536]{1,0:T(8,128)(2,1)} collective-permute-done((bf16[128,1536]{1,0:T(8,128)(2,1)}, bf16[128,1536]{1,0:T(8,128)(2,1)}, u32[]{:S(2)}, u32[]{:S(2)}) %collective-permute-start.3) | collective-permute-done | bytes 393248 | tf_op jit(solution)/shard_map/ppermute | solution.py:23
  155.3 22.9 %all-gather.1 = bf16[32,64,8]{1,2,0:T(8,128)(2,1)S(1)} all-gather(bf16[1,64,8]{1,2,0:T(8,128)(2,1)S(1)} %bitcast.110), channel_id=1, replica_groups=mesh['dp'=8,'tensor'=32] {'tensor'}, dimensions={0}, use_global_device_ids=true | all-gather | bytes 33792 | tf_op jit(solution)/shard_map/all_gather | solution.py:247
  178.3 23.7 %all-gather = s32[32,64,8]{1,2,0:T(8,128)S(1)} all-gather(s32[1,64,8]{1,2,0:T(8,128)S(1)} %bitcast.109), channel_id=1, replica_groups=mesh['dp'=8,'tensor'=32] {'tensor'}, dimensions={0}, use_global_device_ids=true | all-gather | bytes 67584 | tf_op jit(solution)/shard_map/all_gather | solution.py:246
  208.0 37.9 %scatter_custom_fusion.1 = s32[4085]{0:T(1024)S(1)} fusion(s32[10240]{0:T(1024)S(1)} %reshape.400, s32[10240]{0:T(1024)S(1)} %reshape.402, s32[]{:T(128)} %constant.223.clone.1), kind=kCustom, calls=%fused_computation.101 | custom fusion | bytes 16344
  247.4 40.4 %gather_fusion.1 = f32[4080]{0:T(1024)S(1)} fusion(f32[5,2049]{0,1:T(8,128)S(1)} %pad_bitcast_fusion, s32[4080]{0:T(1024)S(1)} %reshape.386), kind=kCustom, calls=%fused_computation.1 | custom fusion | bytes 65280 | tf_op jit(solution)/shard_map/jit(take_along_axis)/gather | solution.py:116
  288.1 5.8 %concatenate.56 = bf16[2049,1536]{1,0:T(8,128)(2,1)} pad(bf16[2048,1536]{1,0:T(8,128)(2,1)} %all-gather.7.cloned.1.call-done, bf16[]{:T(256)} %constant.215.clone.1), padding=0_1x0_0 | pad | bytes 12585986 | tf_op jit(solution)/shard_map/concatenate | solution.py:113
  294.0 28.9 %gather_fusion = bf16[4080,1536]{1,0:T(8,128)(2,1)} fusion(bf16[2049,1536]{1,0:T(8,128)(2,1)} %concatenate.56, s32[4096]{0:T(1024)S(1)} %pad_clamp_fusion), kind=kCustom, calls=%fused_computation | custom fusion | bytes 25083840 | tf_op jit(solution)/shard_map/gather | solution.py:115
  322.9 7.6 %fusion.48 = f32[5,816,256]{2,1,0:T(8,128)S(1)} fusion(bf16[5,816,1536]{2,1,0:T(8,128)(2,1)} %bitcast.94, bf16[5,1536,256]{2,1,0:T(8,128)(2,1)} %param.22), kind=kOutput, calls=%fused_computation.117 | convolution fusion | flops 3208642560 | bytes 20643840 | tf_op jit(solution)/shard_map/ecd,edf->ecf/dot_general | solution.py:117
  330.5 10.1 %convolution_multiply_fusion = f32[5,816,1536]{2,1,0:T(8,128)} fusion(bf16[5,128,1536]{2,1,0:T(8,128)(2,1)S(1)} %copy-done, f32[5,816]{1,0:T(8,128)S(1)} %and_select_fusion, f32[5,816,256]{2,1,0:T(8,128)S(1)} %fusion.48), kind=kOutput, calls=%fused_computation.22 | convolution fusion | flops 1613721600 | bytes 31227840 | tf_op jit(solution)/shard_map/ecf,efd->ecd/dot_general | solution.py:122
  340.7 46.6 %scatter_custom_fusion = f32[2049,1536]{1,0:T(8,128)} fusion(s32[4080]{0:T(1024)S(1)} %bitcast.107, f32[4080,1536]{1,0:T(8,128)} %bitcast.92, f32[]{:T(128)} %constant.216.clone.1), kind=kCustom, calls=%fused_computation.24 | custom fusion | flops 6266880 | bytes 12589568 | tf_op jit(solution)/shard_map/scatter-add | solution.py:128
  387.2 8.0 %slice.188 = bf16[2048,1536]{1,0:T(8,128)(2,1)} slice(f32[2049,1536]{1,0:T(8,128)} %scatter_custom_fusion), slice={[0:2048], [0:1536]} | slice | bytes 12582912 | tf_op jit(solution)/shard_map/slice | solution.py:130
  397.0 93.9 %reduce-scatter.2.cloned.1.call-done = bf16[64,1536]{1,0:T(8,128)(2,1)} async-done(((bf16[2048,1536]{1,0:T(8,128)(2,1)}), bf16[64,1536]{1,0:T(8,128)(2,1)}) %reduce-scatter.2.cloned.1.call-update) | async-done | bytes 196624 | tf_op jit(solution)/shard_map/reduce_scatter | solution.py:258
  (189 shorter events, 51.3 us)
Async XLA Ops:
  7.2 323.4 %copy-start = (bf16[5,128,1536]{2,1,0:T(8,128)(2,1)S(1)}, bf16[5,128,1536]{2,1,0:T(8,128)(2,1)}, u32[]{:S(2)}) copy-start(bf16[5,128,1536]{2,1,0:T(8,128)(2,1)} %param.23) | copy-start | bytes 5898244
  7.2 70.8 %all-gather.5.cloned.1.call-start = ((), (), s32[]{:S(2)}) async-start(), calls=%async_computation.1 | async-start | bytes 6488064 | tf_op jit(solution)/shard_map/all_gather | solution.py:165
  10.2 277.9 %all-gather.7.cloned.1.call-start = ((), (), s32[]{:S(2)}) async-start(), calls=%async_computation.2 | async-start | bytes 6488064 | tf_op jit(solution)/shard_map/all_gather | solution.py:245
  11.3 10.9 %collective-permute-start = (bf16[1536,128]{0,1:T(8,128)(2,1)S(1)}, bf16[1536,128]{0,1:T(8,128)(2,1)S(1)}, u32[]{:S(2)}, u32[]{:S(2)}) collective-permute-start(bf16[1536,128]{0,1:T(8,128)(2,1)S(1)} %pad_maximum_fusion.1), channel_id=1, source_target_pairs={{0,8},{1,9},{2,10},{3,11},{4,12},{5,13},{6,14},{7,15},{8,0},{9,1},... | collective-permute-start | bytes 1179656 | tf_op jit(solution)/shard_map/ppermute | solution.py:23
  23.6 23.2 %collective-permute-start.1 = (bf16[1536,256]{0,1:T(8,128)(2,1)S(1)}, bf16[1536,256]{0,1:T(8,128)(2,1)S(1)}, u32[]{:S(2)}, u32[]{:S(2)}) collective-permute-start(bf16[1536,256]{0,1:T(8,128)(2,1)S(1)} %maximum_select_fusion.1), channel_id=1, source_target_pairs={{0,16},{1,17},{2,18},{3,19},{4,20},{5,21},{6,22},{7,23},{8,24},{9,... | collective-permute-start | bytes 2359304 | tf_op jit(solution)/shard_map/ppermute | solution.py:23
  82.9 4.1 copy-start.2
  87.0 0.7 copy-start.4
  97.4 4.2 copy-start.8
  101.6 0.7 copy-start.9
  106.7 4.2 copy-start.8
  114.2 1.7 copy-start.1
  116.0 21.4 %collective-permute-start.2 = (bf16[256,1536]{1,0:T(8,128)(2,1)S(1)}, bf16[256,1536]{1,0:T(8,128)(2,1)}, u32[]{:S(2)}, u32[]{:S(2)}) collective-permute-start(bf16[256,1536]{1,0:T(8,128)(2,1)S(1)} %select_convert_fusion), channel_id=1, source_target_pairs={{0,4},{1,5},{2,6},{3,7},{4,0},{5,1},{6,2},{7,3},{8,12},{9,13},{10,... | collective-permute-start | bytes 2359304 | tf_op jit(solution)/shard_map/ppermute | solution.py:23
  140.7 10.7 %collective-permute-start.3 = (bf16[128,1536]{1,0:T(8,128)(2,1)}, bf16[128,1536]{1,0:T(8,128)(2,1)}, u32[]{:S(2)}, u32[]{:S(2)}) collective-permute-start(bf16[128,1536]{1,0:T(8,128)(2,1)} %select_convert_fusion.1), channel_id=1, source_target_pairs={{0,2},{1,3},{2,0},{3,1},{4,6},{5,7},{6,4},{7,5},{8,10},{9,11},{10,... | collective-permute-start | bytes 1179656 | tf_op jit(solution)/shard_map/ppermute | solution.py:23
  141.1 13.1 %copy-start.6 = (bf16[64,1536]{1,0:T(8,128)(2,1)S(1)}, bf16[64,1536]{1,0:T(8,128)(2,1)}, u32[]{:S(2)}) copy-start(bf16[64,1536]{1,0:T(8,128)(2,1)} %param.14) | copy-start | bytes 589828
  141.1 13.3 %copy-start.10 = (f32[1536]{0:T(1024)S(1)}, f32[1536]{0:T(1024)}, u32[]{:S(2)}) copy-start(f32[1536]{0:T(1024)} %param.21) | copy-start | bytes 18436
  141.1 14.2 %copy-start.12 = (bf16[64,8]{0,1:T(8,128)(2,1)S(1)}, bf16[64,8]{0,1:T(8,128)(2,1)}, u32[]{:S(2)}) copy-start(bf16[64,8]{0,1:T(8,128)(2,1)} %param.17) | copy-start | bytes 3076
  152.5 25.8 %copy-start.11 = (s32[64,8]{0,1:T(8,128)S(1)}, s32[64,8]{0,1:T(8,128)}, u32[]{:S(2)}) copy-start(s32[64,8]{0,1:T(8,128)} %param.16) | copy-start | bytes 6148
  152.6 51.8 %copy-start.14 = (s32[2]{0:T(128)S(1)}, s32[2]{0:T(128)}, u32[]{:S(2)}) copy-start(s32[2]{0:T(128)} %constant.248) | copy-start | bytes 28
  152.6 51.8 %copy-start.13 = (s32[2]{0:T(128)S(1)}, s32[2]{0:T(128)}, u32[]{:S(2)}) copy-start(s32[2]{0:T(128)} %constant.251) | copy-start | bytes 28
  152.6 1.5 collective-permute-start.4
  154.4 336.5 %copy-start.7 = (bf16[64,1536]{1,0:T(8,128)(2,1)}, bf16[64,1536]{1,0:T(8,128)(2,1)S(1)}, u32[]{:S(2)}) copy-start(bf16[64,1536]{1,0:T(8,128)(2,1)S(1)} %get-tuple-element.314) | copy-start | bytes 589828
  155.2 335.7 %reduce-scatter.2.cloned.1.call-start = ((), (), s32[]{:S(2)}) async-start(), calls=%async_computation.3 | async-start | bytes 6488064 | tf_op jit(solution)/shard_map/reduce_scatter | solution.py:258
  395.2 0.9 copy-start.3
  395.2 1.0 copy-start.5
  (1 other events, 0.7 us)
Sparse Core Ops, SparseCore 0:
  11.1 66.8 all-gather.4
  155.3 55.2 all-gather.6
  395.4 95.4 reduce-scatter.1
where the time goes:
time: 500 us; the launch traced here: 499 us
  waiting for transfers between devices  182 us (36%)
  local copies, waits for them, and re-layouts  145 us (29%)
  other arithmetic  69.5 us (14%)
  blocking collectives  46.6 us (9%)
  matrix products  30 us (6%)
  between operations  14.8 us (3%)
  loops' own time  6.93 us (1%)
    reduce_scatter x1, waiting for transfers between devices, on_device(): lax.psum_scatter(expert_part.astype(jnp.bfloat16), 'tensor', scatter_dime...  93.9 us
    ppermute x5, waiting for transfers between devices, partner(): return lax.ppermute(value, axis, pairs)  58.1 us
    scatter-add x1, other arithmetic, expert_term(): summed = jnp.zeros((row_count + 1, model_width), jnp.float32).at[slot_tab...  46.6 us
    unnamed x33, local copies, waits for them, and re-layouts  45.8 us
    gather x3, local copies, waits for them, and re-layouts, expert_term(): slot_share = jnp.take_along_axis(padded_share.T, slot_table, axis=1)  40.6 us
    all_gather x1, waiting for transfers between devices, on_device(): all_rows = lax.all_gather(normed, 'tensor', axis=0, tiled=True)  30 us
    gather x1, local copies, waits for them, and re-layouts, expert_term(): picked = padded_in[slot_table]  28.9 us
    all_gather x1, blocking collectives, on_device(): lax.all_gather(routes, 'tensor', axis=0, tiled=True)  23.7 us
  transfers between devices with their start and end apart: 8, of which 7 were waited for; matrix products, arithmetic and copies ran while one was open for 19% of the time, Pallas kernels for 0%

commit v1 on v0

--- a/solution.py
+++ b/solution.py
@@ -4,6 +4,8 @@
 import jax.numpy as jnp
 from jax import lax
 from jax.sharding import PartitionSpec as P
+from jax.experimental import pallas as pl
+from jax.experimental.pallas import tpu as pltpu
 
 KVH = 8
 HD = 64
@@ -88,46 +90,37 @@
     return jnp.concatenate([rotated, paired[:, head_size:]], axis=1).astype(jnp.bfloat16)
 
 
-def expert_term(inputs, routes, route_weights, gate_up, down_proj, first_expert, capacity):
-    row_count = inputs.shape[0]
-    model_width = inputs.shape[1]
+def expert_block(rows_ref, share_ref, gate_up_ref, down_ref, out_ref):
+    rows = rows_ref[...]
+    inner_width = down_ref.shape[1]
+    total = jnp.zeros(out_ref.shape, jnp.float32)
+    for expert in range(gate_up_ref.shape[0]):
+        both = jnp.dot(rows, gate_up_ref[expert], preferred_element_type=jnp.float32)
+        gate_val = both[:, :inner_width]
+        up_val = both[:, inner_width:]
+        inner_act = (jax.nn.silu(gate_val) * up_val).astype(jnp.bfloat16)
+        produced = jnp.dot(inner_act, down_ref[expert], preferred_element_type=jnp.float32)
+        total = total + share_ref[:, expert : expert + 1] * produced
+    out_ref[...] = total.astype(out_ref.dtype)
+
+
+def dense_experts(rows_all, shares, gate_up, down_proj):
+    row_count, model_width = rows_all.shape
     expert_count = gate_up.shape[0]
-    inner_width = down_proj.shape[1]
-    expert_ids = first_expert + jnp.arange(expert_count, dtype=jnp.int32)
-    matches = routes[:, None, :] == expert_ids[None, :, None]
-    chosen = jnp.any(matches, axis=2)
-    shares = jnp.sum(jnp.where(matches, route_weights.astype(jnp.float32)[:, None, :], 0.0), axis=2)
-    ranks = jnp.cumsum(chosen.astype(jnp.int32), axis=0) - 1
-    targets = jnp.where(chosen, ranks, capacity)
-    row_ids = jnp.broadcast_to(
-        jnp.arange(row_count, dtype=jnp.int32)[:, None], (row_count, expert_count)
-    )
-    column_ids = jnp.broadcast_to(
-        jnp.arange(expert_count, dtype=jnp.int32)[None, :], (row_count, expert_count)
-    )
-    slot_table = (
-        jnp.full((expert_count, capacity + 1), row_count, jnp.int32)
-        .at[column_ids, targets]
-        .set(row_ids)[:, :capacity]
-    )
-    padded_in = jnp.concatenate([inputs, jnp.zeros((1, model_width), inputs.dtype)], axis=0)
-    padded_share = jnp.concatenate([shares, jnp.zeros((1, expert_count), jnp.float32)], axis=0)
-    picked = padded_in[slot_table]
-    slot_share = jnp.take_along_axis(padded_share.T, slot_table, axis=1)
-    gate_up_out = jnp.einsum("ecd,edf->ecf", picked, gate_up, preferred_element_type=jnp.float32)
-    inner_act = (
-        jax.nn.silu(gate_up_out[..., :inner_width]) * gate_up_out[..., inner_width:]
-    ).astype(jnp.bfloat16)
-    produced = (
-        jnp.einsum("ecf,efd->ecd", inner_act, down_proj, preferred_element_type=jnp.float32)
-        * slot_share[..., None]
-    )
-    summed = (
-        jnp.zeros((row_count + 1, model_width), jnp.float32)
-        .at[slot_table.reshape(-1)]
-        .add(produced.reshape(-1, model_width))
-    )
-    return summed[:row_count]
+    tile = 256
+    return pl.pallas_call(
+        expert_block,
+        grid=(row_count // tile,),
+        in_specs=[
+            pl.BlockSpec((tile, model_width), lambda i: (i, 0)),
+            pl.BlockSpec((tile, expert_count), lambda i: (i, 0)),
+            pl.BlockSpec(gate_up.shape, lambda i: (0, 0, 0)),
+            pl.BlockSpec(down_proj.shape, lambda i: (0, 0, 0)),
+        ],
+        out_specs=pl.BlockSpec((tile, model_width), lambda i: (i, 0)),
+        out_shape=jax.ShapeDtypeStruct((row_count, model_width), jnp.bfloat16),
+        compiler_params=pltpu.CompilerParams(vmem_limit_bytes=48 * 1024 * 1024),
+    )(rows_all, shares, gate_up, down_proj)
 
 
 def on_device(
@@ -144,6 +137,17 @@
     rows_quarter = seq_len // quarters
     model_width = hidden.shape[1]
     starts = segment_starts(segment_ids)
+    expert_total = w_gate_up.shape[0] * KVH
+    expert_ids = jnp.arange(expert_total, dtype=jnp.int32)
+    share_table = jnp.sum(
+        jnp.where(
+            routes[:, None, :] == expert_ids[None, :, None],
+            route_weights[:, None, :],
+            jnp.zeros((), route_weights.dtype),
+        ),
+        axis=2,
+    )
+    shares_all = lax.all_gather(share_table, "tensor", axis=0, tiled=True)
     positions = jnp.arange(seq_len, dtype=jnp.int32) - starts
     own_positions = lax.dynamic_slice_in_dim(
         positions, quarter_index * rows_quarter, rows_quarter, 0
@@ -240,23 +244,13 @@
     )
     expert_in = rms_norm(after_attention, ffn_gain)
     local_experts = w_gate_up.shape[0]
-    capacity = 2 * rows_quarter // 5
-    rows_all, routes_all, shares_all = (
-        lax.all_gather(expert_in, "tensor", axis=0, tiled=True),
-        lax.all_gather(routes, "tensor", axis=0, tiled=True),
-        lax.all_gather(route_weights, "tensor", axis=0, tiled=True),
-    )
-    expert_part = expert_term(
-        rows_all,
-        routes_all,
-        shares_all,
-        w_gate_up,
-        w_down,
-        group_index * local_experts,
-        quarters * capacity,
-    )
+    rows_all = lax.all_gather(expert_in, "tensor", axis=0, tiled=True)
+    local_shares = lax.dynamic_slice_in_dim(
+        shares_all, group_index * local_experts, local_experts, 1
+    ).astype(jnp.float32)
+    expert_part = dense_experts(rows_all, local_shares, w_gate_up, w_down)
     expert_sum = lax.psum_scatter(
-        expert_part.astype(jnp.bfloat16), "tensor", scatter_dimension=0, tiled=True
+        expert_part, "tensor", scatter_dimension=0, tiled=True
     ).astype(jnp.float32)
     hidden_out = (after_attention.astype(jnp.float32) + residual_scale * expert_sum).astype(
         jnp.bfloat16

time: 500 us -> 335 us (0.67)
  local copies, waits for them, and re-layouts: 145 us -> 12.3 us
  other arithmetic: 69.5 us -> 17.5 us
  Pallas kernels: 0 us -> 28.4 us
  waiting for transfers between devices: 182 us -> 210 us
  blocking collectives: 46.6 us -> 26.8 us
  matrix products: 30 us -> 12.2 us
    gather x4 -> x0, local copies, waits for them, and re-layouts: 69.5 us -> none  [the longest x3 40.6 us: expert_term(): slot_share = jnp.take_along_axis(padded_share.T, slot_table, axis=1)]
    scatter-add x1 -> x0, other arithmetic: 46.6 us -> none  [expert_term(): summed = jnp.zeros((row_count + 1, model_width), jnp.float32).at[slot_tab...]
    unnamed x33 -> x26, local copies, waits for them, and re-layouts: 45.8 us -> 3.34 us
    pallas_call x0 -> x1, Pallas kernels: none -> 28.4 us  [dense_experts(): pl.pallas_call(expert_block, grid=(row_count // tile,), in_specs=[pl.Bloc...]
    all_gather x1, waiting for transfers between devices: 0.02 us -> 27.9 us  [on_device(): rows_all = lax.all_gather(expert_in, 'tensor', axis=0, tiled=True)]
    all_gather x2 -> x1, blocking collectives: 46.6 us -> 26.8 us  [on_device(): shares_all = lax.all_gather(share_table, 'tensor', axis=0, tiled=True)]
    dot_general x2 -> x0, matrix products: 17.7 us -> none  [the longest x1 10.1 us: expert_term(): jnp.einsum('ecf,efd->ecd', inner_act, down_proj, preferred_element_type=j...]
    slice x2 -> x1, local copies, waits for them, and re-layouts: 8.09 us -> 0.08 us  [the longest x1 8.02 us: expert_term(): return summed[:row_count]]
  transfers between devices with their start and end apart: 8 -> 8, of which waited for: 7 -> 8; matrix products, arithmetic and copies ran while one was open for 19% -> 2% of each run, Pallas kernels for 0% -> 0%
where the time goes in v1:
time: 335 us; the launch traced here: 334 us
  waiting for transfers between devices  210 us (63%)
  Pallas kernels  28.4 us (8%)
  blocking collectives  26.8 us (8%)
  other arithmetic  17.5 us (5%)
  between operations  14.7 us (4%)
  local copies, waits for them, and re-layouts  12.3 us (4%)
  matrix products  12.2 us (4%)
  loops' own time  7.46 us (2%)
  starting transfers between devices  4.65 us (1%)
    reduce_scatter x1, waiting for transfers between devices, on_device(): lax.psum_scatter(expert_part, 'tensor', scatter_dimension=0, tiled=True)  91.8 us
    ppermute x5, waiting for transfers between devices, partner(): return lax.ppermute(value, axis, pairs)  60.1 us
    all_gather x1, waiting for transfers between devices, on_device(): all_rows = lax.all_gather(normed, 'tensor', axis=0, tiled=True)  30.1 us
    pallas_call x1, Pallas kernels, dense_experts(): pl.pallas_call(expert_block, grid=(row_count // tile,), in_specs=[pl.Bloc...  28.4 us
    all_gather x1, waiting for transfers between devices, on_device(): rows_all = lax.all_gather(expert_in, 'tensor', axis=0, tiled=True)  27.9 us
    all_gather x1, blocking collectives, on_device(): shares_all = lax.all_gather(share_table, 'tensor', axis=0, tiled=True)  26.8 us
    another operation x1, loops' own time, on_device(): lax.map(attend, jnp.arange(rows_quarter // block_rows, dtype=jnp.int32))  7.08 us
  transfers between devices with their start and end apart: 8, of which 8 were waited for; matrix products, arithmetic and copies ran while one was open for 2% of the time, Pallas kernels for 0%

profile of v1, /device:TPU:24, one launch (start us, length us, event | category | flops | bytes accessed | tf_op | source)
XLA Modules:
  0.0 334.1 jit_solution(4713271061986981572)
XLA Ops:
  7.2 1.2 fusion.12
  8.5 1.7 fusion.14
  13.9 8.3 %collective-permute-done = bf16[1536,128]{0,1:T(8,128)(2,1)S(1)} collective-permute-done((bf16[1536,128]{0,1:T(8,128)(2,1)S(1)}, bf16[1536,128]{0,1:T(8,128)(2,1)S(1)}, u32[]{:S(2)}, u32[]{:S(2)}) %collective-permute-start) | collective-permute-done | bytes 393248 | tf_op jit(solution)/shard_map/ppermute | solution.py:25
  22.4 1.3 collective-permute-start.1
  24.9 20.7 %collective-permute-done.1 = bf16[1536,256]{0,1:T(8,128)(2,1)S(1)} collective-permute-done((bf16[1536,256]{0,1:T(8,128)(2,1)S(1)}, bf16[1536,256]{0,1:T(8,128)(2,1)S(1)}, u32[]{:S(2)}, u32[]{:S(2)}) %collective-permute-start.1) | collective-permute-done | bytes 786464 | tf_op jit(solution)/shard_map/ppermute | solution.py:25
  46.8 30.1 %all-gather.4.cloned.1.call-done = bf16[2048,1536]{1,0:T(8,128)(2,1)} async-done(((bf16[64,1536]{1,0:T(8,128)(2,1)}), bf16[2048,1536]{1,0:T(8,128)(2,1)}) %all-gather.4.cloned.1.call-update) | async-done | bytes 6291472 | tf_op jit(solution)/shard_map/all_gather | solution.py:169
  76.9 4.9 %fusion.20 = f32[2048,128]{0,1:T(8,128)S(1)} fusion(bf16[2048,1536]{1,0:T(8,128)(2,1)} %all-gather.4.cloned.1.call-done, bf16[1536,320]{0,1:T(8,128)(2,1)S(1)} %bitcast.57), kind=kOutput, calls=%fused_computation.49 | convolution fusion | flops 805306368 | bytes 7733248 | tf_op jit(solution)/shard_map/dot_general | solution.py:88
  81.9 2.1 fusion.9
  87.2 18.0 %while.59 = (s32[]{:T(128)}, bf16[2,256,192]{1,2,0:T(8,128)(2,1)S(1)}, s32[2]{0:T(128)S(1)}, s32[]{:T(128)}, s32[2048]{0:T(1024)S(1)}, /*index=5*/bf16[3,512,64]...) while((s32[]{:T(128)}, ...), condition=%wide.region_8.9_spmd, body=%wide.region_3.8_spmd.sunk | while | flops 104007976 | bytes 8754148 | solution.py:229
  92.0 4.0 %while.60 = (s32[]{:T(128)}, f32[768]{0:T(1024)S(1)}, f32[768]{0:T(1024)S(1)}, f32[768,64]{0,1:T(8,128)S(1)}, s32[]{:T(128)}, /*index=5*/s32[256]{0:T(256)S(1)},...) while((s32[]{:T(128)}, f32[768]{0:T(1024)S(1)}, ...), condition=%wide.region_7.7_spmd.clone, body=%wide.region_4.6_spmd.clone.sunk | while | flops 103909632 | bytes 7464147 | solution.py:225
  101.0 4.0 %while.60 = (s32[]{:T(128)}, f32[768]{0:T(1024)S(1)}, f32[768]{0:T(1024)S(1)}, f32[768,64]{0,1:T(8,128)S(1)}, s32[]{:T(128)}, /*index=5*/s32[256]{0:T(256)S(1)},...) while((s32[]{:T(128)}, f32[768]{0:T(1024)S(1)}, ...), condition=%wide.region_7.7_spmd.clone, body=%wide.region_4.6_spmd.clone.sunk | while | flops 103909632 | bytes 7464147 | solution.py:225
  105.2 1.7 fusion.38
  107.9 1.8 collective-permute-start.2
  109.7 19.6 %collective-permute-done.2 = bf16[256,1536]{1,0:T(8,128)(2,1)} collective-permute-done((bf16[256,1536]{1,0:T(8,128)(2,1)}, bf16[256,1536]{1,0:T(8,128)(2,1)}, u32[]{:S(2)}, u32[]{:S(2)}) %collective-permute-start.2) | collective-permute-done | bytes 786464 | tf_op jit(solution)/shard_map/ppermute | solution.py:25
  129.4 1.5 convert_add_fusion
  132.5 10.0 %collective-permute-done.3 = bf16[128,1536]{1,0:T(8,128)(2,1)S(1)} collective-permute-done((bf16[128,1536]{1,0:T(8,128)(2,1)S(1)}, bf16[128,1536]{1,0:T(8,128)(2,1)S(1)}, u32[]{:S(2)}, u32[]{:S(2)}) %collective-permute-start.3) | collective-permute-done | bytes 393248 | tf_op jit(solution)/shard_map/ppermute | solution.py:25
  142.5 1.5 convert_add_fusion.1
  144.2 1.4 collective-permute-done.4
  146.9 26.8 %all-gather = bf16[32,64,40]{1,2,0:T(8,128)(2,1)S(1)} all-gather(bf16[1,64,40]{1,2,0:T(8,128)(2,1)S(1)} %bitcast.64), channel_id=1, replica_groups=mesh['dp'=8,'tensor'=32] {'tensor'}, dimensions={0}, use_global_device_ids=true | all-gather | bytes 168960 | tf_op jit(solution)/shard_map/all_gather | solution.py:150
  174.8 1.2 dynamic-slice_convert_fusion.share_ref
  176.0 27.9 %all-gather.6.cloned.1.call-done.rows_ref = bf16[2048,1536]{1,0:T(8,128)(2,1)} async-done(((bf16[64,1536]{1,0:T(8,128)(2,1)}), bf16[2048,1536]{1,0:T(8,128)(2,1)}) %all-gather.6.cloned.1.call-update) | async-done | bytes 6291472 | tf_op jit(solution)/shard_map/all_gather | solution.py:247
  203.9 28.4 %shard_map.121 = bf16[2048,1536]{1,0:T(8,128)(2,1)} custom-call(bf16[2048,1536]{1,0:T(8,128)(2,1)} %all-gather.6.cloned.1.call-done.rows_ref, f32[2048,5]{1,0:T(8,128)S(1)} %dynamic-slice_convert_fusion.share_ref, bf16[5,1536,256]{2,1,0:T(8,128)(2,1)} %gate_up_ref.1, bf16[5,128,1536]{2,1,0:T(8,128)(2,1)S(1)} %copy-done), custom_call_target="tpu_custom_call" | custom-call | tf_op jit(solution)/shard_map/pallas_call | solution.py:111
  234.0 91.8 %reduce-scatter.2.cloned.1.call-done = bf16[64,1536]{1,0:T(8,128)(2,1)} async-done(((bf16[2048,1536]{1,0:T(8,128)(2,1)}), bf16[64,1536]{1,0:T(8,128)(2,1)}) %reduce-scatter.2.cloned.1.call-update) | async-done | bytes 196624 | tf_op jit(solution)/shard_map/reduce_scatter | solution.py:252
  325.9 1.7 fusion.19
  (140 shorter events, 26.1 us)
Async XLA Ops:
  7.2 15.1 %copy-start.7 = (bf16[1536,48]{0,1:T(8,128)(2,1)S(1)}, bf16[1536,48]{0,1:T(8,128)(2,1)}, u32[]{:S(2)}) copy-start(bf16[1536,48]{0,1:T(8,128)(2,1)} %param.20) | copy-start | bytes 442372
  7.2 15.1 %copy-start.6 = (bf16[1536,80]{0,1:T(8,128)(2,1)S(1)}, bf16[1536,80]{0,1:T(8,128)(2,1)}, u32[]{:S(2)}) copy-start(bf16[1536,80]{0,1:T(8,128)(2,1)} %param.19) | copy-start | bytes 737284
  7.2 4.9 %copy-start.8 = (s32[2048]{0:T(1024)S(1)}, s32[2048]{0:T(1024)}, u32[]{:S(2)}) copy-start(s32[2048]{0:T(1024)} %param.15) | copy-start | bytes 24580
  7.2 69.7 %all-gather.4.cloned.1.call-start = ((), (), s32[]{:S(2)}) async-start(), calls=%async_computation.1 | async-start | bytes 6488064 | tf_op jit(solution)/shard_map/all_gather | solution.py:169
  10.2 193.6 %all-gather.6.cloned.1.call-start = ((), (), s32[]{:S(2)}) async-start(), calls=%async_computation.2 | async-start | bytes 6488064 | tf_op jit(solution)/shard_map/all_gather | solution.py:247
  11.3 10.9 %collective-permute-start = (bf16[1536,128]{0,1:T(8,128)(2,1)S(1)}, bf16[1536,128]{0,1:T(8,128)(2,1)S(1)}, u32[]{:S(2)}, u32[]{:S(2)}) collective-permute-start(bf16[1536,128]{0,1:T(8,128)(2,1)S(1)} %pad_maximum_fusion.1), channel_id=1, source_target_pairs={{0,8},{1,9},{2,10},{3,11},{4,12},{5,13},{6,14},{7,15},{8,0},{9,1},... | collective-permute-start | bytes 1179656 | tf_op jit(solution)/shard_map/ppermute | solution.py:25
  22.4 23.2 %collective-permute-start.1 = (bf16[1536,256]{0,1:T(8,128)(2,1)S(1)}, bf16[1536,256]{0,1:T(8,128)(2,1)S(1)}, u32[]{:S(2)}, u32[]{:S(2)}) collective-permute-start(bf16[1536,256]{0,1:T(8,128)(2,1)S(1)} %maximum_select_fusion.1), channel_id=1, source_target_pairs={{0,16},{1,17},{2,18},{3,19},{4,20},{5,21},{6,22},{7,23},{8,24},{9,... | collective-permute-start | bytes 2359304 | tf_op jit(solution)/shard_map/ppermute | solution.py:25
  85.2 0.7 copy-start.2
  107.9 21.5 %collective-permute-start.2 = (bf16[256,1536]{1,0:T(8,128)(2,1)}, bf16[256,1536]{1,0:T(8,128)(2,1)}, u32[]{:S(2)}, u32[]{:S(2)}) collective-permute-start(bf16[256,1536]{1,0:T(8,128)(2,1)} %select_convert_fusion), channel_id=1, source_target_pairs={{0,4},{1,5},{2,6},{3,7},{4,0},{5,1},{6,2},{7,3},{8,12},{9,13},{10,... | collective-permute-start | bytes 2359304 | tf_op jit(solution)/shard_map/ppermute | solution.py:25
  130.9 1.1 copy-start.1
  132.1 10.5 %collective-permute-start.3 = (bf16[128,1536]{1,0:T(8,128)(2,1)S(1)}, bf16[128,1536]{1,0:T(8,128)(2,1)S(1)}, u32[]{:S(2)}, u32[]{:S(2)}) collective-permute-start(bf16[128,1536]{1,0:T(8,128)(2,1)S(1)} %select_convert_fusion.1), channel_id=1, source_target_pairs={{0,2},{1,3},{2,0},{3,1},{4,6},{5,7},{6,4},{7,5},{8,10},{9,11},{10,... | collective-permute-start | bytes 1179656 | tf_op jit(solution)/shard_map/ppermute | solution.py:25
  132.5 13.1 %copy-start.4 = (bf16[64,1536]{1,0:T(8,128)(2,1)S(1)}, bf16[64,1536]{1,0:T(8,128)(2,1)}, u32[]{:S(2)}) copy-start(bf16[64,1536]{1,0:T(8,128)(2,1)} %param.14) | copy-start | bytes 589828
  144.0 1.8 copy-start.9
  144.0 2.7 copy-start.10
  144.1 2.7 copy-start.11
  144.1 1.5 collective-permute-start.4
  145.9 180.0 %copy-start.5 = (bf16[64,1536]{1,0:T(8,128)(2,1)}, bf16[64,1536]{1,0:T(8,128)(2,1)S(1)}, u32[]{:S(2)}) copy-start(bf16[64,1536]{1,0:T(8,128)(2,1)S(1)} %get-tuple-element.314) | copy-start | bytes 589828
  146.7 57.2 %copy-start = (bf16[5,128,1536]{2,1,0:T(8,128)(2,1)S(1)}, bf16[5,128,1536]{2,1,0:T(8,128)(2,1)}, u32[]{:S(2)}) copy-start(bf16[5,128,1536]{2,1,0:T(8,128)(2,1)} %down_ref.1) | copy-start | bytes 5898244
  146.7 179.2 %reduce-scatter.2.cloned.1.call-start = ((), (), s32[]{:S(2)}) async-start(), calls=%async_computation.3 | async-start | bytes 6488064 | tf_op jit(solution)/shard_map/reduce_scatter | solution.py:252
  232.3 0.9 copy-start.3
Sparse Core Ops, SparseCore 0:
  11.1 65.7 all-gather.3
  146.8 56.9 all-gather.5
  232.5 93.3 reduce-scatter.1

commit v2 on v1

--- a/solution.py
+++ b/solution.py
@@ -10,6 +10,8 @@
 KVH = 8
 HD = 64
 GQ = 3
+CHIPS = ("ty", "tx")
+TENSOR = ("ty", "tx", "tc")
 
 
 attn_scale = 0.015625
@@ -57,7 +59,7 @@
 
 
 def gather_levels(parts, level_bits, join_axes, sender):
-    index_now = lax.axis_index("tensor")
+    index_now = lax.axis_index(TENSOR)
     for level_bit in level_bits:
         arrived = sender(parts, level_bit)
         is_upper = index_now >> level_bit & 1 == 1
@@ -71,7 +73,7 @@
 
 
 def fold_levels(partial_sum, level_bits, sender):
-    index_now = lax.axis_index("tensor")
+    index_now = lax.axis_index(TENSOR)
     for level_bit in reversed(level_bits):
         half_rows = partial_sum.shape[0] // 2
         lower_rows = partial_sum[:half_rows]
@@ -105,7 +107,8 @@
 
 
 def dense_experts(rows_all, shares, gate_up, down_proj):
-    row_count, model_width = rows_all.shape
+    row_count = rows_all.shape[0]
+    model_width = gate_up.shape[1]
     expert_count = gate_up.shape[0]
     tile = 256
     return pl.pallas_call(
@@ -126,9 +129,9 @@
 def on_device(
     hidden, segment_ids, routes, route_weights, attn_gain, w_qkv, w_out, ffn_gain, w_gate_up, w_down
 ):
-    device_count = lax.axis_size("tensor")
+    device_count = lax.axis_size(TENSOR)
     quarters = device_count // KVH
-    index_now = lax.axis_index("tensor")
+    index_now = lax.axis_index(TENSOR)
     quarter_index = index_now // KVH
     group_index = index_now % KVH
     group_bits = list(range(KVH.bit_length() - 1))
@@ -147,7 +150,6 @@
         ),
         axis=2,
     )
-    shares_all = lax.all_gather(share_table, "tensor", axis=0, tiled=True)
     positions = jnp.arange(seq_len, dtype=jnp.int32) - starts
     own_positions = lax.dynamic_slice_in_dim(
         positions, quarter_index * rows_quarter, rows_quarter, 0
@@ -159,14 +161,14 @@
         (joined,),
         quarter_bits,
         (1,),
-        lambda payload, level_bit: (partner(payload[0], "tensor", level_bit),),
+        lambda payload, level_bit: (partner(payload[0], TENSOR, level_bit),),
     )
     by_quarter = gathered_cols.reshape(model_width, quarters, joined.shape[1])
     w_group = by_quarter[:, :, :qkv_width].reshape(model_width, quarters * qkv_width)
     w_attn_out = by_quarter[:, :, qkv_width:].reshape(model_width, GQ * HD)
     w_query = w_group[:, : GQ * HD]
     w_pairs = w_group[:, GQ * HD :]
-    all_rows = lax.all_gather(normed, "tensor", axis=0, tiled=True)
+    all_rows = lax.all_gather(normed, TENSOR, axis=0, tiled=True)
     own_rows = lax.dynamic_slice_in_dim(all_rows, quarter_index * rows_quarter, rows_quarter, 0)
     key_values = project_pairs(all_rows, w_pairs, positions)
     kv_block = lax.dynamic_slice_in_dim(key_values, quarter_index * rows_quarter, rows_quarter, 0)
@@ -236,7 +238,7 @@
         partial_proj,
         group_bits,
         lambda sent_rows, level_bit: partner(
-            sent_rows.astype(jnp.bfloat16), "tensor", level_bit
+            sent_rows.astype(jnp.bfloat16), TENSOR, level_bit
         ).astype(sent_rows.dtype),
     )
     after_attention = (hidden.astype(jnp.float32) + residual_scale * projection).astype(
@@ -244,14 +246,28 @@
     )
     expert_in = rms_norm(after_attention, ffn_gain)
     local_experts = w_gate_up.shape[0]
-    rows_all = lax.all_gather(expert_in, "tensor", axis=0, tiled=True)
+    share_cols = 128 * pl.cdiv(expert_total, 128)
+    carried = jnp.concatenate(
+        [
+            expert_in,
+            share_table,
+            jnp.zeros((share_table.shape[0], share_cols - expert_total), jnp.bfloat16),
+        ],
+        axis=1,
+    )
+    by_chip = lax.all_gather(carried, CHIPS, axis=0, tiled=True)
+    rows_all = lax.all_gather(by_chip, "tc", axis=0, tiled=True)
     local_shares = lax.dynamic_slice_in_dim(
-        shares_all, group_index * local_experts, local_experts, 1
+        rows_all[:, model_width : model_width + expert_total],
+        group_index * local_experts,
+        local_experts,
+        1,
     ).astype(jnp.float32)
     expert_part = dense_experts(rows_all, local_shares, w_gate_up, w_down)
-    expert_sum = lax.psum_scatter(
-        expert_part, "tensor", scatter_dimension=0, tiled=True
-    ).astype(jnp.float32)
+    core_sum = lax.psum_scatter(expert_part, "tc", scatter_dimension=0, tiled=True)
+    expert_sum = lax.psum_scatter(core_sum, CHIPS, scatter_dimension=0, tiled=True).astype(
+        jnp.float32
+    )
     hidden_out = (after_attention.astype(jnp.float32) + residual_scale * expert_sum).astype(
         jnp.bfloat16
     )
@@ -259,22 +275,24 @@
 
 
 def solution(mesh):
+    grid = mesh.devices.reshape(mesh.devices.shape[0], -1, 4, 2)
+    mesh = jax.sharding.Mesh(grid, ("dp",) + TENSOR)
     placed = (
-        P(("dp", "tensor"), None),
+        P(("dp",) + TENSOR, None),
         P("dp"),
-        P(("dp", "tensor"), None),
-        P(("dp", "tensor"), None),
+        P(("dp",) + TENSOR, None),
+        P(("dp",) + TENSOR, None),
         P(),
-        P(None, "tensor"),
-        P(None, "tensor"),
+        P(None, TENSOR),
+        P(None, TENSOR),
         P(),
-        P("tensor", None, None),
-        P("tensor", None, None),
+        P(TENSOR, None, None),
+        P(TENSOR, None, None),
     )
     return jax.shard_map(
         on_device,
         mesh=mesh,
         in_specs=placed,
-        out_specs=(P(("dp", "tensor"), None), P(("dp", "tensor"), None), P("tensor", "dp", None)),
+        out_specs=(P(("dp",) + TENSOR, None), P(("dp",) + TENSOR, None), P(TENSOR, "dp", None)),
         check_vma=False,
     )

time: 335 us -> 378 us (1.13)
  waiting for transfers between devices: 210 us -> 276 us
  blocking collectives: 26.8 us -> 0 us
    all_gather x2 -> x3, waiting for transfers between devices: 58 us -> 111 us  [the longest x1 56.8 us: on_device(): by_chip = lax.all_gather(carried, CHIPS, axis=0, tiled=True)]
    all_gather x1 -> x0, blocking collectives: 26.8 us -> none  [on_device(): shares_all = lax.all_gather(share_table, 'tensor', axis=0, tiled=True)]
    reduce_scatter x1 -> x2, waiting for transfers between devices: 91.8 us -> 106 us  [the longest x1 84.3 us: on_device(): lax.psum_scatter(core_sum, CHIPS, scatter_dimension=0, tiled=True)]
  transfers between devices with their start and end apart: 8 -> 10, of which waited for: 8 -> 10; matrix products, arithmetic and copies ran while one was open for 2% -> 2% of each run, Pallas kernels for 0% -> 0%
where the time goes in v2:
time: 378 us; the launch traced here: 377 us
  waiting for transfers between devices  276 us (73%)
  Pallas kernels  28.5 us (8%)
  other arithmetic  17.5 us (5%)
  local copies, waits for them, and re-layouts  15.5 us (4%)
  between operations  14.7 us (4%)
  matrix products  12.2 us (3%)
  loops' own time  7.51 us (2%)
  starting transfers between devices  4.95 us (1%)
    reduce_scatter x1, waiting for transfers between devices, on_device(): lax.psum_scatter(core_sum, CHIPS, scatter_dimension=0, tiled=True)  84.3 us
    ppermute x5, waiting for transfers between devices, partner(): return lax.ppermute(value, axis, pairs)  59.3 us
    all_gather x1, waiting for transfers between devices, on_device(): by_chip = lax.all_gather(carried, CHIPS, axis=0, tiled=True)  56.8 us
    all_gather x1, waiting for transfers between devices, on_device(): all_rows = lax.all_gather(normed, TENSOR, axis=0, tiled=True)  30.1 us
    pallas_call x1, Pallas kernels, dense_experts(): pl.pallas_call(expert_block, grid=(row_count // tile,), in_specs=[pl.Bloc...  28.5 us
    all_gather x1, waiting for transfers between devices, on_device(): rows_all = lax.all_gather(by_chip, 'tc', axis=0, tiled=True)  24.2 us
    reduce_scatter x1, waiting for transfers between devices, on_device(): lax.psum_scatter(expert_part, 'tc', scatter_dimension=0, tiled=True)  21.6 us
  transfers between devices with their start and end apart: 10, of which 10 were waited for; matrix products, arithmetic and copies ran while one was open for 2% of the time, Pallas kernels for 0%

profile of v2, /device:TPU:24, one launch (start us, length us, event | category | flops | bytes accessed | tf_op | source)
XLA Modules:
  0.0 377.3 jit_solution(17616330119270473805)
XLA Ops:
  8.5 1.7 fusion.14
  13.8 8.4 %collective-permute-done = bf16[1536,128]{0,1:T(8,128)(2,1)S(1)} collective-permute-done((bf16[1536,128]{0,1:T(8,128)(2,1)S(1)}, bf16[1536,128]{0,1:T(8,128)(2,1)S(1)}, u32[]{:S(2)}, u32[]{:S(2)}) %collective-permute-start) | collective-permute-done | bytes 393248 | tf_op jit(solution)/shard_map/ppermute | solution.py:27
  22.4 1.3 collective-permute-start.1
  23.9 1.8 multiply_cosine_fusion.1
  25.6 19.9 %collective-permute-done.1 = bf16[1536,256]{0,1:T(8,128)(2,1)S(1)} collective-permute-done((bf16[1536,256]{0,1:T(8,128)(2,1)S(1)}, bf16[1536,256]{0,1:T(8,128)(2,1)S(1)}, u32[]{:S(2)}, u32[]{:S(2)}) %collective-permute-start.1) | collective-permute-done | bytes 786464 | tf_op jit(solution)/shard_map/ppermute | solution.py:27
  46.8 30.1 %all-gather.4.cloned.1.call-done = bf16[2048,1536]{1,0:T(8,128)(2,1)} async-done(((bf16[64,1536]{1,0:T(8,128)(2,1)}), bf16[2048,1536]{1,0:T(8,128)(2,1)}) %all-gather.4.cloned.1.call-update) | async-done | bytes 6291472 | tf_op jit(solution)/shard_map/all_gather | solution.py:171
  76.9 4.9 %fusion.20 = f32[2048,128]{0,1:T(8,128)S(1)} fusion(bf16[2048,1536]{1,0:T(8,128)(2,1)} %all-gather.4.cloned.1.call-done, bf16[1536,320]{0,1:T(8,128)(2,1)S(1)} %bitcast.54), kind=kOutput, calls=%fused_computation.49 | convolution fusion | flops 805306368 | bytes 7733248 | tf_op jit(solution)/shard_map/dot_general | solution.py:90
  81.9 2.1 fusion.9
  88.2 19.4 %while.59 = (s32[]{:T(128)}, bf16[2,256,192]{1,2,0:T(8,128)(2,1)}, s32[2]{0:T(128)S(1)}, s32[]{:T(128)}, s32[2048]{0:T(1024)S(1)}, /*index=5*/bf16[3,512,64]{2,1...) while((s32[]{:T(128)}, bf16[2,256,192]{1,2,0:T(8,128)(2,1)}, ...), condition=%wide.region_8.9_spmd, body=%wide.region_3.8_spmd.sunk | while | flops 104007976 | bytes 10327068 | solution.py:231
  93.0 6.1 %while.60 = (s32[]{:T(128)}, f32[768]{0:T(1024)S(1)}, f32[768]{0:T(1024)S(1)}, f32[768,64]{0,1:T(8,128)S(1)}, s32[]{:T(128)}, /*index=5*/s32[256]{0:T(256)S(1)},...) while((s32[]{:T(128)}, f32[768]{0:T(1024)S(1)}, ...), condition=%wide.region_7.7_spmd.clone, body=%wide.region_4.6_spmd.clone.sunk | while | flops 103909632 | bytes 7464147 | solution.py:227
  104.7 2.0 while.60
  108.5 1.7 fusion.38
  111.2 1.9 collective-permute-start.2
  113.1 19.6 %collective-permute-done.2 = bf16[256,1536]{1,0:T(8,128)(2,1)} collective-permute-done((bf16[256,1536]{1,0:T(8,128)(2,1)}, bf16[256,1536]{1,0:T(8,128)(2,1)}, u32[]{:S(2)}, u32[]{:S(2)}) %collective-permute-start.2) | collective-permute-done | bytes 786464 | tf_op jit(solution)/shard_map/ppermute | solution.py:27
  132.7 1.5 convert_add_fusion
  135.9 10.0 %collective-permute-done.3 = bf16[128,1536]{1,0:T(8,128)(2,1)S(1)} collective-permute-done((bf16[128,1536]{1,0:T(8,128)(2,1)S(1)}, bf16[128,1536]{1,0:T(8,128)(2,1)S(1)}, u32[]{:S(2)}, u32[]{:S(2)}) %collective-permute-start.3) | collective-permute-done | bytes 393248 | tf_op jit(solution)/shard_map/ppermute | solution.py:27
  145.9 1.5 convert_add_fusion.1
  147.8 1.2 collective-permute-done.4
  150.2 56.8 %all-gather.6.cloned.1.call-done = bf16[1024,1664]{1,0:T(8,128)(2,1)} async-done(((bf16[64,1664]{1,0:T(8,128)(2,1)}), bf16[1024,1664]{1,0:T(8,128)(2,1)}) %all-gather.6.cloned.1.call-update) | async-done | bytes 3407888 | tf_op jit(solution)/shard_map/all_gather | solution.py:258
  207.3 24.2 %all-gather.8.cloned.1.call-done.rows_ref = bf16[2048,1664]{1,0:T(8,128)(2,1)} async-done(((bf16[1024,1664]{1,0:T(8,128)(2,1)}), bf16[2048,1664]{1,0:T(8,128)(2,1)}) %all-gather.8.cloned.1.call-update) | async-done | bytes 6815760 | tf_op jit(solution)/shard_map/all_gather | solution.py:259
  232.8 28.5 %shard_map.121 = bf16[2048,1536]{1,0:T(8,128)(2,1)} custom-call(bf16[2048,1664]{1,0:T(8,128)(2,1)} %all-gather.8.cloned.1.call-done.rows_ref, f32[2048,5]{1,0:T(8,128)S(1)} %dynamic-slice_convert_fusion.share_ref, bf16[5,1536,256]{2,1,0:T(8,128)(2,1)} %gate_up_ref.1, bf16[5,128,1536]{2,1,0:T(8,128)(2,1)S(1)} %copy-done), custom_call_target="tpu_custom_call" | custom-call | tf_op jit(solution)/shard_map/pallas_call | solution.py:114
  261.4 21.6 %reduce-scatter.3.cloned.1.call-done = bf16[1024,1536]{1,0:T(8,128)(2,1)} async-done(((bf16[2048,1536]{1,0:T(8,128)(2,1)}), bf16[1024,1536]{1,0:T(8,128)(2,1)}) %reduce-scatter.3.cloned.1.call-update) | async-done | bytes 3145744 | tf_op jit(solution)/shard_map/reduce_scatter | solution.py:267
  284.8 84.3 %reduce-scatter.5.cloned.1.call-done = bf16[64,1536]{1,0:T(8,128)(2,1)} async-done(((bf16[1024,1536]{1,0:T(8,128)(2,1)}), bf16[64,1536]{1,0:T(8,128)(2,1)}) %reduce-scatter.5.cloned.1.call-update) | async-done | bytes 196624 | tf_op jit(solution)/shard_map/reduce_scatter | solution.py:268
  369.1 1.7 fusion.19
  (156 shorter events, 30.3 us)
Async XLA Ops:
  7.2 15.1 %copy-start.7 = (bf16[1536,48]{0,1:T(8,128)(2,1)S(1)}, bf16[1536,48]{0,1:T(8,128)(2,1)}, u32[]{:S(2)}) copy-start(bf16[1536,48]{0,1:T(8,128)(2,1)} %param.20) | copy-start | bytes 442372
  7.2 15.1 %copy-start.6 = (bf16[1536,80]{0,1:T(8,128)(2,1)S(1)}, bf16[1536,80]{0,1:T(8,128)(2,1)}, u32[]{:S(2)}) copy-start(bf16[1536,80]{0,1:T(8,128)(2,1)} %param.19) | copy-start | bytes 737284
  7.2 4.9 %copy-start.10 = (s32[2048]{0:T(1024)S(1)}, s32[2048]{0:T(1024)}, u32[]{:S(2)}) copy-start(s32[2048]{0:T(1024)} %param.15) | copy-start | bytes 24580
  7.2 69.7 %all-gather.4.cloned.1.call-start = ((), (), s32[]{:S(2)}) async-start(), calls=%async_computation.2 | async-start | bytes 6488064 | tf_op jit(solution)/shard_map/all_gather | solution.py:171
  10.2 196.8 %all-gather.6.cloned.1.call-start = ((), (), s32[]{:S(2)}) async-start(), calls=%async_computation.3 | async-start | bytes 3620864 | tf_op jit(solution)/shard_map/all_gather | solution.py:258
  11.3 10.9 %collective-permute-start = (bf16[1536,128]{0,1:T(8,128)(2,1)S(1)}, bf16[1536,128]{0,1:T(8,128)(2,1)S(1)}, u32[]{:S(2)}, u32[]{:S(2)}) collective-permute-start(bf16[1536,128]{0,1:T(8,128)(2,1)S(1)} %pad_maximum_fusion.1), channel_id=1, source_target_pairs={{0,8},{1,9},{2,10},{3,11},{4,12},{5,13},{6,14},{7,15},{8,0},{9,1},... | collective-permute-start | bytes 1179656 | tf_op jit(solution)/shard_map/ppermute | solution.py:27
  22.4 23.2 %collective-permute-start.1 = (bf16[1536,256]{0,1:T(8,128)(2,1)S(1)}, bf16[1536,256]{0,1:T(8,128)(2,1)S(1)}, u32[]{:S(2)}, u32[]{:S(2)}) collective-permute-start(bf16[1536,256]{0,1:T(8,128)(2,1)S(1)} %maximum_select_fusion.1), channel_id=1, source_target_pairs={{0,16},{1,17},{2,18},{3,19},{4,20},{5,21},{6,22},{7,23},{8,24},{9,... | collective-permute-start | bytes 2359304 | tf_op jit(solution)/shard_map/ppermute | solution.py:27
  85.2 0.7 copy-start.2
  93.0 6.2 %copy-start.8 = (bf16[2,256,192]{1,2,0:T(8,128)(2,1)S(1)}, bf16[2,256,192]{1,2,0:T(8,128)(2,1)}, u32[]{:S(2)}) copy-start(bf16[2,256,192]{1,2,0:T(8,128)(2,1)} %get-tuple-element.515) | copy-start | bytes 589828 | tf_op jit(solution)/shard_map/while
  104.7 2.2 copy-start.8
  111.2 21.5 %collective-permute-start.2 = (bf16[256,1536]{1,0:T(8,128)(2,1)}, bf16[256,1536]{1,0:T(8,128)(2,1)}, u32[]{:S(2)}, u32[]{:S(2)}) collective-permute-start(bf16[256,1536]{1,0:T(8,128)(2,1)} %select_convert_fusion), channel_id=1, source_target_pairs={{0,4},{1,5},{2,6},{3,7},{4,0},{5,1},{6,2},{7,3},{8,12},{9,13},{10,... | collective-permute-start | bytes 2359304 | tf_op jit(solution)/shard_map/ppermute | solution.py:27
  134.2 1.2 copy-start.1
  135.4 10.5 %collective-permute-start.3 = (bf16[128,1536]{1,0:T(8,128)(2,1)S(1)}, bf16[128,1536]{1,0:T(8,128)(2,1)S(1)}, u32[]{:S(2)}, u32[]{:S(2)}) collective-permute-start(bf16[128,1536]{1,0:T(8,128)(2,1)S(1)} %select_convert_fusion.1), channel_id=1, source_target_pairs={{0,2},{1,3},{2,0},{3,1},{4,6},{5,7},{6,4},{7,5},{8,10},{9,11},{10,... | collective-permute-start | bytes 1179656 | tf_op jit(solution)/shard_map/ppermute | solution.py:27
  135.9 11.7 %copy-start.12 = (s32[64,8]{0,1:T(8,128)S(1)}, s32[64,8]{0,1:T(8,128)}, u32[]{:S(2)}) copy-start(s32[64,8]{0,1:T(8,128)} %param.16) | copy-start | bytes 6148
  135.9 11.7 %copy-start.13 = (bf16[64,8]{0,1:T(8,128)(2,1)S(1)}, bf16[64,8]{0,1:T(8,128)(2,1)}, u32[]{:S(2)}) copy-start(bf16[64,8]{0,1:T(8,128)(2,1)} %param.17) | copy-start | bytes 3076
  135.9 13.1 %copy-start.4 = (bf16[64,1536]{1,0:T(8,128)(2,1)S(1)}, bf16[64,1536]{1,0:T(8,128)(2,1)}, u32[]{:S(2)}) copy-start(bf16[64,1536]{1,0:T(8,128)(2,1)} %param.14) | copy-start | bytes 589828
  147.4 1.8 copy-start.11
  147.5 1.5 collective-permute-start.4
  149.2 219.9 %copy-start.5 = (bf16[64,1536]{1,0:T(8,128)(2,1)}, bf16[64,1536]{1,0:T(8,128)(2,1)S(1)}, u32[]{:S(2)}) copy-start(bf16[64,1536]{1,0:T(8,128)(2,1)S(1)} %get-tuple-element.307) | copy-start | bytes 589828
  150.2 81.4 %all-gather.8.cloned.1.call-start = ((), (), s32[]{:S(2)}) async-start(), calls=%async_computation.4 | async-start | bytes 10223616 | tf_op jit(solution)/shard_map/all_gather | solution.py:259
  207.1 25.8 %copy-start = (bf16[5,128,1536]{2,1,0:T(8,128)(2,1)S(1)}, bf16[5,128,1536]{2,1,0:T(8,128)(2,1)}, u32[]{:S(2)}) copy-start(bf16[5,128,1536]{2,1,0:T(8,128)(2,1)} %down_ref.1) | copy-start | bytes 5898244
  207.1 76.0 %reduce-scatter.3.cloned.1.call-start = ((), (), s32[]{:S(2)}) async-start(), calls=%async_computation.5 | async-start | bytes 9437184 | tf_op jit(solution)/shard_map/reduce_scatter | solution.py:267
  261.3 107.7 %reduce-scatter.5.cloned.1.call-start = ((), (), s32[]{:S(2)}) async-start(), calls=%async_computation.6 | async-start | bytes 3342336 | tf_op jit(solution)/shard_map/reduce_scatter | solution.py:268
  283.0 0.9 copy-start.3
  (2 other events, 1.4 us)
Sparse Core Ops, SparseCore 0:
  11.1 65.7 all-gather.3
  150.3 56.6 all-gather.5
  208.8 22.6 all-gather.7
  261.5 21.5 reduce-scatter.2
  286.5 82.5 reduce-scatter.4

commit v3 on v2

--- a/solution.py
+++ b/solution.py
@@ -93,9 +93,10 @@
 
 
 def expert_block(rows_ref, share_ref, gate_up_ref, down_ref, out_ref):
-    rows = rows_ref[...]
+    model_width = gate_up_ref.shape[1]
+    rows = rows_ref[:, :model_width]
     inner_width = down_ref.shape[1]
-    total = jnp.zeros(out_ref.shape, jnp.float32)
+    total = jnp.zeros((rows.shape[0], model_width), jnp.float32)
     for expert in range(gate_up_ref.shape[0]):
         both = jnp.dot(rows, gate_up_ref[expert], preferred_element_type=jnp.float32)
         gate_val = both[:, :inner_width]
@@ -103,28 +104,53 @@
         inner_act = (jax.nn.silu(gate_val) * up_val).astype(jnp.bfloat16)
         produced = jnp.dot(inner_act, down_ref[expert], preferred_element_type=jnp.float32)
         total = total + share_ref[:, expert : expert + 1] * produced
-    out_ref[...] = total.astype(out_ref.dtype)
+    piece = out_ref.shape[3]
+    for part in range(4):
+        out_ref[part % 2, part // 2, 0] = total[part * piece : (part + 1) * piece].astype(
+            out_ref.dtype
+        )
+
+
+def tile_slot(tile_number):
+    return (tile_number // 2) % 2 * 4 + (tile_number // 4) % 2 * 2 + tile_number % 2
 
 
 def dense_experts(rows_all, shares, gate_up, down_proj):
-    row_count = rows_all.shape[0]
+    row_count, carried_width = rows_all.shape
     model_width = gate_up.shape[1]
     expert_count = gate_up.shape[0]
-    tile = 256
+    piece = row_count // 32
+    tile = 4 * piece
+    tiles = row_count // tile
     return pl.pallas_call(
         expert_block,
-        grid=(row_count // tile,),
+        grid=(tiles,),
         in_specs=[
-            pl.BlockSpec((tile, model_width), lambda i: (i, 0)),
+            pl.BlockSpec((tile, carried_width), lambda i: (i, 0)),
             pl.BlockSpec((tile, expert_count), lambda i: (i, 0)),
             pl.BlockSpec(gate_up.shape, lambda i: (0, 0, 0)),
             pl.BlockSpec(down_proj.shape, lambda i: (0, 0, 0)),
         ],
-        out_specs=pl.BlockSpec((tile, model_width), lambda i: (i, 0)),
-        out_shape=jax.ShapeDtypeStruct((row_count, model_width), jnp.bfloat16),
+        out_specs=pl.BlockSpec(
+            (2, 2, 1, piece, model_width), lambda i: (0, 0, tile_slot(i), 0, 0)
+        ),
+        out_shape=jax.ShapeDtypeStruct((2, 2, tiles, piece, model_width), jnp.bfloat16),
         compiler_params=pltpu.CompilerParams(vmem_limit_bytes=48 * 1024 * 1024),
     )(rows_all, shares, gate_up, down_proj)
 
+
+def fold_bits(partial_sum, level_bits):
+    index_now = lax.axis_index(TENSOR)
+    for level_bit in level_bits:
+        half_rows = partial_sum.shape[0] // 2
+        lower_rows = partial_sum[:half_rows]
+        upper_rows = partial_sum[half_rows:]
+        is_upper = index_now >> level_bit & 1 == 1
+        kept_rows = jnp.where(is_upper, upper_rows, lower_rows)
+        sent_rows = jnp.where(is_upper, lower_rows, upper_rows)
+        arrived = partner(sent_rows.astype(jnp.bfloat16), TENSOR, level_bit)
+        partial_sum = kept_rows.astype(jnp.float32) + arrived.astype(jnp.float32)
+    return partial_sum
 
 def on_device(
     hidden, segment_ids, routes, route_weights, attn_gain, w_qkv, w_out, ffn_gain, w_gate_up, w_down
@@ -255,8 +281,7 @@
         ],
         axis=1,
     )
-    by_chip = lax.all_gather(carried, CHIPS, axis=0, tiled=True)
-    rows_all = lax.all_gather(by_chip, "tc", axis=0, tiled=True)
+    rows_all = lax.all_gather(carried, TENSOR, axis=0, tiled=True)
     local_shares = lax.dynamic_slice_in_dim(
         rows_all[:, model_width : model_width + expert_total],
         group_index * local_experts,
@@ -264,10 +289,7 @@
         1,
     ).astype(jnp.float32)
     expert_part = dense_experts(rows_all, local_shares, w_gate_up, w_down)
-    core_sum = lax.psum_scatter(expert_part, "tc", scatter_dimension=0, tiled=True)
-    expert_sum = lax.psum_scatter(core_sum, CHIPS, scatter_dimension=0, tiled=True).astype(
-        jnp.float32
-    )
+    expert_sum = fold_bits(expert_part.reshape(-1, model_width), (0, 1, 3, 4, 2))
     hidden_out = (after_attention.astype(jnp.float32) + residual_scale * expert_sum).astype(
         jnp.bfloat16
     )

time: 378 us -> 332 us (0.88)
  waiting for transfers between devices: 276 us -> 222 us
  starting transfers between devices: 4.95 us -> 9.81 us
  other arithmetic: 17.5 us -> 22.3 us
    reduce_scatter x2 -> x0, waiting for transfers between devices: 106 us -> none  [the longest x1 84.3 us: on_device(): lax.psum_scatter(core_sum, CHIPS, scatter_dimension=0, tiled=True)]
    ppermute x5 -> x10, waiting for transfers between devices: 59.3 us -> 133 us  [partner(): return lax.ppermute(value, axis, pairs)]
    all_gather x2 -> x1, waiting for transfers between devices: 81 us -> 58.3 us  [on_device(): rows_all = lax.all_gather(carried, TENSOR, axis=0, tiled=True)]
    ppermute x5 -> x10, starting transfers between devices: 4.57 us -> 9.73 us  [partner(): return lax.ppermute(value, axis, pairs)]
  transfers between devices with their start and end apart: 10 -> 12, of which waited for: 10 -> 12; matrix products, arithmetic and copies ran while one was open for 2% -> 2% of each run, Pallas kernels for 0% -> 0%
where the time goes in v3:
time: 332 us; the launch traced here: 330 us
  waiting for transfers between devices  222 us (67%)
  Pallas kernels  28.8 us (9%)
  other arithmetic  22.3 us (7%)
  between operations  15 us (5%)
  local copies, waits for them, and re-layouts  13.9 us (4%)
  matrix products  11.3 us (3%)
  starting transfers between devices  9.81 us (3%)
  loops' own time  7.34 us (2%)
    ppermute x10, waiting for transfers between devices, partner(): return lax.ppermute(value, axis, pairs)  133 us
    all_gather x1, waiting for transfers between devices, on_device(): rows_all = lax.all_gather(carried, TENSOR, axis=0, tiled=True)  58.3 us
    all_gather x1, waiting for transfers between devices, on_device(): all_rows = lax.all_gather(normed, TENSOR, axis=0, tiled=True)  30.1 us
    pallas_call x1, Pallas kernels, dense_experts(): pl.pallas_call(expert_block, grid=(tiles,), in_specs=[pl.BlockSpec((tile,...  28.8 us
    ppermute x10, starting transfers between devices, partner(): return lax.ppermute(value, axis, pairs)  9.73 us
    another operation x1, loops' own time, on_device(): lax.map(attend, jnp.arange(rows_quarter // block_rows, dtype=jnp.int32))  7.05 us
  transfers between devices with their start and end apart: 12, of which 12 were waited for; matrix products, arithmetic and copies ran while one was open for 2% of the time, Pallas kernels for 0%

profile of v3, /device:TPU:24, one launch (start us, length us, event | category | flops | bytes accessed | tf_op | source)
XLA Modules:
  0.0 330.2 jit_solution(16479356677777707212)
XLA Ops:
  8.5 1.7 fusion.14
  13.8 8.4 %collective-permute-done = bf16[1536,128]{0,1:T(8,128)(2,1)S(1)} collective-permute-done((bf16[1536,128]{0,1:T(8,128)(2,1)S(1)}, bf16[1536,128]{0,1:T(8,128)(2,1)S(1)}, u32[]{:S(2)}, u32[]{:S(2)}) %collective-permute-start) | collective-permute-done | bytes 393248 | tf_op jit(solution)/shard_map/ppermute | solution.py:27
  23.9 1.7 multiply_cosine_fusion.1
  25.6 20.0 %collective-permute-done.1 = bf16[1536,256]{0,1:T(8,128)(2,1)S(1)} collective-permute-done((bf16[1536,256]{0,1:T(8,128)(2,1)S(1)}, bf16[1536,256]{0,1:T(8,128)(2,1)S(1)}, u32[]{:S(2)}, u32[]{:S(2)}) %collective-permute-start.1) | collective-permute-done | bytes 786464 | tf_op jit(solution)/shard_map/ppermute | solution.py:27
  46.8 30.1 %all-gather.3.cloned.1.call-done = bf16[2048,1536]{1,0:T(8,128)(2,1)} async-done(((bf16[64,1536]{1,0:T(8,128)(2,1)}), bf16[2048,1536]{1,0:T(8,128)(2,1)}) %all-gather.3.cloned.1.call-update) | async-done | bytes 6291472 | tf_op jit(solution)/shard_map/all_gather | solution.py:197
  76.9 4.9 %fusion.20 = f32[2048,128]{0,1:T(8,128)S(1)} fusion(bf16[2048,1536]{1,0:T(8,128)(2,1)} %all-gather.3.cloned.1.call-done, bf16[1536,320]{0,1:T(8,128)(2,1)S(1)} %bitcast.59), kind=kOutput, calls=%fused_computation.58 | convolution fusion | flops 805306368 | bytes 7733248 | tf_op jit(solution)/shard_map/dot_general | solution.py:90
  81.9 2.1 fusion.9
  88.2 17.2 %while.59 = (s32[]{:T(128)}, bf16[2,256,192]{1,2,0:T(8,128)(2,1)}, s32[2]{0:T(128)S(1)}, s32[]{:T(128)}, s32[2048]{0:T(1024)S(1)}, /*index=5*/bf16[3,512,64]{2,1...) while((s32[]{:T(128)}, bf16[2,256,192]{1,2,0:T(8,128)(2,1)}, ...), condition=%wide.region_8.9_spmd, body=%wide.region_3.8_spmd.sunk | while | flops 104007976 | bytes 10327068 | solution.py:257
  92.9 4.0 %while.60 = (s32[]{:T(128)}, f32[768]{0:T(1024)S(1)}, f32[768]{0:T(1024)S(1)}, f32[768,64]{0,1:T(8,128)S(1)}, s32[]{:T(128)}, /*index=5*/s32[256]{0:T(256)S(1)},...) while((s32[]{:T(128)}, f32[768]{0:T(1024)S(1)}, ...), condition=%wide.region_7.7_spmd.clone, body=%wide.region_4.6_spmd.clone.sunk | while | flops 103909632 | bytes 7464147 | solution.py:253
  102.5 2.0 while.60
  106.3 1.7 fusion.38
  109.0 1.9 collective-permute-start.2
  110.9 19.6 %collective-permute-done.2 = bf16[256,1536]{1,0:T(8,128)(2,1)} collective-permute-done((bf16[256,1536]{1,0:T(8,128)(2,1)}, bf16[256,1536]{1,0:T(8,128)(2,1)}, u32[]{:S(2)}, u32[]{:S(2)}) %collective-permute-start.2) | collective-permute-done | bytes 786464 | tf_op jit(solution)/shard_map/ppermute | solution.py:27
  133.7 10.0 %collective-permute-done.3 = bf16[128,1536]{1,0:T(8,128)(2,1)S(1)} collective-permute-done((bf16[128,1536]{1,0:T(8,128)(2,1)S(1)}, bf16[128,1536]{1,0:T(8,128)(2,1)S(1)}, u32[]{:S(2)}, u32[]{:S(2)}) %collective-permute-start.3) | collective-permute-done | bytes 393248 | tf_op jit(solution)/shard_map/ppermute | solution.py:27
  148.2 58.3 %all-gather.5.cloned.1.call-done.rows_ref = bf16[2048,1664]{1,0:T(8,128)(2,1)} async-done(((bf16[64,1664]{1,0:T(8,128)(2,1)}), bf16[2048,1664]{1,0:T(8,128)(2,1)}) %all-gather.5.cloned.1.call-update) | async-done | bytes 6815760 | tf_op jit(solution)/shard_map/all_gather | solution.py:284
  207.9 28.8 %shard_map.121 = bf16[2,2,8,64,1536]{4,3,2,1,0:T(8,128)(2,1)} custom-call(bf16[2048,1664]{1,0:T(8,128)(2,1)} %all-gather.5.cloned.1.call-done.rows_ref, f32[2048,5]{1,0:T(8,128)S(1)} %dynamic-slice_convert_fusion.share_ref, bf16[5,1536,256]{2,1,0:T(8,128)(2,1)} %gate_up_ref.1, bf16[5,128,1536]{2,1,0:T(8,128)(2,1)S(1)} %copy-done), custom_call_target="tpu_custom_call" | custom-call | tf_op jit(solution)/shard_map/pallas_call | solution.py:125
  236.7 3.1 broadcast_select_fusion.1
  240.1 5.4 %collective-permute-done.5 = bf16[1024,1536]{1,0:T(8,128)(2,1)S(1)} collective-permute-done((bf16[1024,1536]{1,0:T(8,128)(2,1)S(1)}, bf16[1024,1536]{1,0:T(8,128)(2,1)S(1)}, u32[]{:S(2)}, u32[]{:S(2)}) %collective-permute-start.5) | collective-permute-done | bytes 3145760 | tf_op jit(solution)/shard_map/ppermute | solution.py:27
  247.3 36.3 %collective-permute-done.6 = bf16[512,1536]{1,0:T(8,128)(2,1)S(1)} collective-permute-done((bf16[512,1536]{1,0:T(8,128)(2,1)S(1)}, bf16[512,1536]{1,0:T(8,128)(2,1)S(1)}, u32[]{:S(2)}, u32[]{:S(2)}) %collective-permute-start.6) | collective-permute-done | bytes 1572896 | tf_op jit(solution)/shard_map/ppermute | solution.py:27
  285.5 18.0 %collective-permute-done.7 = bf16[256,1536]{1,0:T(8,128)(2,1)S(1)} collective-permute-done((bf16[256,1536]{1,0:T(8,128)(2,1)S(1)}, bf16[256,1536]{1,0:T(8,128)(2,1)S(1)}, u32[]{:S(2)}, u32[]{:S(2)}) %collective-permute-start.7) | collective-permute-done | bytes 786464 | tf_op jit(solution)/shard_map/ppermute | solution.py:27
  304.0 1.5 collective-permute-start.8
  305.5 9.6 %collective-permute-done.8 = bf16[128,1536]{1,0:T(8,128)(2,1)S(1)} collective-permute-done((bf16[128,1536]{1,0:T(8,128)(2,1)S(1)}, bf16[128,1536]{1,0:T(8,128)(2,1)S(1)}, u32[]{:S(2)}, u32[]{:S(2)}) %collective-permute-start.8) | collective-permute-done | bytes 393248 | tf_op jit(solution)/shard_map/ppermute | solution.py:27
  315.3 1.9 collective-permute-start.9
  318.0 4.6 %collective-permute-done.9 = bf16[64,1536]{1,0:T(8,128)(2,1)S(1)} collective-permute-done((bf16[64,1536]{1,0:T(8,128)(2,1)S(1)}, bf16[64,1536]{1,0:T(8,128)(2,1)S(1)}, u32[]{:S(2)}, u32[]{:S(2)}) %collective-permute-start.9) | collective-permute-done | bytes 196640 | tf_op jit(solution)/shard_map/ppermute | solution.py:27
  (155 shorter events, 38.2 us)
Async XLA Ops:
  7.2 15.1 %copy-start.7 = (bf16[1536,48]{0,1:T(8,128)(2,1)S(1)}, bf16[1536,48]{0,1:T(8,128)(2,1)}, u32[]{:S(2)}) copy-start(bf16[1536,48]{0,1:T(8,128)(2,1)} %param.20) | copy-start | bytes 442372
  7.2 15.1 %copy-start.6 = (bf16[1536,80]{0,1:T(8,128)(2,1)S(1)}, bf16[1536,80]{0,1:T(8,128)(2,1)}, u32[]{:S(2)}) copy-start(bf16[1536,80]{0,1:T(8,128)(2,1)} %param.19) | copy-start | bytes 737284
  7.2 4.9 %copy-start.10 = (s32[2048]{0:T(1024)S(1)}, s32[2048]{0:T(1024)}, u32[]{:S(2)}) copy-start(s32[2048]{0:T(1024)} %param.15) | copy-start | bytes 24580
  7.2 69.7 %all-gather.3.cloned.1.call-start = ((), (), s32[]{:S(2)}) async-start(), calls=%async_computation | async-start | bytes 6488064 | tf_op jit(solution)/shard_map/all_gather | solution.py:197
  10.2 196.4 %all-gather.5.cloned.1.call-start = ((), (), s32[]{:S(2)}) async-start(), calls=%async_computation.1 | async-start | bytes 7028736 | tf_op jit(solution)/shard_map/all_gather | solution.py:284
  11.3 10.9 %collective-permute-start = (bf16[1536,128]{0,1:T(8,128)(2,1)S(1)}, bf16[1536,128]{0,1:T(8,128)(2,1)S(1)}, u32[]{:S(2)}, u32[]{:S(2)}) collective-permute-start(bf16[1536,128]{0,1:T(8,128)(2,1)S(1)} %pad_maximum_fusion.1), channel_id=1, source_target_pairs={{0,8},{1,9},{2,10},{3,11},{4,12},{5,13},{6,14},{7,15},{8,0},{9,1},... | collective-permute-start | bytes 1179656 | tf_op jit(solution)/shard_map/ppermute | solution.py:27
  22.4 23.2 %collective-permute-start.1 = (bf16[1536,256]{0,1:T(8,128)(2,1)S(1)}, bf16[1536,256]{0,1:T(8,128)(2,1)S(1)}, u32[]{:S(2)}, u32[]{:S(2)}) collective-permute-start(bf16[1536,256]{0,1:T(8,128)(2,1)S(1)} %maximum_select_fusion.1), channel_id=1, source_target_pairs={{0,16},{1,17},{2,18},{3,19},{4,20},{5,21},{6,22},{7,23},{8,24},{9,... | collective-permute-start | bytes 2359304 | tf_op jit(solution)/shard_map/ppermute | solution.py:27
  92.9 4.2 %copy-start.8 = (bf16[2,256,192]{1,2,0:T(8,128)(2,1)S(1)}, bf16[2,256,192]{1,2,0:T(8,128)(2,1)}, u32[]{:S(2)}) copy-start(bf16[2,256,192]{1,2,0:T(8,128)(2,1)} %get-tuple-element.517) | copy-start | bytes 589828 | tf_op jit(solution)/shard_map/while
  102.5 2.1 copy-start.8
  109.0 21.5 %collective-permute-start.2 = (bf16[256,1536]{1,0:T(8,128)(2,1)}, bf16[256,1536]{1,0:T(8,128)(2,1)}, u32[]{:S(2)}, u32[]{:S(2)}) collective-permute-start(bf16[256,1536]{1,0:T(8,128)(2,1)} %select_convert_fusion.2), channel_id=1, source_target_pairs={{0,4},{1,5},{2,6},{3,7},{4,0},{5,1},{6,2},{7,3},{8,12},{9,13},{10,... | collective-permute-start | bytes 2359304 | tf_op jit(solution)/shard_map/ppermute | solution.py:27
  133.3 10.5 %collective-permute-start.3 = (bf16[128,1536]{1,0:T(8,128)(2,1)S(1)}, bf16[128,1536]{1,0:T(8,128)(2,1)S(1)}, u32[]{:S(2)}, u32[]{:S(2)}) collective-permute-start(bf16[128,1536]{1,0:T(8,128)(2,1)S(1)} %select_convert_fusion.4), channel_id=1, source_target_pairs={{0,2},{1,3},{2,0},{3,1},{4,6},{5,7},{6,4},{7,5},{8,10},{9,11},{10,... | collective-permute-start | bytes 1179656 | tf_op jit(solution)/shard_map/ppermute | solution.py:27
  133.7 11.9 %copy-start.12 = (s32[64,8]{0,1:T(8,128)S(1)}, s32[64,8]{0,1:T(8,128)}, u32[]{:S(2)}) copy-start(s32[64,8]{0,1:T(8,128)} %param.16) | copy-start | bytes 6148
  133.7 11.9 %copy-start.13 = (bf16[64,8]{0,1:T(8,128)(2,1)S(1)}, bf16[64,8]{0,1:T(8,128)(2,1)}, u32[]{:S(2)}) copy-start(bf16[64,8]{0,1:T(8,128)(2,1)} %param.17) | copy-start | bytes 3076
  133.7 13.3 %copy-start.5 = (bf16[64,1536]{1,0:T(8,128)(2,1)S(1)}, bf16[64,1536]{1,0:T(8,128)(2,1)}, u32[]{:S(2)}) copy-start(bf16[64,1536]{1,0:T(8,128)(2,1)} %param.14) | copy-start | bytes 589828
  145.3 2.0 copy-start.11
  145.3 1.7 collective-permute-start.4
  147.2 175.3 %copy-start.4 = (bf16[64,1536]{1,0:T(8,128)(2,1)}, bf16[64,1536]{1,0:T(8,128)(2,1)S(1)}, u32[]{:S(2)}) copy-start(bf16[64,1536]{1,0:T(8,128)(2,1)S(1)} %get-tuple-element.307) | copy-start | bytes 589828
  147.4 60.5 %copy-start = (bf16[5,128,1536]{2,1,0:T(8,128)(2,1)S(1)}, bf16[5,128,1536]{2,1,0:T(8,128)(2,1)}, u32[]{:S(2)}) copy-start(bf16[5,128,1536]{2,1,0:T(8,128)(2,1)} %down_ref.1) | copy-start | bytes 5898244
  239.8 5.7 %collective-permute-start.5 = (bf16[1024,1536]{1,0:T(8,128)(2,1)S(1)}, bf16[1024,1536]{1,0:T(8,128)(2,1)S(1)}, u32[]{:S(2)}, u32[]{:S(2)}) collective-permute-start(bf16[1024,1536]{1,0:T(8,128)(2,1)S(1)} %bitcast.56), channel_id=1, source_target_pairs={{0,1},{1,0},{2,3},{3,2},{4,5},{5,4},{6,7},{7,6},{8,9},{9,8},{10,11... | collective-permute-start | bytes 9437192 | tf_op jit(solution)/shard_map/ppermute | solution.py:27
  246.9 36.6 %collective-permute-start.6 = (bf16[512,1536]{1,0:T(8,128)(2,1)S(1)}, bf16[512,1536]{1,0:T(8,128)(2,1)S(1)}, u32[]{:S(2)}, u32[]{:S(2)}) collective-permute-start(bf16[512,1536]{1,0:T(8,128)(2,1)S(1)} %select_convert_fusion), channel_id=1, source_target_pairs={{0,2},{1,3},{2,0},{3,1},{4,6},{5,7},{6,4},{7,5},{8,10},{9,11},{10,... | collective-permute-start | bytes 4718600 | tf_op jit(solution)/shard_map/ppermute | solution.py:27
  284.6 18.9 %collective-permute-start.7 = (bf16[256,1536]{1,0:T(8,128)(2,1)S(1)}, bf16[256,1536]{1,0:T(8,128)(2,1)S(1)}, u32[]{:S(2)}, u32[]{:S(2)}) collective-permute-start(bf16[256,1536]{1,0:T(8,128)(2,1)S(1)} %select_convert_fusion.1), channel_id=1, source_target_pairs={{0,8},{1,9},{2,10},{3,11},{4,12},{5,13},{6,14},{7,15},{8,0},{9,1},... | collective-permute-start | bytes 2359304 | tf_op jit(solution)/shard_map/ppermute | solution.py:27
  304.0 13.2 %copy-start.3 = (bf16[2048,64]{0,1:T(8,128)(2,1)S(1)}, bf16[2048,64]{0,1:T(8,128)(2,1)}, u32[]{:S(2)}) copy-start(bf16[2048,64]{0,1:T(8,128)(2,1)} %copy-done.2) | copy-start | bytes 786436
  304.0 11.1 %collective-permute-start.8 = (bf16[128,1536]{1,0:T(8,128)(2,1)S(1)}, bf16[128,1536]{1,0:T(8,128)(2,1)S(1)}, u32[]{:S(2)}, u32[]{:S(2)}) collective-permute-start(bf16[128,1536]{1,0:T(8,128)(2,1)S(1)} %select_convert_fusion.3), channel_id=1, source_target_pairs={{0,16},{1,17},{2,18},{3,19},{4,20},{5,21},{6,22},{7,23},{8,24},{9,... | collective-permute-start | bytes 1179656 | tf_op jit(solution)/shard_map/ppermute | solution.py:27
  315.3 7.3 %collective-permute-start.9 = (bf16[64,1536]{1,0:T(8,128)(2,1)S(1)}, bf16[64,1536]{1,0:T(8,128)(2,1)S(1)}, u32[]{:S(2)}, u32[]{:S(2)}) collective-permute-start(bf16[64,1536]{1,0:T(8,128)(2,1)S(1)} %select_convert_fusion.5), channel_id=1, source_target_pairs={{0,4},{1,5},{2,6},{3,7},{4,0},{5,1},{6,2},{7,3},{8,12},{9,13},{10,... | collective-permute-start | bytes 589832 | tf_op jit(solution)/shard_map/ppermute | solution.py:27
  (4 other events, 3.2 us)
Sparse Core Ops, SparseCore 0:
  11.1 65.7 all-gather.2
  148.3 58.1 all-gather.4

commit v4 on v3

--- a/solution.py
+++ b/solution.py
@@ -194,10 +194,19 @@
     w_attn_out = by_quarter[:, :, qkv_width:].reshape(model_width, GQ * HD)
     w_query = w_group[:, : GQ * HD]
     w_pairs = w_group[:, GQ * HD :]
-    all_rows = lax.all_gather(normed, TENSOR, axis=0, tiled=True)
-    own_rows = lax.dynamic_slice_in_dim(all_rows, quarter_index * rows_quarter, rows_quarter, 0)
-    key_values = project_pairs(all_rows, w_pairs, positions)
-    kv_block = lax.dynamic_slice_in_dim(key_values, quarter_index * rows_quarter, rows_quarter, 0)
+    (own_rows,) = gather_levels(
+        (normed,),
+        group_bits,
+        (0,),
+        lambda payload, level_bit: (partner(payload[0], TENSOR, level_bit),),
+    )
+    kv_block = project_pairs(own_rows, w_pairs, own_positions)
+    (key_values,) = gather_levels(
+        (kv_block,),
+        quarter_bits,
+        (0,),
+        lambda payload, level_bit: (partner(payload[0], TENSOR, level_bit),),
+    )
     query_proj = jnp.dot(own_rows, w_query, preferred_element_type=jnp.float32).reshape(
         rows_quarter, GQ, HD
     )

time: 332 us -> 296 us (0.89)
  waiting for transfers between devices: 222 us -> 183 us
  starting transfers between devices: 9.81 us -> 20.4 us
    all_gather x1 -> x0, waiting for transfers between devices: 30.1 us -> none  [on_device(): all_rows = lax.all_gather(normed, TENSOR, axis=0, tiled=True)]
    ppermute x10 -> x15, starting transfers between devices: 9.73 us -> 20.4 us  [partner(): return lax.ppermute(value, axis, pairs)]
    ppermute x10 -> x15, waiting for transfers between devices: 133 us -> 123 us  [partner(): return lax.ppermute(value, axis, pairs)]
    select_n x2 -> x6, other arithmetic: 0.4 us -> 4.09 us  [gather_levels(): joined_parts.append(jnp.where(is_upper, upper_first, lower_first))]
  transfers between devices with their start and end apart: 12 -> 16, of which waited for: 12 -> 14; matrix products, arithmetic and copies ran while one was open for 2% -> 4% of each run, Pallas kernels for 0% -> 0%
where the time goes in v4:
time: 296 us; the launch traced here: 295 us
  waiting for transfers between devices  183 us (62%)
  Pallas kernels  28.9 us (10%)
  starting transfers between devices  20.4 us (7%)
  other arithmetic  20 us (7%)
  between operations  15.2 us (5%)
  local copies, waits for them, and re-layouts  11.6 us (4%)
  matrix products  8.35 us (3%)
  loops' own time  7.31 us (2%)
    ppermute x15, waiting for transfers between devices, partner(): return lax.ppermute(value, axis, pairs)  123 us
    all_gather x1, waiting for transfers between devices, on_device(): rows_all = lax.all_gather(carried, TENSOR, axis=0, tiled=True)  59.9 us
    pallas_call x1, Pallas kernels, dense_experts(): pl.pallas_call(expert_block, grid=(tiles,), in_specs=[pl.BlockSpec((tile,...  28.9 us
    ppermute x15, starting transfers between devices, partner(): return lax.ppermute(value, axis, pairs)  20.4 us
    another operation x1, loops' own time, on_device(): lax.map(attend, jnp.arange(rows_quarter // block_rows, dtype=jnp.int32))  7.03 us
  transfers between devices with their start and end apart: 16, of which 14 were waited for; matrix products, arithmetic and copies ran while one was open for 4% of the time, Pallas kernels for 0%

profile of v4, /device:TPU:24, one launch (start us, length us, event | category | flops | bytes accessed | tf_op | source)
XLA Modules:
  0.0 294.6 jit_solution(4214878051224788321)
XLA Ops:
  15.6 6.7 %collective-permute-done.3 = bf16[1536,128]{0,1:T(8,128)(2,1)S(1)} collective-permute-done((bf16[1536,128]{0,1:T(8,128)(2,1)S(1)}, bf16[1536,128]{0,1:T(8,128)(2,1)S(1)}, u32[]{:S(2)}, u32[]{:S(2)}) %collective-permute-start.3) | collective-permute-done | bytes 393248 | tf_op jit(solution)/shard_map/ppermute | solution.py:27
  22.4 1.7 collective-permute-start.4
  25.8 3.0 %collective-permute-start.2 = (bf16[256,1536]{1,0:T(8,128)(2,1)}, bf16[256,1536]{1,0:T(8,128)(2,1)}, u32[]{:S(2)}, u32[]{:S(2)}) collective-permute-start(bf16[256,1536]{1,0:T(8,128)(2,1)} %maximum_select_fusion.2), channel_id=1, source_target_pairs={{0,4},{1,5},{2,6},{3,7},{4,0},{5,1},{6,2},{7,3},{8,12},{9,13},{10,... | collective-permute-start | bytes 2359304 | tf_op jit(solution)/shard_map/ppermute | solution.py:27
  30.0 13.1 %collective-permute-done.4 = bf16[1536,256]{0,1:T(8,128)(2,1)S(1)} collective-permute-done((bf16[1536,256]{0,1:T(8,128)(2,1)S(1)}, bf16[1536,256]{0,1:T(8,128)(2,1)S(1)}, u32[]{:S(2)}, u32[]{:S(2)}) %collective-permute-start.4) | collective-permute-done | bytes 786464 | tf_op jit(solution)/shard_map/ppermute | solution.py:27
  44.0 1.6 maximum_select_fusion.1
  46.8 2.5 fusion.19
  51.3 2.5 fusion.9
  56.7 2.3 collective-permute-start.6
  59.5 5.2 %collective-permute-done.6 = bf16[1024,128]{0,1:T(8,128)(2,1)S(1)} collective-permute-done((bf16[1024,128]{0,1:T(8,128)(2,1)S(1)}, bf16[1024,128]{0,1:T(8,128)(2,1)S(1)}, u32[]{:S(2)}, u32[]{:S(2)}) %collective-permute-start.6) | collective-permute-done | bytes 262176 | tf_op jit(solution)/shard_map/ppermute | solution.py:27
  65.1 15.9 %while.59 = (s32[]{:T(128)}, bf16[2,256,192]{1,2,0:T(8,128)(2,1)S(1)}, s32[2]{0:T(128)S(1)}, s32[]{:T(128)}, s32[2048]{0:T(1024)S(1)}, /*index=5*/bf16[3,512,64]...) while((s32[]{:T(128)}, ...), condition=%wide.region_8.9_spmd, body=%wide.region_3.8_spmd.sunk | while | flops 104007976 | bytes 8754148 | solution.py:266
  69.9 4.0 %while.60 = (s32[]{:T(128)}, f32[768]{0:T(1024)S(1)}, f32[768]{0:T(1024)S(1)}, f32[768,64]{0,1:T(8,128)S(1)}, s32[]{:T(128)}, /*index=5*/s32[256]{0:T(256)S(1)},...) while((s32[]{:T(128)}, f32[768]{0:T(1024)S(1)}, ...), condition=%wide.region_7.7_spmd.clone, body=%wide.region_4.6_spmd.clone.sunk | while | flops 103909632 | bytes 7464147 | solution.py:262
  78.8 2.0 while.60
  81.8 3.3 %collective-permute-start.7 = (bf16[256,1536]{1,0:T(8,128)(2,1)S(1)}, bf16[256,1536]{1,0:T(8,128)(2,1)S(1)}, u32[]{:S(2)}, u32[]{:S(2)}) collective-permute-start(bf16[256,1536]{1,0:T(8,128)(2,1)S(1)} %select_convert_fusion.2), channel_id=1, source_target_pairs={{0,4},{1,5},{2,6},{3,7},{4,0},{5,1},{6,2},{7,3},{8,12},{9,13},{10,... | collective-permute-start | bytes 2359304 | tf_op jit(solution)/shard_map/ppermute | solution.py:27
  85.1 14.7 %collective-permute-done.7 = bf16[256,1536]{1,0:T(8,128)(2,1)S(1)} collective-permute-done((bf16[256,1536]{1,0:T(8,128)(2,1)S(1)}, bf16[256,1536]{1,0:T(8,128)(2,1)S(1)}, u32[]{:S(2)}, u32[]{:S(2)}) %collective-permute-start.7) | collective-permute-done | bytes 786464 | tf_op jit(solution)/shard_map/ppermute | solution.py:27
  101.8 6.3 %collective-permute-done.8 = bf16[128,1536]{1,0:T(8,128)(2,1)S(1)} collective-permute-done((bf16[128,1536]{1,0:T(8,128)(2,1)S(1)}, bf16[128,1536]{1,0:T(8,128)(2,1)S(1)}, u32[]{:S(2)}, u32[]{:S(2)}) %collective-permute-start.8) | collective-permute-done | bytes 393248 | tf_op jit(solution)/shard_map/ppermute | solution.py:27
  111.1 59.9 %all-gather.2.cloned.1.call-done.rows_ref = bf16[2048,1664]{1,0:T(8,128)(2,1)} async-done(((bf16[64,1664]{1,0:T(8,128)(2,1)}), bf16[2048,1664]{1,0:T(8,128)(2,1)}) %all-gather.2.cloned.1.call-update) | async-done | bytes 6815760 | tf_op jit(solution)/shard_map/all_gather | solution.py:293
  172.3 28.9 %shard_map.121 = bf16[2,2,8,64,1536]{4,3,2,1,0:T(8,128)(2,1)} custom-call(bf16[2048,1664]{1,0:T(8,128)(2,1)} %all-gather.2.cloned.1.call-done.rows_ref, f32[2048,5]{1,0:T(8,128)S(1)} %dynamic-slice_convert_fusion.share_ref, bf16[5,1536,256]{2,1,0:T(8,128)(2,1)} %gate_up_ref.1, bf16[5,128,1536]{2,1,0:T(8,128)(2,1)S(1)} %copy-done), custom_call_target="tpu_custom_call" | custom-call | tf_op jit(solution)/shard_map/pallas_call | solution.py:125
  201.1 3.1 %broadcast_select_fusion.1 = (bf16[1,2,8,64,1536]{4,3,2,1,0:T(8,128)(2,1)S(1)}, bf16[1,2,8,64,1536]{4,3,2,1,0:T(8,128)(2,1)S(1)}) fusion(pred[]{:T(512)S(6)} %eq.18, bf16[2,2,8,64,1536]{4,3,2,1,0:T(8,128)(2,1)} %shard_map.121), kind=kLoop, calls=%fused_computation.22 | loop fusion | flops 3145728 | bytes 12582913 | tf_op jit(solution)/shard_map/jit(_where)/select_n | solution.py:149
  204.5 5.4 %collective-permute-done.10 = bf16[1024,1536]{1,0:T(8,128)(2,1)S(1)} collective-permute-done((bf16[1024,1536]{1,0:T(8,128)(2,1)S(1)}, bf16[1024,1536]{1,0:T(8,128)(2,1)S(1)}, u32[]{:S(2)}, u32[]{:S(2)}) %collective-permute-start.10) | collective-permute-done | bytes 3145760 | tf_op jit(solution)/shard_map/ppermute | solution.py:27
  211.7 36.3 %collective-permute-done.11 = bf16[512,1536]{1,0:T(8,128)(2,1)S(1)} collective-permute-done((bf16[512,1536]{1,0:T(8,128)(2,1)S(1)}, bf16[512,1536]{1,0:T(8,128)(2,1)S(1)}, u32[]{:S(2)}, u32[]{:S(2)}) %collective-permute-start.11) | collective-permute-done | bytes 1572896 | tf_op jit(solution)/shard_map/ppermute | solution.py:27
  249.9 18.0 %collective-permute-done.12 = bf16[256,1536]{1,0:T(8,128)(2,1)S(1)} collective-permute-done((bf16[256,1536]{1,0:T(8,128)(2,1)S(1)}, bf16[256,1536]{1,0:T(8,128)(2,1)S(1)}, u32[]{:S(2)}, u32[]{:S(2)}) %collective-permute-start.12) | collective-permute-done | bytes 786464 | tf_op jit(solution)/shard_map/ppermute | solution.py:27
  269.8 9.6 %collective-permute-done.13 = bf16[128,1536]{1,0:T(8,128)(2,1)S(1)} collective-permute-done((bf16[128,1536]{1,0:T(8,128)(2,1)S(1)}, bf16[128,1536]{1,0:T(8,128)(2,1)S(1)}, u32[]{:S(2)}, u32[]{:S(2)}) %collective-permute-start.13) | collective-permute-done | bytes 393248 | tf_op jit(solution)/shard_map/ppermute | solution.py:27
  279.7 1.9 collective-permute-start.14
  282.4 4.6 %collective-permute-done.14 = bf16[64,1536]{1,0:T(8,128)(2,1)S(1)} collective-permute-done((bf16[64,1536]{1,0:T(8,128)(2,1)S(1)}, bf16[64,1536]{1,0:T(8,128)(2,1)S(1)}, u32[]{:S(2)}, u32[]{:S(2)}) %collective-permute-start.14) | collective-permute-done | bytes 196640 | tf_op jit(solution)/shard_map/ppermute | solution.py:27
  (157 shorter events, 41.4 us)
Async XLA Ops:
  7.2 15.1 %copy-start.6 = (bf16[1536,48]{0,1:T(8,128)(2,1)S(1)}, bf16[1536,48]{0,1:T(8,128)(2,1)}, u32[]{:S(2)}) copy-start(bf16[1536,48]{0,1:T(8,128)(2,1)} %param.20) | copy-start | bytes 442372
  7.2 15.1 %copy-start.4 = (bf16[1536,80]{0,1:T(8,128)(2,1)S(1)}, bf16[1536,80]{0,1:T(8,128)(2,1)}, u32[]{:S(2)}) copy-start(bf16[1536,80]{0,1:T(8,128)(2,1)} %param.19) | copy-start | bytes 737284
  7.2 163.8 %all-gather.2.cloned.1.call-start = ((), (), s32[]{:S(2)}) async-start(), calls=%async_computation | async-start | bytes 7028736 | tf_op jit(solution)/shard_map/all_gather | solution.py:293
  9.5 3.8 %collective-permute-start = (bf16[64,1536]{1,0:T(8,128)(2,1)S(1)}, bf16[64,1536]{1,0:T(8,128)(2,1)S(1)}, u32[]{:S(2)}, u32[]{:S(2)}) collective-permute-start(bf16[64,1536]{1,0:T(8,128)(2,1)S(1)} %fusion.13), channel_id=1, source_target_pairs={{0,1},{1,0},{2,3},{3,2},{4,5},{5,4},{6,7},{7,6},{8,9},{9,8},{10,11... | collective-permute-start | bytes 589832 | tf_op jit(solution)/shard_map/ppermute | solution.py:27
  10.7 11.6 %collective-permute-start.3 = (bf16[1536,128]{0,1:T(8,128)(2,1)S(1)}, bf16[1536,128]{0,1:T(8,128)(2,1)S(1)}, u32[]{:S(2)}, u32[]{:S(2)}) collective-permute-start(bf16[1536,128]{0,1:T(8,128)(2,1)S(1)} %pad_maximum_fusion), channel_id=1, source_target_pairs={{0,8},{1,9},{2,10},{3,11},{4,12},{5,13},{6,14},{7,15},{8,0},{9,1},... | collective-permute-start | bytes 1179656 | tf_op jit(solution)/shard_map/ppermute | solution.py:27
  13.4 11.3 %collective-permute-start.1 = (bf16[128,1536]{1,0:T(8,128)(2,1)S(1)}, bf16[128,1536]{1,0:T(8,128)(2,1)S(1)}, u32[]{:S(2)}, u32[]{:S(2)}) collective-permute-start(bf16[128,1536]{1,0:T(8,128)(2,1)S(1)} %maximum_select_fusion.5), channel_id=1, source_target_pairs={{0,2},{1,3},{2,0},{3,1},{4,6},{5,7},{6,4},{7,5},{8,10},{9,11},{10,... | collective-permute-start | bytes 1179656 | tf_op jit(solution)/shard_map/ppermute | solution.py:27
  22.4 20.7 %collective-permute-start.4 = (bf16[1536,256]{0,1:T(8,128)(2,1)S(1)}, bf16[1536,256]{0,1:T(8,128)(2,1)S(1)}, u32[]{:S(2)}, u32[]{:S(2)}) collective-permute-start(bf16[1536,256]{0,1:T(8,128)(2,1)S(1)} %maximum_select_fusion.3), channel_id=1, source_target_pairs={{0,16},{1,17},{2,18},{3,19},{4,20},{5,21},{6,22},{7,23},{8,24},{9,... | collective-permute-start | bytes 2359304 | tf_op jit(solution)/shard_map/ppermute | solution.py:27
  25.8 21.0 %collective-permute-start.2 = (bf16[256,1536]{1,0:T(8,128)(2,1)}, bf16[256,1536]{1,0:T(8,128)(2,1)}, u32[]{:S(2)}, u32[]{:S(2)}) collective-permute-start(bf16[256,1536]{1,0:T(8,128)(2,1)} %maximum_select_fusion.2), channel_id=1, source_target_pairs={{0,4},{1,5},{2,6},{3,7},{4,0},{5,1},{6,2},{7,3},{8,12},{9,13},{10,... | collective-permute-start | bytes 2359304 | tf_op jit(solution)/shard_map/ppermute | solution.py:27
  50.4 5.3 %collective-permute-start.5 = (bf16[512,128]{0,1:T(8,128)(2,1)}, bf16[512,128]{0,1:T(8,128)(2,1)}, u32[]{:S(2)}, u32[]{:S(2)}) collective-permute-start(bf16[512,128]{0,1:T(8,128)(2,1)} %pad_maximum_fusion.1), channel_id=1, source_target_pairs={{0,8},{1,9},{2,10},{3,11},{4,12},{5,13},{6,14},{7,15},{8,0},{9,1},... | collective-permute-start | bytes 393224 | tf_op jit(solution)/shard_map/ppermute | solution.py:27
  56.7 8.0 %collective-permute-start.6 = (bf16[1024,128]{0,1:T(8,128)(2,1)S(1)}, bf16[1024,128]{0,1:T(8,128)(2,1)S(1)}, u32[]{:S(2)}, u32[]{:S(2)}) collective-permute-start(bf16[1024,128]{0,1:T(8,128)(2,1)S(1)} %maximum_select_fusion.8), channel_id=1, source_target_pairs={{0,16},{1,17},{2,18},{3,19},{4,20},{5,21},{6,22},{7,23},{8,24},{9,... | collective-permute-start | bytes 786440 | tf_op jit(solution)/shard_map/ppermute | solution.py:27
  65.1 15.9 %slice-start = ((bf16[1536,4,128]{0,2,1:T(8,128)(2,1)}), bf16[1536,4,48]{0,2,1:T(8,128)(2,1)S(1)}, s32[]{:S(2)}) async-start(bf16[1536,4,128]{0,2,1:T(8,128)(2,1)} %copy-done.1), calls=%async_computation.1 | async-start | bytes 1179648 | tf_op jit(solution)/shard_map/slice | solution.py:194
  81.8 18.0 %collective-permute-start.7 = (bf16[256,1536]{1,0:T(8,128)(2,1)S(1)}, bf16[256,1536]{1,0:T(8,128)(2,1)S(1)}, u32[]{:S(2)}, u32[]{:S(2)}) collective-permute-start(bf16[256,1536]{1,0:T(8,128)(2,1)S(1)} %select_convert_fusion.2), channel_id=1, source_target_pairs={{0,4},{1,5},{2,6},{3,7},{4,0},{5,1},{6,2},{7,3},{8,12},{9,13},{10,... | collective-permute-start | bytes 2359304 | tf_op jit(solution)/shard_map/ppermute | solution.py:27
  100.2 8.2 %copy-start.9 = (s32[64,8]{0,1:T(8,128)S(1)}, s32[64,8]{0,1:T(8,128)}, u32[]{:S(2)}) copy-start(s32[64,8]{0,1:T(8,128)} %param.16) | copy-start | bytes 6148
  100.2 8.2 %copy-start.10 = (bf16[64,8]{0,1:T(8,128)(2,1)S(1)}, bf16[64,8]{0,1:T(8,128)(2,1)}, u32[]{:S(2)}) copy-start(bf16[64,8]{0,1:T(8,128)(2,1)} %param.17) | copy-start | bytes 3076
  100.3 9.6 %copy-start.3 = (bf16[64,1536]{1,0:T(8,128)(2,1)S(1)}, bf16[64,1536]{1,0:T(8,128)(2,1)}, u32[]{:S(2)}) copy-start(bf16[64,1536]{1,0:T(8,128)(2,1)} %param.14) | copy-start | bytes 589828
  100.3 7.9 %collective-permute-start.8 = (bf16[128,1536]{1,0:T(8,128)(2,1)S(1)}, bf16[128,1536]{1,0:T(8,128)(2,1)S(1)}, u32[]{:S(2)}, u32[]{:S(2)}) collective-permute-start(bf16[128,1536]{1,0:T(8,128)(2,1)S(1)} %select_convert_fusion.4), channel_id=1, source_target_pairs={{0,2},{1,3},{2,0},{3,1},{4,6},{5,7},{6,4},{7,5},{8,10},{9,11},{10,... | collective-permute-start | bytes 1179656 | tf_op jit(solution)/shard_map/ppermute | solution.py:27
  108.3 1.5 collective-permute-start.9
  110.1 176.9 %copy-start.2 = (bf16[64,1536]{1,0:T(8,128)(2,1)}, bf16[64,1536]{1,0:T(8,128)(2,1)S(1)}, u32[]{:S(2)}) copy-start(bf16[64,1536]{1,0:T(8,128)(2,1)S(1)} %get-tuple-element.319) | copy-start | bytes 589828
  110.2 62.0 %copy-start = (bf16[5,128,1536]{2,1,0:T(8,128)(2,1)S(1)}, bf16[5,128,1536]{2,1,0:T(8,128)(2,1)}, u32[]{:S(2)}) copy-start(bf16[5,128,1536]{2,1,0:T(8,128)(2,1)} %down_ref.1) | copy-start | bytes 5898244
  204.2 5.7 %collective-permute-start.10 = (bf16[1024,1536]{1,0:T(8,128)(2,1)S(1)}, bf16[1024,1536]{1,0:T(8,128)(2,1)S(1)}, u32[]{:S(2)}, u32[]{:S(2)}) collective-permute-start(bf16[1024,1536]{1,0:T(8,128)(2,1)S(1)} %bitcast.58), channel_id=1, source_target_pairs={{0,1},{1,0},{2,3},{3,2},{4,5},{5,4},{6,7},{7,6},{8,9},{9,8},{10,11... | collective-permute-start | bytes 9437192 | tf_op jit(solution)/shard_map/ppermute | solution.py:27
  211.3 36.6 %collective-permute-start.11 = (bf16[512,1536]{1,0:T(8,128)(2,1)S(1)}, bf16[512,1536]{1,0:T(8,128)(2,1)S(1)}, u32[]{:S(2)}, u32[]{:S(2)}) collective-permute-start(bf16[512,1536]{1,0:T(8,128)(2,1)S(1)} %select_convert_fusion), channel_id=1, source_target_pairs={{0,2},{1,3},{2,0},{3,1},{4,6},{5,7},{6,4},{7,5},{8,10},{9,11},{10,... | collective-permute-start | bytes 4718600 | tf_op jit(solution)/shard_map/ppermute | solution.py:27
  249.0 18.9 %collective-permute-start.12 = (bf16[256,1536]{1,0:T(8,128)(2,1)S(1)}, bf16[256,1536]{1,0:T(8,128)(2,1)S(1)}, u32[]{:S(2)}, u32[]{:S(2)}) collective-permute-start(bf16[256,1536]{1,0:T(8,128)(2,1)S(1)} %select_convert_fusion.1), channel_id=1, source_target_pairs={{0,8},{1,9},{2,10},{3,11},{4,12},{5,13},{6,14},{7,15},{8,0},{9,1},... | collective-permute-start | bytes 2359304 | tf_op jit(solution)/shard_map/ppermute | solution.py:27
  268.4 11.1 %collective-permute-start.13 = (bf16[128,1536]{1,0:T(8,128)(2,1)S(1)}, bf16[128,1536]{1,0:T(8,128)(2,1)S(1)}, u32[]{:S(2)}, u32[]{:S(2)}) collective-permute-start(bf16[128,1536]{1,0:T(8,128)(2,1)S(1)} %select_convert_fusion.3), channel_id=1, source_target_pairs={{0,16},{1,17},{2,18},{3,19},{4,20},{5,21},{6,22},{7,23},{8,24},{9,... | collective-permute-start | bytes 1179656 | tf_op jit(solution)/shard_map/ppermute | solution.py:27
  279.7 7.3 %collective-permute-start.14 = (bf16[64,1536]{1,0:T(8,128)(2,1)S(1)}, bf16[64,1536]{1,0:T(8,128)(2,1)S(1)}, u32[]{:S(2)}, u32[]{:S(2)}) collective-permute-start(bf16[64,1536]{1,0:T(8,128)(2,1)S(1)} %select_convert_fusion.5), channel_id=1, source_target_pairs={{0,4},{1,5},{2,6},{3,7},{4,0},{5,1},{6,2},{7,3},{8,12},{9,13},{10,... | collective-permute-start | bytes 589832 | tf_op jit(solution)/shard_map/ppermute | solution.py:27
  (4 other events, 11.7 us)
Sparse Core Ops, SparseCore 0:
  111.2 59.7 all-gather.1

commit v5 on v4

--- a/solution.py
+++ b/solution.py
@@ -83,6 +83,24 @@
         sent_rows = jnp.where(is_upper, lower_rows, upper_rows)
         partial_sum = kept_rows + sender(sent_rows, level_bit)
     return partial_sum
+
+
+def fold_any(partial_sum, layout_bits, level_bits):
+    index_now = lax.axis_index(TENSOR)
+    rows_left = partial_sum.shape[0] >> len(layout_bits)
+    state = partial_sum.reshape((2,) * len(layout_bits) + (rows_left,) + partial_sum.shape[1:])
+    dims = list(layout_bits)
+    for level_bit in level_bits:
+        place = dims.index(level_bit)
+        lower_rows = lax.index_in_dim(state, 0, place, keepdims=False)
+        upper_rows = lax.index_in_dim(state, 1, place, keepdims=False)
+        is_upper = index_now >> level_bit & 1 == 1
+        kept_rows = jnp.where(is_upper, upper_rows, lower_rows)
+        sent_rows = jnp.where(is_upper, lower_rows, upper_rows)
+        arrived = partner(sent_rows.astype(jnp.bfloat16), TENSOR, level_bit)
+        state = kept_rows.astype(jnp.float32) + arrived.astype(jnp.float32)
+        dims.pop(place)
+    return state.reshape((rows_left,) + partial_sum.shape[1:])
 
 
 def project_pairs(row_block, w_pairs, positions):
@@ -269,13 +287,7 @@
     partial_proj = lax.dot_general(
         attended, w_attn_out, (((1,), (1,)), ((), ())), preferred_element_type=jnp.float32
     )
-    projection = fold_levels(
-        partial_proj,
-        group_bits,
-        lambda sent_rows, level_bit: partner(
-            sent_rows.astype(jnp.bfloat16), TENSOR, level_bit
-        ).astype(sent_rows.dtype),
-    )
+    projection = fold_any(partial_proj, group_bits[::-1], group_bits)
     after_attention = (hidden.astype(jnp.float32) + residual_scale * projection).astype(
         jnp.bfloat16
     )
@@ -298,7 +310,16 @@
         1,
     ).astype(jnp.float32)
     expert_part = dense_experts(rows_all, local_shares, w_gate_up, w_down)
-    expert_sum = fold_bits(expert_part.reshape(-1, model_width), (0, 1, 3, 4, 2))
+    flat_part = expert_part.reshape(-1, model_width)
+    half_width = model_width // 2
+    layout = (0, 1, 3, 4, 2)
+    expert_sum = jnp.concatenate(
+        [
+            fold_any(flat_part[:, :half_width], layout, (0, 1, 3, 4, 2)),
+            fold_any(flat_part[:, half_width:], layout, (0, 3, 1, 2, 4)),
+        ],
+        axis=1,
+    )
     hidden_out = (after_attention.astype(jnp.float32) + residual_scale * expert_sum).astype(
         jnp.bfloat16
     )

time: 296 us -> 263 us (0.89)
  waiting for transfers between devices: 183 us -> 134 us
  starting transfers between devices: 20.4 us -> 26.3 us
  local copies, waits for them, and re-layouts: 11.6 us -> 16.2 us
  other arithmetic: 20 us -> 23.2 us
    ppermute x15 -> x20, waiting for transfers between devices: 123 us -> 77.6 us  [partner(): return lax.ppermute(value, axis, pairs)]
    ppermute x15 -> x20, starting transfers between devices: 20.4 us -> 26.3 us  [partner(): return lax.ppermute(value, axis, pairs)]
    all_gather x1, waiting for transfers between devices: 59.9 us -> 56.6 us  [on_device(): rows_all = lax.all_gather(carried, TENSOR, axis=0, tiled=True)]
  transfers between devices with their start and end apart: 16 -> 21, of which waited for: 14 -> 17; matrix products, arithmetic and copies ran while one was open for 4% -> 7% of each run, Pallas kernels for 0% -> 0%
where the time goes in v5:
time: 263 us; the launch traced here: 261 us
  waiting for transfers between devices  134 us (51%)
  Pallas kernels  28.9 us (11%)
  starting transfers between devices  26.3 us (10%)
  other arithmetic  23.2 us (9%)
  local copies, waits for them, and re-layouts  16.2 us (6%)
  between operations  15.3 us (6%)
  matrix products  11 us (4%)
  loops' own time  6.51 us (2%)
    ppermute x20, waiting for transfers between devices, partner(): return lax.ppermute(value, axis, pairs)  77.6 us
    all_gather x1, waiting for transfers between devices, on_device(): rows_all = lax.all_gather(carried, TENSOR, axis=0, tiled=True)  56.6 us
    pallas_call x1, Pallas kernels, dense_experts(): pl.pallas_call(expert_block, grid=(tiles,), in_specs=[pl.BlockSpec((tile,...  28.9 us
    ppermute x20, starting transfers between devices, partner(): return lax.ppermute(value, axis, pairs)  26.3 us
    another operation x1, loops' own time, on_device(): lax.map(attend, jnp.arange(rows_quarter // block_rows, dtype=jnp.int32))  5.95 us
  transfers between devices with their start and end apart: 21, of which 17 were waited for; matrix products, arithmetic and copies ran while one was open for 7% of the time, Pallas kernels for 0%

profile of v5, /device:TPU:24, one launch (start us, length us, event | category | flops | bytes accessed | tf_op | source)
XLA Modules:
  0.0 261.5 jit_solution(10968637429470838822)
XLA Ops:
  15.6 6.7 %collective-permute-done.3 = bf16[1536,128]{0,1:T(8,128)(2,1)S(1)} collective-permute-done((bf16[1536,128]{0,1:T(8,128)(2,1)S(1)}, bf16[1536,128]{0,1:T(8,128)(2,1)S(1)}, u32[]{:S(2)}, u32[]{:S(2)}) %collective-permute-start.3) | collective-permute-done | bytes 393248 | tf_op jit(solution)/shard_map/ppermute | solution.py:27
  25.8 3.0 %collective-permute-start.2 = (bf16[256,1536]{1,0:T(8,128)(2,1)}, bf16[256,1536]{1,0:T(8,128)(2,1)}, u32[]{:S(2)}, u32[]{:S(2)}) collective-permute-start(bf16[256,1536]{1,0:T(8,128)(2,1)} %maximum_select_fusion.2), channel_id=1, source_target_pairs={{0,4},{1,5},{2,6},{3,7},{4,0},{5,1},{6,2},{7,3},{8,12},{9,13},{10,... | collective-permute-start | bytes 2359304 | tf_op jit(solution)/shard_map/ppermute | solution.py:27
  30.0 13.1 %collective-permute-done.4 = bf16[1536,256]{0,1:T(8,128)(2,1)S(1)} collective-permute-done((bf16[1536,256]{0,1:T(8,128)(2,1)S(1)}, bf16[1536,256]{0,1:T(8,128)(2,1)S(1)}, u32[]{:S(2)}, u32[]{:S(2)}) %collective-permute-start.4) | collective-permute-done | bytes 786464 | tf_op jit(solution)/shard_map/ppermute | solution.py:27
  46.8 2.5 fusion.25
  50.9 2.5 fusion.12
  55.1 2.4 collective-permute-start.6
  57.9 5.1 %collective-permute-done.6 = bf16[1024,128]{0,1:T(8,128)(2,1)S(1)} collective-permute-done((bf16[1024,128]{0,1:T(8,128)(2,1)S(1)}, bf16[1024,128]{0,1:T(8,128)(2,1)S(1)}, u32[]{:S(2)}, u32[]{:S(2)}) %collective-permute-start.6) | collective-permute-done | bytes 262176 | tf_op jit(solution)/shard_map/ppermute | solution.py:27
  63.5 20.6 %while.59 = (s32[]{:T(128)}, bf16[2,256,192]{1,2,0:T(8,128)(2,1)S(1)}, s32[2]{0:T(128)S(1)}, s32[]{:T(128)}, s32[2048]{0:T(1024)S(1)}, /*index=5*/bf16[3,512,64]...) while((s32[]{:T(128)}, ...), condition=%wide.region_8.9_spmd, body=%wide.region_3.8_spmd.sunk | while | flops 104007976 | bytes 8754148 | solution.py:284
  67.6 6.1 %while.60 = (s32[]{:T(128)}, f32[768]{0:T(1024)S(1)}, f32[768]{0:T(1024)S(1)}, f32[768,64]{0,1:T(8,128)S(1)}, s32[]{:T(128)}, /*index=5*/s32[256]{0:T(256)S(1)},...) while((s32[]{:T(128)}, f32[768]{0:T(1024)S(1)}, ...), condition=%wide.region_7.7_spmd.clone, body=%wide.region_4.6_spmd.clone.sunk | while | flops 103909632 | bytes 7464147 | solution.py:280
  77.9 6.1 %while.60 = (s32[]{:T(128)}, f32[768]{0:T(1024)S(1)}, f32[768]{0:T(1024)S(1)}, f32[768,64]{0,1:T(8,128)S(1)}, s32[]{:T(128)}, /*index=5*/s32[256]{0:T(256)S(1)},...) while((s32[]{:T(128)}, f32[768]{0:T(1024)S(1)}, ...), condition=%wide.region_7.7_spmd.clone, body=%wide.region_4.6_spmd.clone.sunk | while | flops 103909632 | bytes 7464147 | solution.py:280
  85.3 2.3 collective-permute-done.7
  89.6 9.7 %collective-permute-done.8 = bf16[2,64,1536]{2,1,0:T(8,128)(2,1)S(1)} collective-permute-done((bf16[2,64,1536]{2,1,0:T(8,128)(2,1)S(1)}, bf16[2,64,1536]{2,1,0:T(8,128)(2,1)S(1)}, u32[]{:S(2)}, u32[]{:S(2)}) %collective-permute-start.8) | collective-permute-done | bytes 393248 | tf_op jit(solution)/shard_map/ppermute | solution.py:27
  99.5 3.1 %collective-permute-start.9 = (bf16[64,1536]{1,0:T(8,128)(2,1)S(1)}, bf16[64,1536]{1,0:T(8,128)(2,1)S(1)}, u32[]{:S(2)}, u32[]{:S(2)}) collective-permute-start(bf16[64,1536]{1,0:T(8,128)(2,1)S(1)} %fusion.30), channel_id=1, source_target_pairs={{0,4},{1,5},{2,6},{3,7},{4,0},{5,1},{6,2},{7,3},{8,12},{9,13},{10,... | collective-permute-start | bytes 589832 | tf_op jit(solution)/shard_map/ppermute | solution.py:27
  102.8 4.4 %collective-permute-done.9 = bf16[64,1536]{1,0:T(8,128)(2,1)S(1)} collective-permute-done((bf16[64,1536]{1,0:T(8,128)(2,1)S(1)}, bf16[64,1536]{1,0:T(8,128)(2,1)S(1)}, u32[]{:S(2)}, u32[]{:S(2)}) %collective-permute-start.9) | collective-permute-done | bytes 196640 | tf_op jit(solution)/shard_map/ppermute | solution.py:27
  108.4 56.6 %all-gather.2.cloned.1.call-done.rows_ref = bf16[2048,1664]{1,0:T(8,128)(2,1)} async-done(((bf16[64,1664]{1,0:T(8,128)(2,1)}), bf16[2048,1664]{1,0:T(8,128)(2,1)}) %all-gather.2.cloned.1.call-update) | async-done | bytes 6815760 | tf_op jit(solution)/shard_map/all_gather | solution.py:305
  166.3 28.9 %shard_map.121 = bf16[2,2,8,64,1536]{4,3,2,1,0:T(8,128)(2,1)} custom-call(bf16[2048,1664]{1,0:T(8,128)(2,1)} %all-gather.2.cloned.1.call-done.rows_ref, f32[2048,5]{1,0:T(8,128)S(1)} %dynamic-slice_convert_fusion.share_ref, bf16[5,1536,256]{2,1,0:T(8,128)(2,1)} %gate_up_ref.1, bf16[5,128,1536]{2,1,0:T(8,128)(2,1)S(1)} %copy-done), custom_call_target="tpu_custom_call" | custom-call | tf_op jit(solution)/shard_map/pallas_call | solution.py:143
  195.1 3.0 %broadcast_select_fusion.2 = (bf16[1024,768]{1,0:T(8,128)(2,1)S(1)}, bf16[1024,768]{1,0:T(8,128)(2,1)S(1)}, bf16[1024,768]{1,0:T(8,128)(2,1)S(1)}, bf16[1024,768]{1,0:T(8,128)(2,1)S(1)}) fusion(pred[]{:T(512)S(6)} %eq.20, bf16[2048,1536]{1,0:T(8,128)(2,1)} %bitcast.107), kind=kLoop, calls=%fused_computation.30 | loop fusion | flops 3145728 | bytes 12582913 | tf_op jit(solution)/shard_map/jit(_where)/select_n | solution.py:99
  198.9 2.9 %collective-permute-done.15 = bf16[2,2,2,2,64,768]{5,4,2,3,0,1:T(8,128)(2,1)S(1)} collective-permute-done((bf16[2,2,2,2,64,768]{5,4,2,3,0,1:T(8,128)(2,1)S(1)}, bf16[2,2,2,2,64,768]{5,4,2,3,0,1:T(8,128)(2,1)S(1)}, u32[]{:S(2)}, u32[]{:S(2)}) %collective-permute-start.15) | collective-permute-done | bytes 1572896 | tf_op jit(solution)/shard_map/ppermute | solution.py:27
  209.1 14.2 %collective-permute-done.16 = bf16[2,2,2,64,768]{4,3,1,2,0:T(8,128)(2,1)} collective-permute-done((bf16[2,2,2,64,768]{4,3,1,2,0:T(8,128)(2,1)}, bf16[2,2,2,64,768]{4,3,1,2,0:T(8,128)(2,1)}, u32[]{:S(2)}, u32[]{:S(2)}) %collective-permute-start.16) | collective-permute-done | bytes 786464 | tf_op jit(solution)/shard_map/ppermute | solution.py:27
  225.2 1.9 collective-permute-done.11
  229.9 5.5 %collective-permute-done.17 = bf16[2,2,64,768]{3,2,0,1:T(8,128)(2,1)S(1)} collective-permute-done((bf16[2,2,64,768]{3,2,0,1:T(8,128)(2,1)S(1)}, bf16[2,2,64,768]{3,2,0,1:T(8,128)(2,1)S(1)}, u32[]{:S(2)}, u32[]{:S(2)}) %collective-permute-start.17) | collective-permute-done | bytes 393248 | tf_op jit(solution)/shard_map/ppermute | solution.py:27
  242.9 2.1 collective-permute-start.19
  245.0 2.5 collective-permute-done.13
  249.6 4.2 %collective-permute-done.14 = bf16[64,768]{1,0:T(8,128)(2,1)S(1)} collective-permute-done((bf16[64,768]{1,0:T(8,128)(2,1)S(1)}, bf16[64,768]{1,0:T(8,128)(2,1)S(1)}, u32[]{:S(2)}, u32[]{:S(2)}) %collective-permute-start.14) | collective-permute-done | bytes 98336 | tf_op jit(solution)/shard_map/ppermute | solution.py:27
  (219 shorter events, 63.0 us)
Async XLA Ops:
  7.2 157.8 %all-gather.2.cloned.1.call-start = ((), (), s32[]{:S(2)}) async-start(), calls=%async_computation | async-start | bytes 7028736 | tf_op jit(solution)/shard_map/all_gather | solution.py:305
  9.5 3.8 %collective-permute-start = (bf16[64,1536]{1,0:T(8,128)(2,1)S(1)}, bf16[64,1536]{1,0:T(8,128)(2,1)S(1)}, u32[]{:S(2)}, u32[]{:S(2)}) collective-permute-start(bf16[64,1536]{1,0:T(8,128)(2,1)S(1)} %fusion.16), channel_id=1, source_target_pairs={{0,1},{1,0},{2,3},{3,2},{4,5},{5,4},{6,7},{7,6},{8,9},{9,8},{10,11... | collective-permute-start | bytes 589832 | tf_op jit(solution)/shard_map/ppermute | solution.py:27
  10.7 11.6 %collective-permute-start.3 = (bf16[1536,128]{0,1:T(8,128)(2,1)S(1)}, bf16[1536,128]{0,1:T(8,128)(2,1)S(1)}, u32[]{:S(2)}, u32[]{:S(2)}) collective-permute-start(bf16[1536,128]{0,1:T(8,128)(2,1)S(1)} %pad_maximum_fusion), channel_id=1, source_target_pairs={{0,8},{1,9},{2,10},{3,11},{4,12},{5,13},{6,14},{7,15},{8,0},{9,1},... | collective-permute-start | bytes 1179656 | tf_op jit(solution)/shard_map/ppermute | solution.py:27
  13.4 11.3 %collective-permute-start.1 = (bf16[128,1536]{1,0:T(8,128)(2,1)S(1)}, bf16[128,1536]{1,0:T(8,128)(2,1)S(1)}, u32[]{:S(2)}, u32[]{:S(2)}) collective-permute-start(bf16[128,1536]{1,0:T(8,128)(2,1)S(1)} %maximum_select_fusion.5), channel_id=1, source_target_pairs={{0,2},{1,3},{2,0},{3,1},{4,6},{5,7},{6,4},{7,5},{8,10},{9,11},{10,... | collective-permute-start | bytes 1179656 | tf_op jit(solution)/shard_map/ppermute | solution.py:27
  22.4 20.7 %collective-permute-start.4 = (bf16[1536,256]{0,1:T(8,128)(2,1)S(1)}, bf16[1536,256]{0,1:T(8,128)(2,1)S(1)}, u32[]{:S(2)}, u32[]{:S(2)}) collective-permute-start(bf16[1536,256]{0,1:T(8,128)(2,1)S(1)} %maximum_select_fusion.3), channel_id=1, source_target_pairs={{0,16},{1,17},{2,18},{3,19},{4,20},{5,21},{6,22},{7,23},{8,24},{9,... | collective-permute-start | bytes 2359304 | tf_op jit(solution)/shard_map/ppermute | solution.py:27
  25.8 21.0 %collective-permute-start.2 = (bf16[256,1536]{1,0:T(8,128)(2,1)}, bf16[256,1536]{1,0:T(8,128)(2,1)}, u32[]{:S(2)}, u32[]{:S(2)}) collective-permute-start(bf16[256,1536]{1,0:T(8,128)(2,1)} %maximum_select_fusion.2), channel_id=1, source_target_pairs={{0,4},{1,5},{2,6},{3,7},{4,0},{5,1},{6,2},{7,3},{8,12},{9,13},{10,... | collective-permute-start | bytes 2359304 | tf_op jit(solution)/shard_map/ppermute | solution.py:27
  50.0 5.0 %collective-permute-start.5 = (bf16[512,128]{0,1:T(8,128)(2,1)S(1)}, bf16[512,128]{0,1:T(8,128)(2,1)S(1)}, u32[]{:S(2)}, u32[]{:S(2)}) collective-permute-start(bf16[512,128]{0,1:T(8,128)(2,1)S(1)} %pad_maximum_fusion.1), channel_id=1, source_target_pairs={{0,8},{1,9},{2,10},{3,11},{4,12},{5,13},{6,14},{7,15},{8,0},{9,1},... | collective-permute-start | bytes 393224 | tf_op jit(solution)/shard_map/ppermute | solution.py:27
  55.1 8.0 %collective-permute-start.6 = (bf16[1024,128]{0,1:T(8,128)(2,1)S(1)}, bf16[1024,128]{0,1:T(8,128)(2,1)S(1)}, u32[]{:S(2)}, u32[]{:S(2)}) collective-permute-start(bf16[1024,128]{0,1:T(8,128)(2,1)S(1)} %maximum_select_fusion.8), channel_id=1, source_target_pairs={{0,16},{1,17},{2,18},{3,19},{4,20},{5,21},{6,22},{7,23},{8,24},{9,... | collective-permute-start | bytes 786440 | tf_op jit(solution)/shard_map/ppermute | solution.py:27
  63.5 20.8 %slice-start = ((bf16[1536,4,128]{0,2,1:T(8,128)(2,1)}), bf16[1536,4,48]{0,2,1:T(8,128)(2,1)S(1)}, s32[]{:S(2)}) async-start(bf16[1536,4,128]{0,2,1:T(8,128)(2,1)} %copy-done.3), calls=%async_computation.1 | async-start | bytes 1179648 | tf_op jit(solution)/shard_map/slice | solution.py:212
  85.0 2.6 collective-permute-start.7
  88.0 11.2 %collective-permute-start.8 = (bf16[2,64,1536]{2,1,0:T(8,128)(2,1)S(1)}, bf16[2,64,1536]{2,1,0:T(8,128)(2,1)S(1)}, u32[]{:S(2)}, u32[]{:S(2)}) collective-permute-start(bf16[2,64,1536]{2,1,0:T(8,128)(2,1)S(1)} %fusion.22), channel_id=1, source_target_pairs={{0,2},{1,3},{2,0},{3,1},{4,6},{5,7},{6,4},{7,5},{8,10},{9,11},{10,... | collective-permute-start | bytes 1179656 | tf_op jit(solution)/shard_map/ppermute | solution.py:27
  99.5 7.7 %collective-permute-start.9 = (bf16[64,1536]{1,0:T(8,128)(2,1)S(1)}, bf16[64,1536]{1,0:T(8,128)(2,1)S(1)}, u32[]{:S(2)}, u32[]{:S(2)}) collective-permute-start(bf16[64,1536]{1,0:T(8,128)(2,1)S(1)} %fusion.30), channel_id=1, source_target_pairs={{0,4},{1,5},{2,6},{3,7},{4,0},{5,1},{6,2},{7,3},{8,12},{9,13},{10,... | collective-permute-start | bytes 589832 | tf_op jit(solution)/shard_map/ppermute | solution.py:27
  107.4 146.5 %copy-start.5 = (bf16[64,1536]{1,0:T(8,128)(2,1)}, bf16[64,1536]{1,0:T(8,128)(2,1)S(1)}, u32[]{:S(2)}) copy-start(bf16[64,1536]{1,0:T(8,128)(2,1)S(1)} %get-tuple-element.319) | copy-start | bytes 589828
  107.5 58.7 %copy-start = (bf16[5,128,1536]{2,1,0:T(8,128)(2,1)S(1)}, bf16[5,128,1536]{2,1,0:T(8,128)(2,1)}, u32[]{:S(2)}) copy-start(bf16[5,128,1536]{2,1,0:T(8,128)(2,1)} %down_ref.1) | copy-start | bytes 5898244
  198.3 3.5 %collective-permute-start.15 = (bf16[2,2,2,2,64,768]{5,4,2,3,0,1:T(8,128)(2,1)S(1)}, bf16[2,2,2,2,64,768]{5,4,2,3,0,1:T(8,128)(2,1)S(1)}, u32[]{:S(2)}, u32[]{:S(2)}) collective-permute-start(bf16[2,2,2,2,64,768]{5,4,2,3,0,1:T(8,128)(2,1)S(1)} %copy.57), channel_id=1, source_target_pairs={{0,1},{1,0},{2,3},{3,2},{4,5},{5,4},{6,7},{7,6},{8,9},{9,8},{10,11... | collective-permute-start | bytes 4718600 | tf_op jit(solution)/shard_map/ppermute | solution.py:27
  198.6 5.5 %collective-permute-start.10 = (bf16[2,2,2,2,64,768]{5,4,3,2,1,0:T(8,128)(2,1)S(1)}, bf16[2,2,2,2,64,768]{5,4,3,2,1,0:T(8,128)(2,1)S(1)}, u32[]{:S(2)}, u32[]{:S(2)}) collective-permute-start(bf16[2,2,2,2,64,768]{5,4,3,2,1,0:T(8,128)(2,1)S(1)} %bitcast.115), channel_id=1, source_target_pairs={{0,1},{1,0},{2,3},{3,2},{4,5},{5,4},{6,7},{7,6},{8,9},{9,8},{10,11... | collective-permute-start | bytes 4718600 | tf_op jit(solution)/shard_map/ppermute | solution.py:27
  203.2 20.0 %collective-permute-start.16 = (bf16[2,2,2,64,768]{4,3,1,2,0:T(8,128)(2,1)}, bf16[2,2,2,64,768]{4,3,1,2,0:T(8,128)(2,1)}, u32[]{:S(2)}, u32[]{:S(2)}) collective-permute-start(bf16[2,2,2,64,768]{4,3,1,2,0:T(8,128)(2,1)} %fusion.11), channel_id=1, source_target_pairs={{0,8},{1,9},{2,10},{3,11},{4,12},{5,13},{6,14},{7,15},{8,0},{9,1},... | collective-permute-start | bytes 2359304 | tf_op jit(solution)/shard_map/ppermute | solution.py:27
  207.2 20.0 %collective-permute-start.11 = (bf16[2,2,2,64,768]{4,3,2,1,0:T(8,128)(2,1)}, bf16[2,2,2,64,768]{4,3,2,1,0:T(8,128)(2,1)}, u32[]{:S(2)}, u32[]{:S(2)}) collective-permute-start(bf16[2,2,2,64,768]{4,3,2,1,0:T(8,128)(2,1)} %fusion.10), channel_id=1, source_target_pairs={{0,2},{1,3},{2,0},{3,1},{4,6},{5,7},{6,4},{7,5},{8,10},{9,11},{10,... | collective-permute-start | bytes 2359304 | tf_op jit(solution)/shard_map/ppermute | solution.py:27
  224.9 10.6 %collective-permute-start.17 = (bf16[2,2,64,768]{3,2,0,1:T(8,128)(2,1)S(1)}, bf16[2,2,64,768]{3,2,0,1:T(8,128)(2,1)S(1)}, u32[]{:S(2)}, u32[]{:S(2)}) collective-permute-start(bf16[2,2,64,768]{3,2,0,1:T(8,128)(2,1)S(1)} %fusion.24), channel_id=1, source_target_pairs={{0,2},{1,3},{2,0},{3,1},{4,6},{5,7},{6,4},{7,5},{8,10},{9,11},{10,... | collective-permute-start | bytes 1179656 | tf_op jit(solution)/shard_map/ppermute | solution.py:27
  228.7 10.4 %collective-permute-start.12 = (bf16[2,2,64,768]{3,2,1,0:T(8,128)(2,1)S(1)}, bf16[2,2,64,768]{3,2,1,0:T(8,128)(2,1)S(1)}, u32[]{:S(2)}, u32[]{:S(2)}) collective-permute-start(bf16[2,2,64,768]{3,2,1,0:T(8,128)(2,1)S(1)} %fusion.23), channel_id=1, source_target_pairs={{0,8},{1,9},{2,10},{3,11},{4,12},{5,13},{6,14},{7,15},{8,0},{9,1},... | collective-permute-start | bytes 1179656 | tf_op jit(solution)/shard_map/ppermute | solution.py:27
  235.6 7.3 %collective-permute-start.18 = (bf16[2,64,768]{2,1,0:T(8,128)(2,1)S(1)}, bf16[2,64,768]{2,1,0:T(8,128)(2,1)S(1)}, u32[]{:S(2)}, u32[]{:S(2)}) collective-permute-start(bf16[2,64,768]{2,1,0:T(8,128)(2,1)S(1)} %fusion.32), channel_id=1, source_target_pairs={{0,4},{1,5},{2,6},{3,7},{4,0},{5,1},{6,2},{7,3},{8,12},{9,13},{10,... | collective-permute-start | bytes 589832 | tf_op jit(solution)/shard_map/ppermute | solution.py:27
  239.3 8.3 %collective-permute-start.13 = (bf16[2,64,768]{2,1,0:T(8,128)(2,1)S(1)}, bf16[2,64,768]{2,1,0:T(8,128)(2,1)S(1)}, u32[]{:S(2)}, u32[]{:S(2)}) collective-permute-start(bf16[2,64,768]{2,1,0:T(8,128)(2,1)S(1)} %fusion.31), channel_id=1, source_target_pairs={{0,16},{1,17},{2,18},{3,19},{4,20},{5,21},{6,22},{7,23},{8,24},{9,... | collective-permute-start | bytes 589832 | tf_op jit(solution)/shard_map/ppermute | solution.py:27
  242.9 6.7 %collective-permute-start.19 = (bf16[64,768]{1,0:T(8,128)(2,1)S(1)}, bf16[64,768]{1,0:T(8,128)(2,1)S(1)}, u32[]{:S(2)}, u32[]{:S(2)}) collective-permute-start(bf16[64,768]{1,0:T(8,128)(2,1)S(1)} %fusion.35), channel_id=1, source_target_pairs={{0,16},{1,17},{2,18},{3,19},{4,20},{5,21},{6,22},{7,23},{8,24},{9,... | collective-permute-start | bytes 294920 | tf_op jit(solution)/shard_map/ppermute | solution.py:27
  247.7 6.2 %collective-permute-start.14 = (bf16[64,768]{1,0:T(8,128)(2,1)S(1)}, bf16[64,768]{1,0:T(8,128)(2,1)S(1)}, u32[]{:S(2)}, u32[]{:S(2)}) collective-permute-start(bf16[64,768]{1,0:T(8,128)(2,1)S(1)} %fusion.34), channel_id=1, source_target_pairs={{0,4},{1,5},{2,6},{3,7},{4,0},{5,1},{6,2},{7,3},{8,12},{9,13},{10,... | collective-permute-start | bytes 294920 | tf_op jit(solution)/shard_map/ppermute | solution.py:27
  (13 other events, 108.4 us)
Sparse Core Ops, SparseCore 0:
  108.5 56.4 all-gather.1

commit v6 on v5

--- a/solution.py
+++ b/solution.py
@@ -103,6 +103,18 @@
     return state.reshape((rows_left,) + partial_sum.shape[1:])
 
 
+def gather_any(part, level_bits):
+    index_now = lax.axis_index(TENSOR)
+    state = part
+    for level_bit in level_bits:
+        arrived = partner(state, TENSOR, level_bit)
+        is_upper = index_now >> level_bit & 1 == 1
+        lower_rows = jnp.where(is_upper, arrived, state)
+        upper_rows = jnp.where(is_upper, state, arrived)
+        state = jnp.stack([lower_rows, upper_rows], axis=0)
+    return state
+
+
 def project_pairs(row_block, w_pairs, positions):
     head_size = w_pairs.shape[1] // 2
     paired = jnp.dot(row_block, w_pairs, preferred_element_type=jnp.float32)
@@ -110,11 +122,11 @@
     return jnp.concatenate([rotated, paired[:, head_size:]], axis=1).astype(jnp.bfloat16)
 
 
-def expert_block(rows_ref, share_ref, gate_up_ref, down_ref, out_ref):
-    model_width = gate_up_ref.shape[1]
-    rows = rows_ref[:, :model_width]
+def expert_block(first_ref, second_ref, share_ref, gate_up_ref, down_ref, out_ref):
+    half_width = second_ref.shape[1]
+    rows = jnp.concatenate([first_ref[:, :half_width], second_ref[...]], axis=1)
     inner_width = down_ref.shape[1]
-    total = jnp.zeros((rows.shape[0], model_width), jnp.float32)
+    total = jnp.zeros(out_ref.shape, jnp.float32)
     for expert in range(gate_up_ref.shape[0]):
         both = jnp.dot(rows, gate_up_ref[expert], preferred_element_type=jnp.float32)
         gate_val = both[:, :inner_width]
@@ -122,39 +134,29 @@
         inner_act = (jax.nn.silu(gate_val) * up_val).astype(jnp.bfloat16)
         produced = jnp.dot(inner_act, down_ref[expert], preferred_element_type=jnp.float32)
         total = total + share_ref[:, expert : expert + 1] * produced
-    piece = out_ref.shape[3]
-    for part in range(4):
-        out_ref[part % 2, part // 2, 0] = total[part * piece : (part + 1) * piece].astype(
-            out_ref.dtype
-        )
-
-
-def tile_slot(tile_number):
-    return (tile_number // 2) % 2 * 4 + (tile_number // 4) % 2 * 2 + tile_number % 2
-
-
-def dense_experts(rows_all, shares, gate_up, down_proj):
-    row_count, carried_width = rows_all.shape
+    out_ref[...] = total.astype(out_ref.dtype)
+
+
+def dense_experts(first_rows, second_rows, shares, gate_up, down_proj):
+    row_count, first_width = first_rows.shape
+    second_width = second_rows.shape[1]
     model_width = gate_up.shape[1]
     expert_count = gate_up.shape[0]
-    piece = row_count // 32
-    tile = 4 * piece
-    tiles = row_count // tile
+    tile = 256
     return pl.pallas_call(
         expert_block,
-        grid=(tiles,),
+        grid=(row_count // tile,),
         in_specs=[
-            pl.BlockSpec((tile, carried_width), lambda i: (i, 0)),
+            pl.BlockSpec((tile, first_width), lambda i: (i, 0)),
+            pl.BlockSpec((tile, second_width), lambda i: (i, 0)),
             pl.BlockSpec((tile, expert_count), lambda i: (i, 0)),
             pl.BlockSpec(gate_up.shape, lambda i: (0, 0, 0)),
             pl.BlockSpec(down_proj.shape, lambda i: (0, 0, 0)),
         ],
-        out_specs=pl.BlockSpec(
-            (2, 2, 1, piece, model_width), lambda i: (0, 0, tile_slot(i), 0, 0)
-        ),
-        out_shape=jax.ShapeDtypeStruct((2, 2, tiles, piece, model_width), jnp.bfloat16),
+        out_specs=pl.BlockSpec((tile, model_width), lambda i: (i, 0)),
+        out_shape=jax.ShapeDtypeStruct((row_count, model_width), jnp.bfloat16),
         compiler_params=pltpu.CompilerParams(vmem_limit_bytes=48 * 1024 * 1024),
-    )(rows_all, shares, gate_up, down_proj)
+    )(first_rows, second_rows, shares, gate_up, down_proj)
 
 
 def fold_bits(partial_sum, level_bits):
@@ -294,25 +296,34 @@
     expert_in = rms_norm(after_attention, ffn_gain)
     local_experts = w_gate_up.shape[0]
     share_cols = 128 * pl.cdiv(expert_total, 128)
+    half_width = model_width // 2
     carried = jnp.concatenate(
         [
-            expert_in,
+            expert_in[:, :half_width],
             share_table,
             jnp.zeros((share_table.shape[0], share_cols - expert_total), jnp.bfloat16),
         ],
         axis=1,
     )
-    rows_all = lax.all_gather(carried, TENSOR, axis=0, tiled=True)
+    layout = (0, 1, 3, 4, 2)
+    first_order = (2, 4, 3, 1, 0)
+    second_order = (4, 2, 1, 3, 0)
+    first_rows = gather_any(carried, first_order)
+    second_rows = gather_any(expert_in[:, half_width:], second_order)
+    second_dims = list(second_order[::-1])
+    second_rows = second_rows.transpose(
+        [second_dims.index(bit) for bit in layout] + [len(layout), len(layout) + 1]
+    )
+    first_rows = first_rows.reshape(-1, first_rows.shape[-1])
+    second_rows = second_rows.reshape(-1, second_rows.shape[-1])
     local_shares = lax.dynamic_slice_in_dim(
-        rows_all[:, model_width : model_width + expert_total],
+        first_rows[:, half_width : half_width + expert_total],
         group_index * local_experts,
         local_experts,
         1,
     ).astype(jnp.float32)
-    expert_part = dense_experts(rows_all, local_shares, w_gate_up, w_down)
-    flat_part = expert_part.reshape(-1, model_width)
-    half_width = model_width // 2
-    layout = (0, 1, 3, 4, 2)
+    expert_part = dense_experts(first_rows, second_rows, local_shares, w_gate_up, w_down)
+    flat_part = expert_part
     expert_sum = jnp.concatenate(
         [
             fold_any(flat_part[:, :half_width], layout, (0, 1, 3, 4, 2)),

time: 263 us -> 252 us (0.958)
  waiting for transfers between devices: 134 us -> 114 us
  starting transfers between devices: 26.3 us -> 43.8 us
  between operations: 15.3 us -> 1.99 us
  other arithmetic: 23.2 us -> 30.1 us
    all_gather x1 -> x0, waiting for transfers between devices: 56.6 us -> none  [on_device(): rows_all = lax.all_gather(carried, TENSOR, axis=0, tiled=True)]
    ppermute x20 -> x30, waiting for transfers between devices: 77.6 us -> 114 us  [partner(): return lax.ppermute(value, axis, pairs)]
    ppermute x20 -> x30, starting transfers between devices: 26.3 us -> 43.8 us  [partner(): return lax.ppermute(value, axis, pairs)]
    another operation x3 -> x22, other arithmetic: 0.53 us -> 8.13 us  [the longest x19 7.6 us: gather_any(): state = jnp.stack([lower_rows, upper_rows], axis=0)]
    unnamed x33 -> x37, local copies, waits for them, and re-layouts: 5.24 us -> 8.56 us
  transfers between devices with their start and end apart: 21 -> 30, of which waited for: 17 -> 25; matrix products, arithmetic and copies ran while one was open for 7% -> 10% of each run, Pallas kernels for 0% -> 0%
where the time goes in v6:
time: 252 us; the launch traced here: 250 us
  waiting for transfers between devices  114 us (45%)
  starting transfers between devices  43.8 us (17%)
  other arithmetic  30.1 us (12%)
  Pallas kernels  28.3 us (11%)
  local copies, waits for them, and re-layouts  17 us (7%)
  matrix products  9.19 us (4%)
  loops' own time  6.43 us (3%)
    ppermute x30, waiting for transfers between devices, partner(): return lax.ppermute(value, axis, pairs)  114 us
    ppermute x30, starting transfers between devices, partner(): return lax.ppermute(value, axis, pairs)  43.8 us
    pallas_call x1, Pallas kernels, dense_experts(): pl.pallas_call(expert_block, grid=(row_count // tile,), in_specs=[pl.Bloc...  28.3 us
    unnamed x37, local copies, waits for them, and re-layouts  8.56 us
    another operation x19, other arithmetic, gather_any(): state = jnp.stack([lower_rows, upper_rows], axis=0)  7.6 us
    another operation x1, loops' own time, on_device(): lax.map(attend, jnp.arange(rows_quarter // block_rows, dtype=jnp.int32))  6.05 us
  transfers between devices with their start and end apart: 30, of which 25 were waited for; matrix products, arithmetic and copies ran while one was open for 10% of the time, Pallas kernels for 0%

profile of v6, /device:TPU:24, one launch (start us, length us, event | category | flops | bytes accessed | tf_op | source)
XLA Modules:
  0.0 250.3 jit_solution(14399771618018828907)
XLA Ops:
  8.9 6.7 %collective-permute-done.3 = bf16[1536,128]{0,1:T(8,128)(2,1)S(1)} collective-permute-done((bf16[1536,128]{0,1:T(8,128)(2,1)S(1)}, bf16[1536,128]{0,1:T(8,128)(2,1)S(1)}, u32[]{:S(2)}, u32[]{:S(2)}) %collective-permute-start.3) | collective-permute-done | bytes 393248 | tf_op jit(solution)/shard_map/ppermute | solution.py:27
  19.2 3.0 %collective-permute-start.2 = (bf16[256,1536]{1,0:T(8,128)(2,1)}, bf16[256,1536]{1,0:T(8,128)(2,1)}, u32[]{:S(2)}, u32[]{:S(2)}) collective-permute-start(bf16[256,1536]{1,0:T(8,128)(2,1)} %maximum_select_fusion.2), channel_id=1, source_target_pairs={{0,4},{1,5},{2,6},{3,7},{4,0},{5,1},{6,2},{7,3},{8,12},{9,13},{10,... | collective-permute-start | bytes 2359304 | tf_op jit(solution)/shard_map/ppermute | solution.py:27
  23.3 13.1 %collective-permute-done.4 = bf16[1536,256]{0,1:T(8,128)(2,1)S(1)} collective-permute-done((bf16[1536,256]{0,1:T(8,128)(2,1)S(1)}, bf16[1536,256]{0,1:T(8,128)(2,1)S(1)}, u32[]{:S(2)}, u32[]{:S(2)}) %collective-permute-start.4) | collective-permute-done | bytes 786464 | tf_op jit(solution)/shard_map/ppermute | solution.py:27
  51.3 5.2 %collective-permute-done.6 = bf16[1024,128]{0,1:T(8,128)(2,1)S(1)} collective-permute-done((bf16[1024,128]{0,1:T(8,128)(2,1)S(1)}, bf16[1024,128]{0,1:T(8,128)(2,1)S(1)}, u32[]{:S(2)}, u32[]{:S(2)}) %collective-permute-start.6) | collective-permute-done | bytes 262176 | tf_op jit(solution)/shard_map/ppermute | solution.py:27
  56.9 16.8 %while.59 = (s32[]{:T(128)}, bf16[2,256,192]{1,2,0:T(8,128)(2,1)S(1)}, s32[2]{0:T(128)S(1)}, s32[]{:T(128)}, s32[2048]{0:T(1024)S(1)}, /*index=5*/bf16[3,512,64]...) while((s32[]{:T(128)}, ...), condition=%wide.region_8.9_spmd, body=%wide.region_3.8_spmd.sunk | while | flops 104007976 | bytes 8754148 | solution.py:286
  61.1 4.0 %while.60 = (s32[]{:T(128)}, f32[768]{0:T(1024)S(1)}, f32[768]{0:T(1024)S(1)}, f32[768,64]{0,1:T(8,128)S(1)}, s32[]{:T(128)}, /*index=5*/s32[256]{0:T(256)S(1)},...) while((s32[]{:T(128)}, f32[768]{0:T(1024)S(1)}, ...), condition=%wide.region_7.7_spmd.clone, body=%wide.region_4.6_spmd.clone.sunk | while | flops 103909632 | bytes 7464147 | solution.py:282
  69.5 4.0 %while.60 = (s32[]{:T(128)}, f32[768]{0:T(1024)S(1)}, f32[768]{0:T(1024)S(1)}, f32[768,64]{0,1:T(8,128)S(1)}, s32[]{:T(128)}, /*index=5*/s32[256]{0:T(256)S(1)},...) while((s32[]{:T(128)}, f32[768]{0:T(1024)S(1)}, ...), condition=%wide.region_7.7_spmd.clone, body=%wide.region_4.6_spmd.clone.sunk | while | flops 103909632 | bytes 7464147 | solution.py:282
  79.1 9.7 %collective-permute-done.8 = bf16[2,64,1536]{2,1,0:T(8,128)(2,1)S(1)} collective-permute-done((bf16[2,64,1536]{2,1,0:T(8,128)(2,1)S(1)}, bf16[2,64,1536]{2,1,0:T(8,128)(2,1)S(1)}, u32[]{:S(2)}, u32[]{:S(2)}) %collective-permute-start.8) | collective-permute-done | bytes 393248 | tf_op jit(solution)/shard_map/ppermute | solution.py:27
  89.0 3.1 %collective-permute-start.9 = (bf16[64,1536]{1,0:T(8,128)(2,1)S(1)}, bf16[64,1536]{1,0:T(8,128)(2,1)S(1)}, u32[]{:S(2)}, u32[]{:S(2)}) collective-permute-start(bf16[64,1536]{1,0:T(8,128)(2,1)S(1)} %fusion.32), channel_id=1, source_target_pairs={{0,4},{1,5},{2,6},{3,7},{4,0},{5,1},{6,2},{7,3},{8,12},{9,13},{10,... | collective-permute-start | bytes 589832 | tf_op jit(solution)/shard_map/ppermute | solution.py:27
  92.1 4.6 %collective-permute-done.9 = bf16[64,1536]{1,0:T(8,128)(2,1)S(1)} collective-permute-done((bf16[64,1536]{1,0:T(8,128)(2,1)S(1)}, bf16[64,1536]{1,0:T(8,128)(2,1)S(1)}, u32[]{:S(2)}, u32[]{:S(2)}) %collective-permute-start.9) | collective-permute-done | bytes 196640 | tf_op jit(solution)/shard_map/ppermute | solution.py:27
  100.3 3.6 %collective-permute-done.15 = bf16[64,768]{1,0:T(8,128)(2,1)S(1)} collective-permute-done((bf16[64,768]{1,0:T(8,128)(2,1)S(1)}, bf16[64,768]{1,0:T(8,128)(2,1)S(1)}, u32[]{:S(2)}, u32[]{:S(2)}) %collective-permute-start.15) | collective-permute-done | bytes 98336 | tf_op jit(solution)/shard_map/ppermute | solution.py:27
  104.0 3.1 %collective-permute-start.10 = (bf16[64,896]{1,0:T(8,128)(2,1)S(1)}, bf16[64,896]{1,0:T(8,128)(2,1)S(1)}, u32[]{:S(2)}, u32[]{:S(2)}) collective-permute-start(bf16[64,896]{1,0:T(8,128)(2,1)S(1)} %maximum_maximum_fusion), channel_id=1, source_target_pairs={{0,4},{1,5},{2,6},{3,7},{4,0},{5,1},{6,2},{7,3},{8,12},{9,13},{10,... | collective-permute-start | bytes 344072 | tf_op jit(solution)/shard_map/ppermute | solution.py:27
  107.7 3.9 %collective-permute-done.10 = bf16[64,896]{1,0:T(8,128)(2,1)S(1)} collective-permute-done((bf16[64,896]{1,0:T(8,128)(2,1)S(1)}, bf16[64,896]{1,0:T(8,128)(2,1)S(1)}, u32[]{:S(2)}, u32[]{:S(2)}) %collective-permute-start.10) | collective-permute-done | bytes 114720 | tf_op jit(solution)/shard_map/ppermute | solution.py:27
  116.3 3.0 %collective-permute-done.11 = bf16[2,64,896]{2,1,0:T(8,128)(2,1)S(1)} collective-permute-done((bf16[2,64,896]{2,1,0:T(8,128)(2,1)S(1)}, bf16[2,64,896]{2,1,0:T(8,128)(2,1)S(1)}, u32[]{:S(2)}, u32[]{:S(2)}) %collective-permute-start.11) | collective-permute-done | bytes 229408 | tf_op jit(solution)/shard_map/ppermute | solution.py:27
  119.4 7.5 %collective-permute-start.12 = (bf16[2,2,64,896]{3,2,1,0:T(8,128)(2,1)S(1)}, bf16[2,2,64,896]{3,2,1,0:T(8,128)(2,1)S(1)}, u32[]{:S(2)}, u32[]{:S(2)}) collective-permute-start(bf16[2,2,64,896]{3,2,1,0:T(8,128)(2,1)S(1)} %pad_maximum_fusion.5), channel_id=1, source_target_pairs={{0,8},{1,9},{2,10},{3,11},{4,12},{5,13},{6,14},{7,15},{8,0},{9,1},... | collective-permute-start | bytes 1376264 | tf_op jit(solution)/shard_map/ppermute | solution.py:27
  128.3 10.0 %collective-permute-done.12 = bf16[2,2,64,896]{3,2,1,0:T(8,128)(2,1)S(1)} collective-permute-done((bf16[2,2,64,896]{3,2,1,0:T(8,128)(2,1)S(1)}, bf16[2,2,64,896]{3,2,1,0:T(8,128)(2,1)S(1)}, u32[]{:S(2)}, u32[]{:S(2)}) %collective-permute-start.12) | collective-permute-done | bytes 458784 | tf_op jit(solution)/shard_map/ppermute | solution.py:27
  139.2 8.2 %collective-permute-done.18 = bf16[2,2,2,64,768]{4,3,2,1,0:T(8,128)(2,1)S(1)} collective-permute-done((bf16[2,2,2,64,768]{4,3,2,1,0:T(8,128)(2,1)S(1)}, bf16[2,2,2,64,768]{4,3,2,1,0:T(8,128)(2,1)S(1)}, u32[]{:S(2)}, u32[]{:S(2)}) %collective-permute-start.18) | collective-permute-done | bytes 786464 | tf_op jit(solution)/shard_map/ppermute | solution.py:27
  148.8 3.1 %collective-permute-done.13 = bf16[2,2,2,64,896]{4,3,2,1,0:T(8,128)(2,1)S(1)} collective-permute-done((bf16[2,2,2,64,896]{4,3,2,1,0:T(8,128)(2,1)S(1)}, bf16[2,2,2,64,896]{4,3,2,1,0:T(8,128)(2,1)S(1)}, u32[]{:S(2)}, u32[]{:S(2)}) %collective-permute-start.13) | collective-permute-done | bytes 917536 | tf_op jit(solution)/shard_map/ppermute | solution.py:27
  162.9 28.3 %shard_map.121 = bf16[2048,1536]{1,0:T(8,128)(2,1)} custom-call(bf16[2048,896]{1,0:T(8,128)(2,1)} %bitcast.187, bf16[2048,768]{1,0:T(8,128)(2,1)S(1)} %bitcast.183, f32[2048,5]{1,0:T(8,128)S(1)} %dynamic-slice_convert_fusion.share_ref, bf16[5,1536,256]{2,1,0:T(8,128)(2,1)} %gate_up_ref.1, bf16[5,128,1536]{2,1,0:T(8,128)(2,1)S(1)} %copy-done), custom_call_target="tpu_custom_call" | custom-call | tf_op jit(solution)/shard_map/pallas_call | solution.py:146
  191.3 3.0 %broadcast_select_fusion.2 = (bf16[1024,768]{1,0:T(8,128)(2,1)S(1)}, bf16[1024,768]{1,0:T(8,128)(2,1)S(1)}, bf16[1024,768]{1,0:T(8,128)(2,1)S(1)}, bf16[1024,768]{1,0:T(8,128)(2,1)S(1)}) fusion(pred[]{:T(512)S(6)} %eq.20, bf16[2048,1536]{1,0:T(8,128)(2,1)} %shard_map.121), kind=kLoop, calls=%fused_computation.40 | loop fusion | flops 3145728 | bytes 12582913 | tf_op jit(solution)/shard_map/jit(_where)/select_n | solution.py:99
  206.7 12.5 %collective-permute-done.26 = bf16[2,2,2,64,768]{4,3,1,2,0:T(8,128)(2,1)} collective-permute-done((bf16[2,2,2,64,768]{4,3,1,2,0:T(8,128)(2,1)}, bf16[2,2,2,64,768]{4,3,1,2,0:T(8,128)(2,1)}, u32[]{:S(2)}, u32[]{:S(2)}) %collective-permute-start.26) | collective-permute-done | bytes 786464 | tf_op jit(solution)/shard_map/ppermute | solution.py:27
  226.6 5.4 %collective-permute-done.27 = bf16[2,2,64,768]{3,2,0,1:T(8,128)(2,1)S(1)} collective-permute-done((bf16[2,2,64,768]{3,2,0,1:T(8,128)(2,1)S(1)}, bf16[2,2,64,768]{3,2,0,1:T(8,128)(2,1)S(1)}, u32[]{:S(2)}, u32[]{:S(2)}) %collective-permute-start.27) | collective-permute-done | bytes 393248 | tf_op jit(solution)/shard_map/ppermute | solution.py:27
  236.1 3.6 %collective-permute-done.28 = bf16[2,64,768]{2,1,0:T(8,128)(2,1)S(1)} collective-permute-done((bf16[2,64,768]{2,1,0:T(8,128)(2,1)S(1)}, bf16[2,64,768]{2,1,0:T(8,128)(2,1)S(1)}, u32[]{:S(2)}, u32[]{:S(2)}) %collective-permute-start.28) | collective-permute-done | bytes 196640 | tf_op jit(solution)/shard_map/ppermute | solution.py:27
  246.1 3.5 %collective-permute-done.24 = bf16[64,768]{1,0:T(8,128)(2,1)S(1)} collective-permute-done((bf16[64,768]{1,0:T(8,128)(2,1)S(1)}, bf16[64,768]{1,0:T(8,128)(2,1)S(1)}, u32[]{:S(2)}, u32[]{:S(2)}) %collective-permute-start.24) | collective-permute-done | bytes 98336 | tf_op jit(solution)/shard_map/ppermute | solution.py:27
  (241 shorter events, 97.9 us)
Async XLA Ops:
  4.0 11.6 %collective-permute-start.3 = (bf16[1536,128]{0,1:T(8,128)(2,1)S(1)}, bf16[1536,128]{0,1:T(8,128)(2,1)S(1)}, u32[]{:S(2)}, u32[]{:S(2)}) collective-permute-start(bf16[1536,128]{0,1:T(8,128)(2,1)S(1)} %pad_maximum_fusion.6), channel_id=1, source_target_pairs={{0,8},{1,9},{2,10},{3,11},{4,12},{5,13},{6,14},{7,15},{8,0},{9,1},... | collective-permute-start | bytes 1179656 | tf_op jit(solution)/shard_map/ppermute | solution.py:27
  6.8 11.3 %collective-permute-start.1 = (bf16[128,1536]{1,0:T(8,128)(2,1)S(1)}, bf16[128,1536]{1,0:T(8,128)(2,1)S(1)}, u32[]{:S(2)}, u32[]{:S(2)}) collective-permute-start(bf16[128,1536]{1,0:T(8,128)(2,1)S(1)} %maximum_select_fusion.5), channel_id=1, source_target_pairs={{0,2},{1,3},{2,0},{3,1},{4,6},{5,7},{6,4},{7,5},{8,10},{9,11},{10,... | collective-permute-start | bytes 1179656 | tf_op jit(solution)/shard_map/ppermute | solution.py:27
  15.8 20.7 %collective-permute-start.4 = (bf16[1536,256]{0,1:T(8,128)(2,1)S(1)}, bf16[1536,256]{0,1:T(8,128)(2,1)S(1)}, u32[]{:S(2)}, u32[]{:S(2)}) collective-permute-start(bf16[1536,256]{0,1:T(8,128)(2,1)S(1)} %maximum_select_fusion.3), channel_id=1, source_target_pairs={{0,16},{1,17},{2,18},{3,19},{4,20},{5,21},{6,22},{7,23},{8,24},{9,... | collective-permute-start | bytes 2359304 | tf_op jit(solution)/shard_map/ppermute | solution.py:27
  19.2 21.0 %collective-permute-start.2 = (bf16[256,1536]{1,0:T(8,128)(2,1)}, bf16[256,1536]{1,0:T(8,128)(2,1)}, u32[]{:S(2)}, u32[]{:S(2)}) collective-permute-start(bf16[256,1536]{1,0:T(8,128)(2,1)} %maximum_select_fusion.2), channel_id=1, source_target_pairs={{0,4},{1,5},{2,6},{3,7},{4,0},{5,1},{6,2},{7,3},{8,12},{9,13},{10,... | collective-permute-start | bytes 2359304 | tf_op jit(solution)/shard_map/ppermute | solution.py:27
  48.5 8.0 %collective-permute-start.6 = (bf16[1024,128]{0,1:T(8,128)(2,1)S(1)}, bf16[1024,128]{0,1:T(8,128)(2,1)S(1)}, u32[]{:S(2)}, u32[]{:S(2)}) collective-permute-start(bf16[1024,128]{0,1:T(8,128)(2,1)S(1)} %maximum_select_fusion.8), channel_id=1, source_target_pairs={{0,16},{1,17},{2,18},{3,19},{4,20},{5,21},{6,22},{7,23},{8,24},{9,... | collective-permute-start | bytes 786440 | tf_op jit(solution)/shard_map/ppermute | solution.py:27
  77.5 11.2 %collective-permute-start.8 = (bf16[2,64,1536]{2,1,0:T(8,128)(2,1)S(1)}, bf16[2,64,1536]{2,1,0:T(8,128)(2,1)S(1)}, u32[]{:S(2)}, u32[]{:S(2)}) collective-permute-start(bf16[2,64,1536]{2,1,0:T(8,128)(2,1)S(1)} %fusion.26), channel_id=1, source_target_pairs={{0,2},{1,3},{2,0},{3,1},{4,6},{5,7},{6,4},{7,5},{8,10},{9,11},{10,... | collective-permute-start | bytes 1179656 | tf_op jit(solution)/shard_map/ppermute | solution.py:27
  89.0 7.7 %collective-permute-start.9 = (bf16[64,1536]{1,0:T(8,128)(2,1)S(1)}, bf16[64,1536]{1,0:T(8,128)(2,1)S(1)}, u32[]{:S(2)}, u32[]{:S(2)}) collective-permute-start(bf16[64,1536]{1,0:T(8,128)(2,1)S(1)} %fusion.32), channel_id=1, source_target_pairs={{0,4},{1,5},{2,6},{3,7},{4,0},{5,1},{6,2},{7,3},{8,12},{9,13},{10,... | collective-permute-start | bytes 589832 | tf_op jit(solution)/shard_map/ppermute | solution.py:27
  97.7 6.2 %collective-permute-start.15 = (bf16[64,768]{1,0:T(8,128)(2,1)S(1)}, bf16[64,768]{1,0:T(8,128)(2,1)S(1)}, u32[]{:S(2)}, u32[]{:S(2)}) collective-permute-start(bf16[64,768]{1,0:T(8,128)(2,1)S(1)} %slice.220), channel_id=1, source_target_pairs={{0,16},{1,17},{2,18},{3,19},{4,20},{5,21},{6,22},{7,23},{8,24},{9,... | collective-permute-start | bytes 294920 | tf_op jit(solution)/shard_map/ppermute | solution.py:27
  104.0 7.6 %collective-permute-start.10 = (bf16[64,896]{1,0:T(8,128)(2,1)S(1)}, bf16[64,896]{1,0:T(8,128)(2,1)S(1)}, u32[]{:S(2)}, u32[]{:S(2)}) collective-permute-start(bf16[64,896]{1,0:T(8,128)(2,1)S(1)} %maximum_maximum_fusion), channel_id=1, source_target_pairs={{0,4},{1,5},{2,6},{3,7},{4,0},{5,1},{6,2},{7,3},{8,12},{9,13},{10,... | collective-permute-start | bytes 344072 | tf_op jit(solution)/shard_map/ppermute | solution.py:27
  107.1 8.1 %collective-permute-start.16 = (bf16[2,64,768]{2,1,0:T(8,128)(2,1)S(1)}, bf16[2,64,768]{2,1,0:T(8,128)(2,1)S(1)}, u32[]{:S(2)}, u32[]{:S(2)}) collective-permute-start(bf16[2,64,768]{2,1,0:T(8,128)(2,1)S(1)} %pad_maximum_fusion.9), channel_id=1, source_target_pairs={{0,4},{1,5},{2,6},{3,7},{4,0},{5,1},{6,2},{7,3},{8,12},{9,13},{10,... | collective-permute-start | bytes 589832 | tf_op jit(solution)/shard_map/ppermute | solution.py:27
  111.7 7.6 %collective-permute-start.11 = (bf16[2,64,896]{2,1,0:T(8,128)(2,1)S(1)}, bf16[2,64,896]{2,1,0:T(8,128)(2,1)S(1)}, u32[]{:S(2)}, u32[]{:S(2)}) collective-permute-start(bf16[2,64,896]{2,1,0:T(8,128)(2,1)S(1)} %pad_maximum_fusion.8), channel_id=1, source_target_pairs={{0,16},{1,17},{2,18},{3,19},{4,20},{5,21},{6,22},{7,23},{8,24},{9,... | collective-permute-start | bytes 688136 | tf_op jit(solution)/shard_map/ppermute | solution.py:27
  115.3 11.6 %collective-permute-start.17 = (bf16[2,2,64,768]{3,2,1,0:T(8,128)(2,1)S(1)}, bf16[2,2,64,768]{3,2,1,0:T(8,128)(2,1)S(1)}, u32[]{:S(2)}, u32[]{:S(2)}) collective-permute-start(bf16[2,2,64,768]{3,2,1,0:T(8,128)(2,1)S(1)} %pad_maximum_fusion.7), channel_id=1, source_target_pairs={{0,2},{1,3},{2,0},{3,1},{4,6},{5,7},{6,4},{7,5},{8,10},{9,11},{10,... | collective-permute-start | bytes 1179656 | tf_op jit(solution)/shard_map/ppermute | solution.py:27
  119.4 18.8 %collective-permute-start.12 = (bf16[2,2,64,896]{3,2,1,0:T(8,128)(2,1)S(1)}, bf16[2,2,64,896]{3,2,1,0:T(8,128)(2,1)S(1)}, u32[]{:S(2)}, u32[]{:S(2)}) collective-permute-start(bf16[2,2,64,896]{3,2,1,0:T(8,128)(2,1)S(1)} %pad_maximum_fusion.5), channel_id=1, source_target_pairs={{0,8},{1,9},{2,10},{3,11},{4,12},{5,13},{6,14},{7,15},{8,0},{9,1},... | collective-permute-start | bytes 1376264 | tf_op jit(solution)/shard_map/ppermute | solution.py:27
  127.0 20.4 %collective-permute-start.18 = (bf16[2,2,2,64,768]{4,3,2,1,0:T(8,128)(2,1)S(1)}, bf16[2,2,2,64,768]{4,3,2,1,0:T(8,128)(2,1)S(1)}, u32[]{:S(2)}, u32[]{:S(2)}) collective-permute-start(bf16[2,2,2,64,768]{4,3,2,1,0:T(8,128)(2,1)S(1)} %pad_maximum_fusion.4), channel_id=1, source_target_pairs={{0,8},{1,9},{2,10},{3,11},{4,12},{5,13},{6,14},{7,15},{8,0},{9,1},... | collective-permute-start | bytes 2359304 | tf_op jit(solution)/shard_map/ppermute | solution.py:27
  138.5 13.5 %collective-permute-start.13 = (bf16[2,2,2,64,896]{4,3,2,1,0:T(8,128)(2,1)S(1)}, bf16[2,2,2,64,896]{4,3,2,1,0:T(8,128)(2,1)S(1)}, u32[]{:S(2)}, u32[]{:S(2)}) collective-permute-start(bf16[2,2,2,64,896]{4,3,2,1,0:T(8,128)(2,1)S(1)} %pad_maximum_fusion.3), channel_id=1, source_target_pairs={{0,2},{1,3},{2,0},{3,1},{4,6},{5,7},{6,4},{7,5},{8,10},{9,11},{10,... | collective-permute-start | bytes 2752520 | tf_op jit(solution)/shard_map/ppermute | solution.py:27
  194.6 6.4 %collective-permute-start.20 = (bf16[2,2,2,2,64,768]{5,4,3,2,1,0:T(8,128)(2,1)S(1)}, bf16[2,2,2,2,64,768]{5,4,3,2,1,0:T(8,128)(2,1)S(1)}, u32[]{:S(2)}, u32[]{:S(2)}) collective-permute-start(bf16[2,2,2,2,64,768]{5,4,3,2,1,0:T(8,128)(2,1)S(1)} %bitcast.195), channel_id=1, source_target_pairs={{0,1},{1,0},{2,3},{3,2},{4,5},{5,4},{6,7},{7,6},{8,9},{9,8},{10,11... | collective-permute-start | bytes 4718600 | tf_op jit(solution)/shard_map/ppermute | solution.py:27
  199.3 19.9 %collective-permute-start.26 = (bf16[2,2,2,64,768]{4,3,1,2,0:T(8,128)(2,1)}, bf16[2,2,2,64,768]{4,3,1,2,0:T(8,128)(2,1)}, u32[]{:S(2)}, u32[]{:S(2)}) collective-permute-start(bf16[2,2,2,64,768]{4,3,1,2,0:T(8,128)(2,1)} %fusion.13), channel_id=1, source_target_pairs={{0,8},{1,9},{2,10},{3,11},{4,12},{5,13},{6,14},{7,15},{8,0},{9,1},... | collective-permute-start | bytes 2359304 | tf_op jit(solution)/shard_map/ppermute | solution.py:27
  204.1 20.4 %collective-permute-start.21 = (bf16[2,2,2,64,768]{4,3,2,1,0:T(8,128)(2,1)}, bf16[2,2,2,64,768]{4,3,2,1,0:T(8,128)(2,1)}, u32[]{:S(2)}, u32[]{:S(2)}) collective-permute-start(bf16[2,2,2,64,768]{4,3,2,1,0:T(8,128)(2,1)} %fusion.12), channel_id=1, source_target_pairs={{0,2},{1,3},{2,0},{3,1},{4,6},{5,7},{6,4},{7,5},{8,10},{9,11},{10,... | collective-permute-start | bytes 2359304 | tf_op jit(solution)/shard_map/ppermute | solution.py:27
  220.9 11.1 %collective-permute-start.27 = (bf16[2,2,64,768]{3,2,0,1:T(8,128)(2,1)S(1)}, bf16[2,2,64,768]{3,2,0,1:T(8,128)(2,1)S(1)}, u32[]{:S(2)}, u32[]{:S(2)}) collective-permute-start(bf16[2,2,64,768]{3,2,0,1:T(8,128)(2,1)S(1)} %fusion.28), channel_id=1, source_target_pairs={{0,2},{1,3},{2,0},{3,1},{4,6},{5,7},{6,4},{7,5},{8,10},{9,11},{10,... | collective-permute-start | bytes 1179656 | tf_op jit(solution)/shard_map/ppermute | solution.py:27
  226.0 9.4 %collective-permute-start.22 = (bf16[2,2,64,768]{3,2,1,0:T(8,128)(2,1)S(1)}, bf16[2,2,64,768]{3,2,1,0:T(8,128)(2,1)S(1)}, u32[]{:S(2)}, u32[]{:S(2)}) collective-permute-start(bf16[2,2,64,768]{3,2,1,0:T(8,128)(2,1)S(1)} %fusion.27), channel_id=1, source_target_pairs={{0,8},{1,9},{2,10},{3,11},{4,12},{5,13},{6,14},{7,15},{8,0},{9,1},... | collective-permute-start | bytes 1179656 | tf_op jit(solution)/shard_map/ppermute | solution.py:27
  232.2 7.6 %collective-permute-start.28 = (bf16[2,64,768]{2,1,0:T(8,128)(2,1)S(1)}, bf16[2,64,768]{2,1,0:T(8,128)(2,1)S(1)}, u32[]{:S(2)}, u32[]{:S(2)}) collective-permute-start(bf16[2,64,768]{2,1,0:T(8,128)(2,1)S(1)} %fusion.34), channel_id=1, source_target_pairs={{0,4},{1,5},{2,6},{3,7},{4,0},{5,1},{6,2},{7,3},{8,12},{9,13},{10,... | collective-permute-start | bytes 589832 | tf_op jit(solution)/shard_map/ppermute | solution.py:27
  235.5 7.7 %collective-permute-start.23 = (bf16[2,64,768]{2,1,0:T(8,128)(2,1)S(1)}, bf16[2,64,768]{2,1,0:T(8,128)(2,1)S(1)}, u32[]{:S(2)}, u32[]{:S(2)}) collective-permute-start(bf16[2,64,768]{2,1,0:T(8,128)(2,1)S(1)} %fusion.33), channel_id=1, source_target_pairs={{0,16},{1,17},{2,18},{3,19},{4,20},{5,21},{6,22},{7,23},{8,24},{9,... | collective-permute-start | bytes 589832 | tf_op jit(solution)/shard_map/ppermute | solution.py:27
  239.8 6.2 %collective-permute-start.29 = (bf16[64,768]{1,0:T(8,128)(2,1)S(1)}, bf16[64,768]{1,0:T(8,128)(2,1)S(1)}, u32[]{:S(2)}, u32[]{:S(2)}) collective-permute-start(bf16[64,768]{1,0:T(8,128)(2,1)S(1)} %fusion.37), channel_id=1, source_target_pairs={{0,16},{1,17},{2,18},{3,19},{4,20},{5,21},{6,22},{7,23},{8,24},{9,... | collective-permute-start | bytes 294920 | tf_op jit(solution)/shard_map/ppermute | solution.py:27
  243.3 6.2 %collective-permute-start.24 = (bf16[64,768]{1,0:T(8,128)(2,1)S(1)}, bf16[64,768]{1,0:T(8,128)(2,1)S(1)}, u32[]{:S(2)}, u32[]{:S(2)}) collective-permute-start(bf16[64,768]{1,0:T(8,128)(2,1)S(1)} %fusion.36), channel_id=1, source_target_pairs={{0,4},{1,5},{2,6},{3,7},{4,0},{5,1},{6,2},{7,3},{8,12},{9,13},{10,... | collective-permute-start | bytes 294920 | tf_op jit(solution)/shard_map/ppermute | solution.py:27
  (24 other events, 159.1 us)

commit v7 on v6

--- a/solution.py
+++ b/solution.py
@@ -216,9 +216,14 @@
     w_pairs = w_group[:, GQ * HD :]
     (own_rows,) = gather_levels(
         (normed,),
-        group_bits,
+        group_bits[::-1],
         (0,),
         lambda payload, level_bit: (partner(payload[0], TENSOR, level_bit),),
+    )
+    own_rows = (
+        own_rows.reshape((2,) * len(group_bits) + normed.shape)
+        .transpose(list(range(len(group_bits)))[::-1] + [len(group_bits), len(group_bits) + 1])
+        .reshape(rows_quarter, model_width)
     )
     kv_block = project_pairs(own_rows, w_pairs, own_positions)
     (key_values,) = gather_levels(

time: 252 us -> 252 us (level)
  waiting for transfers between devices: 114 us -> 135 us
  starting transfers between devices: 43.8 us -> 24.7 us
    ppermute x30, waiting for transfers between devices: 114 us -> 135 us  [partner(): return lax.ppermute(value, axis, pairs)]
    ppermute x30, starting transfers between devices: 43.8 us -> 24.7 us  [partner(): return lax.ppermute(value, axis, pairs)]
    unnamed x37 -> x29, local copies, waits for them, and re-layouts: 8.56 us -> 6.82 us
  transfers between devices with their start and end apart: 30 -> 30, of which waited for: 25 -> 26; matrix products, arithmetic and copies ran while one was open for 10% -> 8% of each run, Pallas kernels for 0% -> 0%
where the time goes in v7:
time: 252 us; the launch traced here: 251 us
  waiting for transfers between devices  135 us (54%)
  other arithmetic  29 us (12%)
  Pallas kernels  28.4 us (11%)
  starting transfers between devices  24.7 us (10%)
  local copies, waits for them, and re-layouts  17 us (7%)
  loops' own time  7.56 us (3%)
  matrix products  7.17 us (3%)
    ppermute x30, waiting for transfers between devices, partner(): return lax.ppermute(value, axis, pairs)  135 us
    pallas_call x1, Pallas kernels, dense_experts(): pl.pallas_call(expert_block, grid=(row_count // tile,), in_specs=[pl.Bloc...  28.4 us
    ppermute x30, starting transfers between devices, partner(): return lax.ppermute(value, axis, pairs)  24.7 us
    another operation x19, other arithmetic, gather_any(): state = jnp.stack([lower_rows, upper_rows], axis=0)  7.56 us
    another operation x1, loops' own time, on_device(): lax.map(attend, jnp.arange(rows_quarter // block_rows, dtype=jnp.int32))  7 us
    unnamed x29, local copies, waits for them, and re-layouts  6.82 us
  transfers between devices with their start and end apart: 30, of which 26 were waited for; matrix products, arithmetic and copies ran while one was open for 8% of the time, Pallas kernels for 0%

profile of v7, /device:TPU:24, one launch (start us, length us, event | category | flops | bytes accessed | tf_op | source)
XLA Modules:
  0.0 251.1 jit_solution(4151343545446756865)
XLA Ops:
  2.8 3.1 %collective-permute-start = (bf16[64,1536]{1,0:T(8,128)(2,1)S(1)}, bf16[64,1536]{1,0:T(8,128)(2,1)S(1)}, u32[]{:S(2)}, u32[]{:S(2)}) collective-permute-start(bf16[64,1536]{1,0:T(8,128)(2,1)S(1)} %fusion.18), channel_id=1, source_target_pairs={{0,4},{1,5},{2,6},{3,7},{4,0},{5,1},{6,2},{7,3},{8,12},{9,13},{10,... | collective-permute-start | bytes 589832 | tf_op jit(solution)/shard_map/ppermute | solution.py:27
  13.3 4.4 %collective-permute-done.3 = bf16[1536,128]{0,1:T(8,128)(2,1)S(1)} collective-permute-done((bf16[1536,128]{0,1:T(8,128)(2,1)S(1)}, bf16[1536,128]{0,1:T(8,128)(2,1)S(1)}, u32[]{:S(2)}, u32[]{:S(2)}) %collective-permute-start.3) | collective-permute-done | bytes 393248 | tf_op jit(solution)/shard_map/ppermute | solution.py:27
  22.0 15.6 %collective-permute-done.4 = bf16[1536,256]{0,1:T(8,128)(2,1)S(1)} collective-permute-done((bf16[1536,256]{0,1:T(8,128)(2,1)S(1)}, bf16[1536,256]{0,1:T(8,128)(2,1)S(1)}, u32[]{:S(2)}, u32[]{:S(2)}) %collective-permute-start.4) | collective-permute-done | bytes 786464 | tf_op jit(solution)/shard_map/ppermute | solution.py:27
  42.4 5.0 %collective-permute-done.5 = bf16[512,128]{0,1:T(8,128)(2,1)S(1)} collective-permute-done((bf16[512,128]{0,1:T(8,128)(2,1)S(1)}, bf16[512,128]{0,1:T(8,128)(2,1)S(1)}, u32[]{:S(2)}, u32[]{:S(2)}) %collective-permute-start.5) | collective-permute-done | bytes 131104 | tf_op jit(solution)/shard_map/ppermute | solution.py:27
  47.6 7.8 %collective-permute-done.6 = bf16[1024,128]{0,1:T(8,128)(2,1)S(1)} collective-permute-done((bf16[1024,128]{0,1:T(8,128)(2,1)S(1)}, bf16[1024,128]{0,1:T(8,128)(2,1)S(1)}, u32[]{:S(2)}, u32[]{:S(2)}) %collective-permute-start.6) | collective-permute-done | bytes 262176 | tf_op jit(solution)/shard_map/ppermute | solution.py:27
  55.8 22.2 %while.59 = (s32[]{:T(128)}, bf16[2,256,192]{1,2,0:T(8,128)(2,1)S(1)}, s32[2]{0:T(128)S(1)}, s32[]{:T(128)}, s32[2048]{0:T(1024)S(1)}, /*index=5*/bf16[3,512,64]...) while((s32[]{:T(128)}, ...), condition=%wide.region_8.9_spmd, body=%wide.region_3.8_spmd.sunk | while | flops 104007976 | bytes 8950756 | solution.py:291
  60.7 6.1 %while.60 = (s32[]{:T(128)}, f32[768]{0:T(1024)S(1)}, f32[768]{0:T(1024)S(1)}, f32[768,64]{0,1:T(8,128)S(1)}, s32[]{:T(128)}, /*index=5*/s32[256]{0:T(256)S(1)},...) while((s32[]{:T(128)}, f32[768]{0:T(1024)S(1)}, ...), condition=%wide.region_7.7_spmd.clone, body=%wide.region_4.6_spmd.clone.sunk | while | flops 103909632 | bytes 7464147 | solution.py:287
  71.8 6.1 %while.60 = (s32[]{:T(128)}, f32[768]{0:T(1024)S(1)}, f32[768]{0:T(1024)S(1)}, f32[768,64]{0,1:T(8,128)S(1)}, s32[]{:T(128)}, /*index=5*/s32[256]{0:T(256)S(1)},...) while((s32[]{:T(128)}, f32[768]{0:T(1024)S(1)}, ...), condition=%wide.region_7.7_spmd.clone, body=%wide.region_4.6_spmd.clone.sunk | while | flops 103909632 | bytes 7464147 | solution.py:287
  82.6 10.6 %collective-permute-done.8 = bf16[2,64,1536]{2,1,0:T(8,128)(2,1)S(1)} collective-permute-done((bf16[2,64,1536]{2,1,0:T(8,128)(2,1)S(1)}, bf16[2,64,1536]{2,1,0:T(8,128)(2,1)S(1)}, u32[]{:S(2)}, u32[]{:S(2)}) %collective-permute-start.8) | collective-permute-done | bytes 393248 | tf_op jit(solution)/shard_map/ppermute | solution.py:27
  94.3 6.7 %collective-permute-done.9 = bf16[64,1536]{1,0:T(8,128)(2,1)S(1)} collective-permute-done((bf16[64,1536]{1,0:T(8,128)(2,1)S(1)}, bf16[64,1536]{1,0:T(8,128)(2,1)S(1)}, u32[]{:S(2)}, u32[]{:S(2)}) %collective-permute-start.9) | collective-permute-done | bytes 196640 | tf_op jit(solution)/shard_map/ppermute | solution.py:27
  102.5 5.8 %collective-permute-done.15 = bf16[64,768]{1,0:T(8,128)(2,1)S(1)} collective-permute-done((bf16[64,768]{1,0:T(8,128)(2,1)S(1)}, bf16[64,768]{1,0:T(8,128)(2,1)S(1)}, u32[]{:S(2)}, u32[]{:S(2)}) %collective-permute-start.15) | collective-permute-done | bytes 98336 | tf_op jit(solution)/shard_map/ppermute | solution.py:27
  112.1 2.7 %collective-permute-done.10 = bf16[64,896]{1,0:T(8,128)(2,1)S(1)} collective-permute-done((bf16[64,896]{1,0:T(8,128)(2,1)S(1)}, bf16[64,896]{1,0:T(8,128)(2,1)S(1)}, u32[]{:S(2)}, u32[]{:S(2)}) %collective-permute-start.10) | collective-permute-done | bytes 114720 | tf_op jit(solution)/shard_map/ppermute | solution.py:27
  117.9 7.0 %collective-permute-done.11 = bf16[2,64,896]{2,1,0:T(8,128)(2,1)S(1)} collective-permute-done((bf16[2,64,896]{2,1,0:T(8,128)(2,1)S(1)}, bf16[2,64,896]{2,1,0:T(8,128)(2,1)S(1)}, u32[]{:S(2)}, u32[]{:S(2)}) %collective-permute-start.11) | collective-permute-done | bytes 229408 | tf_op jit(solution)/shard_map/ppermute | solution.py:27
  127.4 11.1 %collective-permute-done.12 = bf16[2,2,64,896]{3,2,1,0:T(8,128)(2,1)S(1)} collective-permute-done((bf16[2,2,64,896]{3,2,1,0:T(8,128)(2,1)S(1)}, bf16[2,2,64,896]{3,2,1,0:T(8,128)(2,1)S(1)}, u32[]{:S(2)}, u32[]{:S(2)}) %collective-permute-start.12) | collective-permute-done | bytes 458784 | tf_op jit(solution)/shard_map/ppermute | solution.py:27
  139.4 7.5 %collective-permute-done.18 = bf16[2,2,2,64,768]{4,3,2,1,0:T(8,128)(2,1)S(1)} collective-permute-done((bf16[2,2,2,64,768]{4,3,2,1,0:T(8,128)(2,1)S(1)}, bf16[2,2,2,64,768]{4,3,2,1,0:T(8,128)(2,1)S(1)}, u32[]{:S(2)}, u32[]{:S(2)}) %collective-permute-start.18) | collective-permute-done | bytes 786464 | tf_op jit(solution)/shard_map/ppermute | solution.py:27
  148.3 3.9 %collective-permute-done.13 = bf16[2,2,2,64,896]{4,3,2,1,0:T(8,128)(2,1)S(1)} collective-permute-done((bf16[2,2,2,64,896]{4,3,2,1,0:T(8,128)(2,1)S(1)}, bf16[2,2,2,64,896]{4,3,2,1,0:T(8,128)(2,1)S(1)}, u32[]{:S(2)}, u32[]{:S(2)}) %collective-permute-start.13) | collective-permute-done | bytes 917536 | tf_op jit(solution)/shard_map/ppermute | solution.py:27
  163.1 28.4 %shard_map.121 = bf16[2048,1536]{1,0:T(8,128)(2,1)} custom-call(bf16[2048,896]{1,0:T(8,128)(2,1)} %bitcast.198, bf16[2048,768]{1,0:T(8,128)(2,1)S(1)} %bitcast.194, f32[2048,5]{1,0:T(8,128)S(1)} %dynamic-slice_convert_fusion.share_ref, bf16[5,1536,256]{2,1,0:T(8,128)(2,1)} %gate_up_ref.1, bf16[5,128,1536]{2,1,0:T(8,128)(2,1)S(1)} %copy-done), custom_call_target="tpu_custom_call" | custom-call | tf_op jit(solution)/shard_map/pallas_call | solution.py:146
  191.5 3.0 %broadcast_select_fusion.2 = (bf16[1024,768]{1,0:T(8,128)(2,1)S(1)}, bf16[1024,768]{1,0:T(8,128)(2,1)S(1)}, bf16[1024,768]{1,0:T(8,128)(2,1)S(1)}, bf16[1024,768]{1,0:T(8,128)(2,1)S(1)}) fusion(pred[]{:T(512)S(6)} %eq.20, bf16[2048,1536]{1,0:T(8,128)(2,1)} %shard_map.121), kind=kLoop, calls=%fused_computation.40 | loop fusion | flops 3145728 | bytes 12582913 | tf_op jit(solution)/shard_map/jit(_where)/select_n | solution.py:99
  195.2 2.9 %collective-permute-done.25 = bf16[2,2,2,2,64,768]{5,4,2,3,0,1:T(8,128)(2,1)S(1)} collective-permute-done((bf16[2,2,2,2,64,768]{5,4,2,3,0,1:T(8,128)(2,1)S(1)}, bf16[2,2,2,2,64,768]{5,4,2,3,0,1:T(8,128)(2,1)S(1)}, u32[]{:S(2)}, u32[]{:S(2)}) %collective-permute-start.25) | collective-permute-done | bytes 1572896 | tf_op jit(solution)/shard_map/ppermute | solution.py:27
  205.7 13.7 %collective-permute-done.26 = bf16[2,2,2,64,768]{4,3,1,2,0:T(8,128)(2,1)} collective-permute-done((bf16[2,2,2,64,768]{4,3,1,2,0:T(8,128)(2,1)}, bf16[2,2,2,64,768]{4,3,1,2,0:T(8,128)(2,1)}, u32[]{:S(2)}, u32[]{:S(2)}) %collective-permute-start.26) | collective-permute-done | bytes 786464 | tf_op jit(solution)/shard_map/ppermute | solution.py:27
  226.5 5.1 %collective-permute-done.27 = bf16[2,2,64,768]{3,2,0,1:T(8,128)(2,1)S(1)} collective-permute-done((bf16[2,2,64,768]{3,2,0,1:T(8,128)(2,1)S(1)}, bf16[2,2,64,768]{3,2,0,1:T(8,128)(2,1)S(1)}, u32[]{:S(2)}, u32[]{:S(2)}) %collective-permute-start.27) | collective-permute-done | bytes 393248 | tf_op jit(solution)/shard_map/ppermute | solution.py:27
  236.3 2.8 %collective-permute-done.28 = bf16[2,64,768]{2,1,0:T(8,128)(2,1)S(1)} collective-permute-done((bf16[2,64,768]{2,1,0:T(8,128)(2,1)S(1)}, bf16[2,64,768]{2,1,0:T(8,128)(2,1)S(1)}, u32[]{:S(2)}, u32[]{:S(2)}) %collective-permute-start.28) | collective-permute-done | bytes 196640 | tf_op jit(solution)/shard_map/ppermute | solution.py:27
  240.0 4.1 %collective-permute-done.23 = bf16[2,64,768]{2,1,0:T(8,128)(2,1)S(1)} collective-permute-done((bf16[2,64,768]{2,1,0:T(8,128)(2,1)S(1)}, bf16[2,64,768]{2,1,0:T(8,128)(2,1)S(1)}, u32[]{:S(2)}, u32[]{:S(2)}) %collective-permute-start.23) | collective-permute-done | bytes 196640 | tf_op jit(solution)/shard_map/ppermute | solution.py:27
  245.7 4.6 %collective-permute-done.24 = bf16[64,768]{1,0:T(8,128)(2,1)S(1)} collective-permute-done((bf16[64,768]{1,0:T(8,128)(2,1)S(1)}, bf16[64,768]{1,0:T(8,128)(2,1)S(1)}, u32[]{:S(2)}, u32[]{:S(2)}) %collective-permute-start.24) | collective-permute-done | bytes 98336 | tf_op jit(solution)/shard_map/ppermute | solution.py:27
  (259 shorter events, 85.8 us)
Async XLA Ops:
  2.8 8.2 %collective-permute-start = (bf16[64,1536]{1,0:T(8,128)(2,1)S(1)}, bf16[64,1536]{1,0:T(8,128)(2,1)S(1)}, u32[]{:S(2)}, u32[]{:S(2)}) collective-permute-start(bf16[64,1536]{1,0:T(8,128)(2,1)S(1)} %fusion.18), channel_id=1, source_target_pairs={{0,4},{1,5},{2,6},{3,7},{4,0},{5,1},{6,2},{7,3},{8,12},{9,13},{10,... | collective-permute-start | bytes 589832 | tf_op jit(solution)/shard_map/ppermute | solution.py:27
  7.0 10.7 %collective-permute-start.3 = (bf16[1536,128]{0,1:T(8,128)(2,1)S(1)}, bf16[1536,128]{0,1:T(8,128)(2,1)S(1)}, u32[]{:S(2)}, u32[]{:S(2)}) collective-permute-start(bf16[1536,128]{0,1:T(8,128)(2,1)S(1)} %pad_maximum_fusion.6), channel_id=1, source_target_pairs={{0,8},{1,9},{2,10},{3,11},{4,12},{5,13},{6,14},{7,15},{8,0},{9,1},... | collective-permute-start | bytes 1179656 | tf_op jit(solution)/shard_map/ppermute | solution.py:27
  11.1 10.1 %collective-permute-start.1 = (bf16[128,1536]{1,0:T(8,128)(2,1)S(1)}, bf16[128,1536]{1,0:T(8,128)(2,1)S(1)}, u32[]{:S(2)}, u32[]{:S(2)}) collective-permute-start(bf16[128,1536]{1,0:T(8,128)(2,1)S(1)} %maximum_select_fusion.5), channel_id=1, source_target_pairs={{0,2},{1,3},{2,0},{3,1},{4,6},{5,7},{6,4},{7,5},{8,10},{9,11},{10,... | collective-permute-start | bytes 1179656 | tf_op jit(solution)/shard_map/ppermute | solution.py:27
  17.8 19.7 %collective-permute-start.4 = (bf16[1536,256]{0,1:T(8,128)(2,1)S(1)}, bf16[1536,256]{0,1:T(8,128)(2,1)S(1)}, u32[]{:S(2)}, u32[]{:S(2)}) collective-permute-start(bf16[1536,256]{0,1:T(8,128)(2,1)S(1)} %maximum_select_fusion.3), channel_id=1, source_target_pairs={{0,16},{1,17},{2,18},{3,19},{4,20},{5,21},{6,22},{7,23},{8,24},{9,... | collective-permute-start | bytes 2359304 | tf_op jit(solution)/shard_map/ppermute | solution.py:27
  21.4 17.6 %collective-permute-start.2 = (bf16[256,1536]{1,0:T(8,128)(2,1)S(1)}, bf16[256,1536]{1,0:T(8,128)(2,1)S(1)}, u32[]{:S(2)}, u32[]{:S(2)}) collective-permute-start(bf16[256,1536]{1,0:T(8,128)(2,1)S(1)} %maximum_select_fusion.2), channel_id=1, source_target_pairs={{0,1},{1,0},{2,3},{3,2},{4,5},{5,4},{6,7},{7,6},{8,9},{9,8},{10,11... | collective-permute-start | bytes 2359304 | tf_op jit(solution)/shard_map/ppermute | solution.py:27
  40.9 6.5 %collective-permute-start.5 = (bf16[512,128]{0,1:T(8,128)(2,1)S(1)}, bf16[512,128]{0,1:T(8,128)(2,1)S(1)}, u32[]{:S(2)}, u32[]{:S(2)}) collective-permute-start(bf16[512,128]{0,1:T(8,128)(2,1)S(1)} %pad_maximum_fusion.10), channel_id=1, source_target_pairs={{0,8},{1,9},{2,10},{3,11},{4,12},{5,13},{6,14},{7,15},{8,0},{9,1},... | collective-permute-start | bytes 393224 | tf_op jit(solution)/shard_map/ppermute | solution.py:27
  47.4 8.0 %collective-permute-start.6 = (bf16[1024,128]{0,1:T(8,128)(2,1)S(1)}, bf16[1024,128]{0,1:T(8,128)(2,1)S(1)}, u32[]{:S(2)}, u32[]{:S(2)}) collective-permute-start(bf16[1024,128]{0,1:T(8,128)(2,1)S(1)} %maximum_select_fusion.6), channel_id=1, source_target_pairs={{0,16},{1,17},{2,18},{3,19},{4,20},{5,21},{6,22},{7,23},{8,24},{9,... | collective-permute-start | bytes 786440 | tf_op jit(solution)/shard_map/ppermute | solution.py:27
  81.7 11.4 %collective-permute-start.8 = (bf16[2,64,1536]{2,1,0:T(8,128)(2,1)S(1)}, bf16[2,64,1536]{2,1,0:T(8,128)(2,1)S(1)}, u32[]{:S(2)}, u32[]{:S(2)}) collective-permute-start(bf16[2,64,1536]{2,1,0:T(8,128)(2,1)S(1)} %fusion.24), channel_id=1, source_target_pairs={{0,2},{1,3},{2,0},{3,1},{4,6},{5,7},{6,4},{7,5},{8,10},{9,11},{10,... | collective-permute-start | bytes 1179656 | tf_op jit(solution)/shard_map/ppermute | solution.py:27
  93.4 7.7 %collective-permute-start.9 = (bf16[64,1536]{1,0:T(8,128)(2,1)S(1)}, bf16[64,1536]{1,0:T(8,128)(2,1)S(1)}, u32[]{:S(2)}, u32[]{:S(2)}) collective-permute-start(bf16[64,1536]{1,0:T(8,128)(2,1)S(1)} %fusion.30), channel_id=1, source_target_pairs={{0,4},{1,5},{2,6},{3,7},{4,0},{5,1},{6,2},{7,3},{8,12},{9,13},{10,... | collective-permute-start | bytes 589832 | tf_op jit(solution)/shard_map/ppermute | solution.py:27
  102.1 6.2 %collective-permute-start.15 = (bf16[64,768]{1,0:T(8,128)(2,1)S(1)}, bf16[64,768]{1,0:T(8,128)(2,1)S(1)}, u32[]{:S(2)}, u32[]{:S(2)}) collective-permute-start(bf16[64,768]{1,0:T(8,128)(2,1)S(1)} %slice.220), channel_id=1, source_target_pairs={{0,16},{1,17},{2,18},{3,19},{4,20},{5,21},{6,22},{7,23},{8,24},{9,... | collective-permute-start | bytes 294920 | tf_op jit(solution)/shard_map/ppermute | solution.py:27
  108.4 6.4 %collective-permute-start.10 = (bf16[64,896]{1,0:T(8,128)(2,1)S(1)}, bf16[64,896]{1,0:T(8,128)(2,1)S(1)}, u32[]{:S(2)}, u32[]{:S(2)}) collective-permute-start(bf16[64,896]{1,0:T(8,128)(2,1)S(1)} %maximum_maximum_fusion), channel_id=1, source_target_pairs={{0,4},{1,5},{2,6},{3,7},{4,0},{5,1},{6,2},{7,3},{8,12},{9,13},{10,... | collective-permute-start | bytes 344072 | tf_op jit(solution)/shard_map/ppermute | solution.py:27
  109.6 7.3 %collective-permute-start.16 = (bf16[2,64,768]{2,1,0:T(8,128)(2,1)S(1)}, bf16[2,64,768]{2,1,0:T(8,128)(2,1)S(1)}, u32[]{:S(2)}, u32[]{:S(2)}) collective-permute-start(bf16[2,64,768]{2,1,0:T(8,128)(2,1)S(1)} %pad_maximum_fusion.9), channel_id=1, source_target_pairs={{0,4},{1,5},{2,6},{3,7},{4,0},{5,1},{6,2},{7,3},{8,12},{9,13},{10,... | collective-permute-start | bytes 589832 | tf_op jit(solution)/shard_map/ppermute | solution.py:27
  114.8 10.1 %collective-permute-start.11 = (bf16[2,64,896]{2,1,0:T(8,128)(2,1)S(1)}, bf16[2,64,896]{2,1,0:T(8,128)(2,1)S(1)}, u32[]{:S(2)}, u32[]{:S(2)}) collective-permute-start(bf16[2,64,896]{2,1,0:T(8,128)(2,1)S(1)} %pad_maximum_fusion.8), channel_id=1, source_target_pairs={{0,16},{1,17},{2,18},{3,19},{4,20},{5,21},{6,22},{7,23},{8,24},{9,... | collective-permute-start | bytes 688136 | tf_op jit(solution)/shard_map/ppermute | solution.py:27
  117.0 8.2 %collective-permute-start.17 = (bf16[2,2,64,768]{3,2,1,0:T(8,128)(2,1)S(1)}, bf16[2,2,64,768]{3,2,1,0:T(8,128)(2,1)S(1)}, u32[]{:S(2)}, u32[]{:S(2)}) collective-permute-start(bf16[2,2,64,768]{3,2,1,0:T(8,128)(2,1)S(1)} %pad_maximum_fusion.7), channel_id=1, source_target_pairs={{0,2},{1,3},{2,0},{3,1},{4,6},{5,7},{6,4},{7,5},{8,10},{9,11},{10,... | collective-permute-start | bytes 1179656 | tf_op jit(solution)/shard_map/ppermute | solution.py:27
  125.0 13.5 %collective-permute-start.12 = (bf16[2,2,64,896]{3,2,1,0:T(8,128)(2,1)S(1)}, bf16[2,2,64,896]{3,2,1,0:T(8,128)(2,1)S(1)}, u32[]{:S(2)}, u32[]{:S(2)}) collective-permute-start(bf16[2,2,64,896]{3,2,1,0:T(8,128)(2,1)S(1)} %pad_maximum_fusion.5), channel_id=1, source_target_pairs={{0,8},{1,9},{2,10},{3,11},{4,12},{5,13},{6,14},{7,15},{8,0},{9,1},... | collective-permute-start | bytes 1376264 | tf_op jit(solution)/shard_map/ppermute | solution.py:27
  125.3 21.6 %collective-permute-start.18 = (bf16[2,2,2,64,768]{4,3,2,1,0:T(8,128)(2,1)S(1)}, bf16[2,2,2,64,768]{4,3,2,1,0:T(8,128)(2,1)S(1)}, u32[]{:S(2)}, u32[]{:S(2)}) collective-permute-start(bf16[2,2,2,64,768]{4,3,2,1,0:T(8,128)(2,1)S(1)} %pad_maximum_fusion.4), channel_id=1, source_target_pairs={{0,8},{1,9},{2,10},{3,11},{4,12},{5,13},{6,14},{7,15},{8,0},{9,1},... | collective-permute-start | bytes 2359304 | tf_op jit(solution)/shard_map/ppermute | solution.py:27
  138.7 13.5 %collective-permute-start.13 = (bf16[2,2,2,64,896]{4,3,2,1,0:T(8,128)(2,1)S(1)}, bf16[2,2,2,64,896]{4,3,2,1,0:T(8,128)(2,1)S(1)}, u32[]{:S(2)}, u32[]{:S(2)}) collective-permute-start(bf16[2,2,2,64,896]{4,3,2,1,0:T(8,128)(2,1)S(1)} %pad_maximum_fusion.3), channel_id=1, source_target_pairs={{0,2},{1,3},{2,0},{3,1},{4,6},{5,7},{6,4},{7,5},{8,10},{9,11},{10,... | collective-permute-start | bytes 2752520 | tf_op jit(solution)/shard_map/ppermute | solution.py:27
  199.5 19.9 %collective-permute-start.26 = (bf16[2,2,2,64,768]{4,3,1,2,0:T(8,128)(2,1)}, bf16[2,2,2,64,768]{4,3,1,2,0:T(8,128)(2,1)}, u32[]{:S(2)}, u32[]{:S(2)}) collective-permute-start(bf16[2,2,2,64,768]{4,3,1,2,0:T(8,128)(2,1)} %fusion.13), channel_id=1, source_target_pairs={{0,8},{1,9},{2,10},{3,11},{4,12},{5,13},{6,14},{7,15},{8,0},{9,1},... | collective-permute-start | bytes 2359304 | tf_op jit(solution)/shard_map/ppermute | solution.py:27
  203.5 20.1 %collective-permute-start.21 = (bf16[2,2,2,64,768]{4,3,2,1,0:T(8,128)(2,1)}, bf16[2,2,2,64,768]{4,3,2,1,0:T(8,128)(2,1)}, u32[]{:S(2)}, u32[]{:S(2)}) collective-permute-start(bf16[2,2,2,64,768]{4,3,2,1,0:T(8,128)(2,1)} %fusion.12), channel_id=1, source_target_pairs={{0,2},{1,3},{2,0},{3,1},{4,6},{5,7},{6,4},{7,5},{8,10},{9,11},{10,... | collective-permute-start | bytes 2359304 | tf_op jit(solution)/shard_map/ppermute | solution.py:27
  221.1 10.6 %collective-permute-start.27 = (bf16[2,2,64,768]{3,2,0,1:T(8,128)(2,1)S(1)}, bf16[2,2,64,768]{3,2,0,1:T(8,128)(2,1)S(1)}, u32[]{:S(2)}, u32[]{:S(2)}) collective-permute-start(bf16[2,2,64,768]{3,2,0,1:T(8,128)(2,1)S(1)} %fusion.26), channel_id=1, source_target_pairs={{0,2},{1,3},{2,0},{3,1},{4,6},{5,7},{6,4},{7,5},{8,10},{9,11},{10,... | collective-permute-start | bytes 1179656 | tf_op jit(solution)/shard_map/ppermute | solution.py:27
  225.1 10.9 %collective-permute-start.22 = (bf16[2,2,64,768]{3,2,1,0:T(8,128)(2,1)S(1)}, bf16[2,2,64,768]{3,2,1,0:T(8,128)(2,1)S(1)}, u32[]{:S(2)}, u32[]{:S(2)}) collective-permute-start(bf16[2,2,64,768]{3,2,1,0:T(8,128)(2,1)S(1)} %fusion.25), channel_id=1, source_target_pairs={{0,8},{1,9},{2,10},{3,11},{4,12},{5,13},{6,14},{7,15},{8,0},{9,1},... | collective-permute-start | bytes 1179656 | tf_op jit(solution)/shard_map/ppermute | solution.py:27
  231.8 7.3 %collective-permute-start.28 = (bf16[2,64,768]{2,1,0:T(8,128)(2,1)S(1)}, bf16[2,64,768]{2,1,0:T(8,128)(2,1)S(1)}, u32[]{:S(2)}, u32[]{:S(2)}) collective-permute-start(bf16[2,64,768]{2,1,0:T(8,128)(2,1)S(1)} %fusion.32), channel_id=1, source_target_pairs={{0,4},{1,5},{2,6},{3,7},{4,0},{5,1},{6,2},{7,3},{8,12},{9,13},{10,... | collective-permute-start | bytes 589832 | tf_op jit(solution)/shard_map/ppermute | solution.py:27
  236.2 7.9 %collective-permute-start.23 = (bf16[2,64,768]{2,1,0:T(8,128)(2,1)S(1)}, bf16[2,64,768]{2,1,0:T(8,128)(2,1)S(1)}, u32[]{:S(2)}, u32[]{:S(2)}) collective-permute-start(bf16[2,64,768]{2,1,0:T(8,128)(2,1)S(1)} %fusion.31), channel_id=1, source_target_pairs={{0,16},{1,17},{2,18},{3,19},{4,20},{5,21},{6,22},{7,23},{8,24},{9,... | collective-permute-start | bytes 589832 | tf_op jit(solution)/shard_map/ppermute | solution.py:27
  239.2 6.5 %collective-permute-start.29 = (bf16[64,768]{1,0:T(8,128)(2,1)S(1)}, bf16[64,768]{1,0:T(8,128)(2,1)S(1)}, u32[]{:S(2)}, u32[]{:S(2)}) collective-permute-start(bf16[64,768]{1,0:T(8,128)(2,1)S(1)} %fusion.35), channel_id=1, source_target_pairs={{0,16},{1,17},{2,18},{3,19},{4,20},{5,21},{6,22},{7,23},{8,24},{9,... | collective-permute-start | bytes 294920 | tf_op jit(solution)/shard_map/ppermute | solution.py:27
  (21 other events, 154.9 us)

commit v8 on v7

--- a/solution.py
+++ b/solution.py
@@ -202,16 +202,18 @@
     )
     normed = rms_norm(hidden, attn_gain)
     qkv_width = w_qkv.shape[1]
-    joined = jnp.concatenate([w_qkv, w_out], axis=1)
-    (gathered_cols,) = gather_levels(
-        (joined,),
+    (w_group,) = gather_levels(
+        (w_qkv,),
         quarter_bits,
         (1,),
         lambda payload, level_bit: (partner(payload[0], TENSOR, level_bit),),
     )
-    by_quarter = gathered_cols.reshape(model_width, quarters, joined.shape[1])
-    w_group = by_quarter[:, :, :qkv_width].reshape(model_width, quarters * qkv_width)
-    w_attn_out = by_quarter[:, :, qkv_width:].reshape(model_width, GQ * HD)
+    (w_attn_out,) = gather_levels(
+        (w_out,),
+        quarter_bits,
+        (1,),
+        lambda payload, level_bit: (partner(payload[0], TENSOR, level_bit),),
+    )
     w_query = w_group[:, : GQ * HD]
     w_pairs = w_group[:, GQ * HD :]
     (own_rows,) = gather_levels(

time: 252 us -> 241 us (0.956)
  waiting for transfers between devices: 135 us -> 107 us
  starting transfers between devices: 24.7 us -> 47.7 us
  local copies, waits for them, and re-layouts: 17 us -> 14.1 us
  matrix products: 7.17 us -> 4.55 us
    ppermute x30 -> x32, waiting for transfers between devices: 135 us -> 107 us  [partner(): return lax.ppermute(value, axis, pairs)]
    ppermute x30 -> x32, starting transfers between devices: 24.7 us -> 47.7 us  [partner(): return lax.ppermute(value, axis, pairs)]
    unnamed x29 -> x31, local copies, waits for them, and re-layouts: 6.82 us -> 5.73 us
  transfers between devices with their start and end apart: 30 -> 32, of which waited for: 26 -> 25; matrix products, arithmetic and copies ran while one was open for 8% -> 14% of each run, Pallas kernels for 0% -> 0%
where the time goes in v8:
time: 241 us; the launch traced here: 239 us
  waiting for transfers between devices  107 us (44%)
  starting transfers between devices  47.7 us (20%)
  Pallas kernels  28.4 us (12%)
  other arithmetic  27.3 us (11%)
  local copies, waits for them, and re-layouts  14.1 us (6%)
  loops' own time  7.26 us (3%)
  matrix products  4.55 us (2%)
    ppermute x32, waiting for transfers between devices, partner(): return lax.ppermute(value, axis, pairs)  107 us
    ppermute x32, starting transfers between devices, partner(): return lax.ppermute(value, axis, pairs)  47.7 us
    pallas_call x1, Pallas kernels, dense_experts(): pl.pallas_call(expert_block, grid=(row_count // tile,), in_specs=[pl.Bloc...  28.4 us
    another operation x19, other arithmetic, gather_any(): state = jnp.stack([lower_rows, upper_rows], axis=0)  7.56 us
    another operation x1, loops' own time, on_device(): lax.map(attend, jnp.arange(rows_quarter // block_rows, dtype=jnp.int32))  6.97 us
    unnamed x31, local copies, waits for them, and re-layouts  5.73 us
  transfers between devices with their start and end apart: 32, of which 25 were waited for; matrix products, arithmetic and copies ran while one was open for 14% of the time, Pallas kernels for 0%

profile of v8, /device:TPU:24, one launch (start us, length us, event | category | flops | bytes accessed | tf_op | source)
XLA Modules:
  0.0 238.5 jit_solution(736399022616416201)
XLA Ops:
  3.6 3.1 %collective-permute-start = (bf16[64,1536]{1,0:T(8,128)(2,1)S(1)}, bf16[64,1536]{1,0:T(8,128)(2,1)S(1)}, u32[]{:S(2)}, u32[]{:S(2)}) collective-permute-start(bf16[64,1536]{1,0:T(8,128)(2,1)S(1)} %fusion.27), channel_id=1, source_target_pairs={{0,4},{1,5},{2,6},{3,7},{4,0},{5,1},{6,2},{7,3},{8,12},{9,13},{10,... | collective-permute-start | bytes 589832 | tf_op jit(solution)/shard_map/ppermute | solution.py:27
  15.2 6.3 %collective-permute-done.1 = bf16[128,1536]{1,0:T(8,128)(2,1)S(1)} collective-permute-done((bf16[128,1536]{1,0:T(8,128)(2,1)S(1)}, bf16[128,1536]{1,0:T(8,128)(2,1)S(1)}, u32[]{:S(2)}, u32[]{:S(2)}) %collective-permute-start.1) | collective-permute-done | bytes 393248 | tf_op jit(solution)/shard_map/ppermute | solution.py:27
  23.4 4.3 %collective-permute-done.4 = bf16[1536,160]{0,1:T(8,128)(2,1)S(1)} collective-permute-done((bf16[1536,160]{0,1:T(8,128)(2,1)S(1)}, bf16[1536,160]{0,1:T(8,128)(2,1)S(1)}, u32[]{:S(2)}, u32[]{:S(2)}) %collective-permute-start.4) | collective-permute-done | bytes 491552 | tf_op jit(solution)/shard_map/ppermute | solution.py:27
  32.6 3.0 %collective-permute-done.5 = bf16[512,128]{0,1:T(8,128)(2,1)S(1)} collective-permute-done((bf16[512,128]{0,1:T(8,128)(2,1)S(1)}, bf16[512,128]{0,1:T(8,128)(2,1)S(1)}, u32[]{:S(2)}, u32[]{:S(2)}) %collective-permute-start.5) | collective-permute-done | bytes 131104 | tf_op jit(solution)/shard_map/ppermute | solution.py:27
  38.6 6.0 %collective-permute-done.6 = bf16[1024,128]{0,1:T(8,128)(2,1)S(1)} collective-permute-done((bf16[1024,128]{0,1:T(8,128)(2,1)S(1)}, bf16[1024,128]{0,1:T(8,128)(2,1)S(1)}, u32[]{:S(2)}, u32[]{:S(2)}) %collective-permute-start.6) | collective-permute-done | bytes 262176 | tf_op jit(solution)/shard_map/ppermute | solution.py:27
  45.0 16.1 %while.59 = (s32[]{:T(128)}, bf16[2,256,192]{1,2,0:T(8,128)(2,1)S(1)}, s32[2]{0:T(128)S(1)}, s32[]{:T(128)}, s32[2048]{0:T(1024)S(1)}, /*index=5*/bf16[3,512,64]...) while((s32[]{:T(128)}, ...), condition=%wide.region_8.9_spmd, body=%wide.region_3.8_spmd.sunk | while | flops 104007976 | bytes 8950756 | solution.py:293
  49.9 4.0 %while.60 = (s32[]{:T(128)}, f32[768]{0:T(1024)S(1)}, f32[768]{0:T(1024)S(1)}, f32[768,64]{0,1:T(8,128)S(1)}, s32[]{:T(128)}, /*index=5*/s32[256]{0:T(256)S(1)},...) while((s32[]{:T(128)}, f32[768]{0:T(1024)S(1)}, ...), condition=%wide.region_7.7_spmd.clone, body=%wide.region_4.6_spmd.clone.sunk | while | flops 103909632 | bytes 7464147 | solution.py:289
  66.1 10.2 %collective-permute-done.10 = bf16[2,64,1536]{2,1,0:T(8,128)(2,1)S(1)} collective-permute-done((bf16[2,64,1536]{2,1,0:T(8,128)(2,1)S(1)}, bf16[2,64,1536]{2,1,0:T(8,128)(2,1)S(1)}, u32[]{:S(2)}, u32[]{:S(2)}) %collective-permute-start.10) | collective-permute-done | bytes 393248 | tf_op jit(solution)/shard_map/ppermute | solution.py:27
  79.2 5.1 %collective-permute-done.11 = bf16[64,1536]{1,0:T(8,128)(2,1)S(1)} collective-permute-done((bf16[64,1536]{1,0:T(8,128)(2,1)S(1)}, bf16[64,1536]{1,0:T(8,128)(2,1)S(1)}, u32[]{:S(2)}, u32[]{:S(2)}) %collective-permute-start.11) | collective-permute-done | bytes 196640 | tf_op jit(solution)/shard_map/ppermute | solution.py:27
  85.2 5.3 %collective-permute-start.17 = (bf16[64,768]{1,0:T(8,128)(2,1)S(1)}, bf16[64,768]{1,0:T(8,128)(2,1)S(1)}, u32[]{:S(2)}, u32[]{:S(2)}) collective-permute-start(bf16[64,768]{1,0:T(8,128)(2,1)S(1)} %slice.210), channel_id=1, source_target_pairs={{0,16},{1,17},{2,18},{3,19},{4,20},{5,21},{6,22},{7,23},{8,24},{9,... | collective-permute-start | bytes 294920 | tf_op jit(solution)/shard_map/ppermute | solution.py:27
  97.0 3.7 %collective-permute-done.12 = bf16[64,896]{1,0:T(8,128)(2,1)S(1)} collective-permute-done((bf16[64,896]{1,0:T(8,128)(2,1)S(1)}, bf16[64,896]{1,0:T(8,128)(2,1)S(1)}, u32[]{:S(2)}, u32[]{:S(2)}) %collective-permute-start.12) | collective-permute-done | bytes 114720 | tf_op jit(solution)/shard_map/ppermute | solution.py:27
  100.8 3.3 %collective-permute-start.13 = (bf16[2,64,896]{2,1,0:T(8,128)(2,1)S(1)}, bf16[2,64,896]{2,1,0:T(8,128)(2,1)S(1)}, u32[]{:S(2)}, u32[]{:S(2)}) collective-permute-start(bf16[2,64,896]{2,1,0:T(8,128)(2,1)S(1)} %pad_maximum_fusion.7), channel_id=1, source_target_pairs={{0,16},{1,17},{2,18},{3,19},{4,20},{5,21},{6,22},{7,23},{8,24},{9,... | collective-permute-start | bytes 688136 | tf_op jit(solution)/shard_map/ppermute | solution.py:27
  104.9 3.5 %collective-permute-done.13 = bf16[2,64,896]{2,1,0:T(8,128)(2,1)S(1)} collective-permute-done((bf16[2,64,896]{2,1,0:T(8,128)(2,1)S(1)}, bf16[2,64,896]{2,1,0:T(8,128)(2,1)S(1)}, u32[]{:S(2)}, u32[]{:S(2)}) %collective-permute-start.13) | collective-permute-done | bytes 229408 | tf_op jit(solution)/shard_map/ppermute | solution.py:27
  108.5 6.5 %collective-permute-start.14 = (bf16[2,2,64,896]{3,2,1,0:T(8,128)(2,1)S(1)}, bf16[2,2,64,896]{3,2,1,0:T(8,128)(2,1)S(1)}, u32[]{:S(2)}, u32[]{:S(2)}) collective-permute-start(bf16[2,2,64,896]{3,2,1,0:T(8,128)(2,1)S(1)} %pad_maximum_fusion.5), channel_id=1, source_target_pairs={{0,8},{1,9},{2,10},{3,11},{4,12},{5,13},{6,14},{7,15},{8,0},{9,1},... | collective-permute-start | bytes 1376264 | tf_op jit(solution)/shard_map/ppermute | solution.py:27
  116.1 10.3 %collective-permute-done.14 = bf16[2,2,64,896]{3,2,1,0:T(8,128)(2,1)S(1)} collective-permute-done((bf16[2,2,64,896]{3,2,1,0:T(8,128)(2,1)S(1)}, bf16[2,2,64,896]{3,2,1,0:T(8,128)(2,1)S(1)}, u32[]{:S(2)}, u32[]{:S(2)}) %collective-permute-start.14) | collective-permute-done | bytes 458784 | tf_op jit(solution)/shard_map/ppermute | solution.py:27
  127.5 8.2 %collective-permute-done.20 = bf16[2,2,2,64,768]{4,3,2,1,0:T(8,128)(2,1)S(1)} collective-permute-done((bf16[2,2,2,64,768]{4,3,2,1,0:T(8,128)(2,1)S(1)}, bf16[2,2,2,64,768]{4,3,2,1,0:T(8,128)(2,1)S(1)}, u32[]{:S(2)}, u32[]{:S(2)}) %collective-permute-start.20) | collective-permute-done | bytes 786464 | tf_op jit(solution)/shard_map/ppermute | solution.py:27
  137.2 2.9 %collective-permute-done.15 = bf16[2,2,2,64,896]{4,3,2,1,0:T(8,128)(2,1)S(1)} collective-permute-done((bf16[2,2,2,64,896]{4,3,2,1,0:T(8,128)(2,1)S(1)}, bf16[2,2,2,64,896]{4,3,2,1,0:T(8,128)(2,1)S(1)}, u32[]{:S(2)}, u32[]{:S(2)}) %collective-permute-start.15) | collective-permute-done | bytes 917536 | tf_op jit(solution)/shard_map/ppermute | solution.py:27
  151.0 28.4 %shard_map.121 = bf16[2048,1536]{1,0:T(8,128)(2,1)} custom-call(bf16[2048,896]{1,0:T(8,128)(2,1)} %bitcast.194, bf16[2048,768]{1,0:T(8,128)(2,1)S(1)} %bitcast.190, f32[2048,5]{1,0:T(8,128)S(1)} %dynamic-slice_convert_fusion.share_ref, bf16[5,1536,256]{2,1,0:T(8,128)(2,1)} %gate_up_ref.1, bf16[5,128,1536]{2,1,0:T(8,128)(2,1)S(1)} %copy-done), custom_call_target="tpu_custom_call" | custom-call | tf_op jit(solution)/shard_map/pallas_call | solution.py:146
  179.3 3.0 %broadcast_select_fusion.2 = (bf16[1024,768]{1,0:T(8,128)(2,1)S(1)}, bf16[1024,768]{1,0:T(8,128)(2,1)S(1)}, bf16[1024,768]{1,0:T(8,128)(2,1)S(1)}, bf16[1024,768]{1,0:T(8,128)(2,1)S(1)}) fusion(pred[]{:T(512)S(6)} %eq.20, bf16[2048,1536]{1,0:T(8,128)(2,1)} %shard_map.121), kind=kLoop, calls=%fused_computation.39 | loop fusion | flops 3145728 | bytes 12582913 | tf_op jit(solution)/shard_map/jit(_where)/select_n | solution.py:99
  183.1 2.9 %collective-permute-done.27 = bf16[2,2,2,2,64,768]{5,4,2,3,0,1:T(8,128)(2,1)S(1)} collective-permute-done((bf16[2,2,2,2,64,768]{5,4,2,3,0,1:T(8,128)(2,1)S(1)}, bf16[2,2,2,2,64,768]{5,4,2,3,0,1:T(8,128)(2,1)S(1)}, u32[]{:S(2)}, u32[]{:S(2)}) %collective-permute-start.27) | collective-permute-done | bytes 1572896 | tf_op jit(solution)/shard_map/ppermute | solution.py:27
  194.9 12.7 %collective-permute-done.28 = bf16[2,2,2,64,768]{4,3,1,2,0:T(8,128)(2,1)} collective-permute-done((bf16[2,2,2,64,768]{4,3,1,2,0:T(8,128)(2,1)}, bf16[2,2,2,64,768]{4,3,1,2,0:T(8,128)(2,1)}, u32[]{:S(2)}, u32[]{:S(2)}) %collective-permute-start.28) | collective-permute-done | bytes 786464 | tf_op jit(solution)/shard_map/ppermute | solution.py:27
  215.1 5.4 %collective-permute-done.29 = bf16[2,2,64,768]{3,2,0,1:T(8,128)(2,1)S(1)} collective-permute-done((bf16[2,2,64,768]{3,2,0,1:T(8,128)(2,1)S(1)}, bf16[2,2,64,768]{3,2,0,1:T(8,128)(2,1)S(1)}, u32[]{:S(2)}, u32[]{:S(2)}) %collective-permute-start.29) | collective-permute-done | bytes 393248 | tf_op jit(solution)/shard_map/ppermute | solution.py:27
  224.2 4.1 %collective-permute-done.30 = bf16[2,64,768]{2,1,0:T(8,128)(2,1)S(1)} collective-permute-done((bf16[2,64,768]{2,1,0:T(8,128)(2,1)S(1)}, bf16[2,64,768]{2,1,0:T(8,128)(2,1)S(1)}, u32[]{:S(2)}, u32[]{:S(2)}) %collective-permute-start.30) | collective-permute-done | bytes 196640 | tf_op jit(solution)/shard_map/ppermute | solution.py:27
  234.6 3.1 %collective-permute-done.26 = bf16[64,768]{1,0:T(8,128)(2,1)S(1)} collective-permute-done((bf16[64,768]{1,0:T(8,128)(2,1)S(1)}, bf16[64,768]{1,0:T(8,128)(2,1)S(1)}, u32[]{:S(2)}, u32[]{:S(2)}) %collective-permute-start.26) | collective-permute-done | bytes 98336 | tf_op jit(solution)/shard_map/ppermute | solution.py:27
  (229 shorter events, 90.1 us)
Async XLA Ops:
  0.6 21.4 %collective-permute-start.7 = (bf16[1536,48]{0,1:T(8,128)(2,1)}, bf16[1536,48]{0,1:T(8,128)(2,1)S(1)}, u32[]{:S(2)}, u32[]{:S(2)}) collective-permute-start(bf16[1536,48]{0,1:T(8,128)(2,1)} %param.20), channel_id=1, source_target_pairs={{0,8},{1,9},{2,10},{3,11},{4,12},{5,13},{6,14},{7,15},{8,0},{9,1},... | collective-permute-start | bytes 442376 | tf_op jit(solution)/shard_map/ppermute | solution.py:27
  3.6 8.0 %collective-permute-start = (bf16[64,1536]{1,0:T(8,128)(2,1)S(1)}, bf16[64,1536]{1,0:T(8,128)(2,1)S(1)}, u32[]{:S(2)}, u32[]{:S(2)}) collective-permute-start(bf16[64,1536]{1,0:T(8,128)(2,1)S(1)} %fusion.27), channel_id=1, source_target_pairs={{0,4},{1,5},{2,6},{3,7},{4,0},{5,1},{6,2},{7,3},{8,12},{9,13},{10,... | collective-permute-start | bytes 589832 | tf_op jit(solution)/shard_map/ppermute | solution.py:27
  6.7 7.3 %collective-permute-start.3 = (bf16[1536,80]{0,1:T(8,128)(2,1)}, bf16[1536,80]{0,1:T(8,128)(2,1)S(1)}, u32[]{:S(2)}, u32[]{:S(2)}) collective-permute-start(bf16[1536,80]{0,1:T(8,128)(2,1)} %param.19), channel_id=1, source_target_pairs={{0,8},{1,9},{2,10},{3,11},{4,12},{5,13},{6,14},{7,15},{8,0},{9,1},... | collective-permute-start | bytes 737288 | tf_op jit(solution)/shard_map/ppermute | solution.py:27
  11.6 9.8 %collective-permute-start.1 = (bf16[128,1536]{1,0:T(8,128)(2,1)S(1)}, bf16[128,1536]{1,0:T(8,128)(2,1)S(1)}, u32[]{:S(2)}, u32[]{:S(2)}) collective-permute-start(bf16[128,1536]{1,0:T(8,128)(2,1)S(1)} %maximum_select_fusion.6), channel_id=1, source_target_pairs={{0,2},{1,3},{2,0},{3,1},{4,6},{5,7},{6,4},{7,5},{8,10},{9,11},{10,... | collective-permute-start | bytes 1179656 | tf_op jit(solution)/shard_map/ppermute | solution.py:27
  14.2 13.6 %collective-permute-start.4 = (bf16[1536,160]{0,1:T(8,128)(2,1)S(1)}, bf16[1536,160]{0,1:T(8,128)(2,1)S(1)}, u32[]{:S(2)}, u32[]{:S(2)}) collective-permute-start(bf16[1536,160]{0,1:T(8,128)(2,1)S(1)} %maximum_select_fusion.5), channel_id=1, source_target_pairs={{0,16},{1,17},{2,18},{3,19},{4,20},{5,21},{6,22},{7,23},{8,24},{9,... | collective-permute-start | bytes 1474568 | tf_op jit(solution)/shard_map/ppermute | solution.py:27
  22.1 39.1 %collective-permute-start.8 = (bf16[1536,96]{0,1:T(8,128)(2,1)S(1)}, bf16[1536,96]{0,1:T(8,128)(2,1)S(1)}, u32[]{:S(2)}, u32[]{:S(2)}) collective-permute-start(bf16[1536,96]{0,1:T(8,128)(2,1)S(1)} %maximum_select_fusion.7), channel_id=1, source_target_pairs={{0,16},{1,17},{2,18},{3,19},{4,20},{5,21},{6,22},{7,23},{8,24},{9,... | collective-permute-start | bytes 884744 | tf_op jit(solution)/shard_map/ppermute | solution.py:27
  35.7 8.9 %collective-permute-start.6 = (bf16[1024,128]{0,1:T(8,128)(2,1)S(1)}, bf16[1024,128]{0,1:T(8,128)(2,1)S(1)}, u32[]{:S(2)}, u32[]{:S(2)}) collective-permute-start(bf16[1024,128]{0,1:T(8,128)(2,1)S(1)} %maximum_select_fusion.8), channel_id=1, source_target_pairs={{0,16},{1,17},{2,18},{3,19},{4,20},{5,21},{6,22},{7,23},{8,24},{9,... | collective-permute-start | bytes 786440 | tf_op jit(solution)/shard_map/ppermute | solution.py:27
  65.1 11.2 %collective-permute-start.10 = (bf16[2,64,1536]{2,1,0:T(8,128)(2,1)S(1)}, bf16[2,64,1536]{2,1,0:T(8,128)(2,1)S(1)}, u32[]{:S(2)}, u32[]{:S(2)}) collective-permute-start(bf16[2,64,1536]{2,1,0:T(8,128)(2,1)S(1)} %fusion.33), channel_id=1, source_target_pairs={{0,2},{1,3},{2,0},{3,1},{4,6},{5,7},{6,4},{7,5},{8,10},{9,11},{10,... | collective-permute-start | bytes 1179656 | tf_op jit(solution)/shard_map/ppermute | solution.py:27
  76.5 7.7 %collective-permute-start.11 = (bf16[64,1536]{1,0:T(8,128)(2,1)S(1)}, bf16[64,1536]{1,0:T(8,128)(2,1)S(1)}, u32[]{:S(2)}, u32[]{:S(2)}) collective-permute-start(bf16[64,1536]{1,0:T(8,128)(2,1)S(1)} %fusion.39), channel_id=1, source_target_pairs={{0,4},{1,5},{2,6},{3,7},{4,0},{5,1},{6,2},{7,3},{8,12},{9,13},{10,... | collective-permute-start | bytes 589832 | tf_op jit(solution)/shard_map/ppermute | solution.py:27
  85.2 7.9 %collective-permute-start.17 = (bf16[64,768]{1,0:T(8,128)(2,1)S(1)}, bf16[64,768]{1,0:T(8,128)(2,1)S(1)}, u32[]{:S(2)}, u32[]{:S(2)}) collective-permute-start(bf16[64,768]{1,0:T(8,128)(2,1)S(1)} %slice.210), channel_id=1, source_target_pairs={{0,16},{1,17},{2,18},{3,19},{4,20},{5,21},{6,22},{7,23},{8,24},{9,... | collective-permute-start | bytes 294920 | tf_op jit(solution)/shard_map/ppermute | solution.py:27
  93.2 7.4 %collective-permute-start.12 = (bf16[64,896]{1,0:T(8,128)(2,1)S(1)}, bf16[64,896]{1,0:T(8,128)(2,1)S(1)}, u32[]{:S(2)}, u32[]{:S(2)}) collective-permute-start(bf16[64,896]{1,0:T(8,128)(2,1)S(1)} %maximum_maximum_fusion), channel_id=1, source_target_pairs={{0,4},{1,5},{2,6},{3,7},{4,0},{5,1},{6,2},{7,3},{8,12},{9,13},{10,... | collective-permute-start | bytes 344072 | tf_op jit(solution)/shard_map/ppermute | solution.py:27
  95.9 8.2 %collective-permute-start.18 = (bf16[2,64,768]{2,1,0:T(8,128)(2,1)S(1)}, bf16[2,64,768]{2,1,0:T(8,128)(2,1)S(1)}, u32[]{:S(2)}, u32[]{:S(2)}) collective-permute-start(bf16[2,64,768]{2,1,0:T(8,128)(2,1)S(1)} %pad_maximum_fusion.8), channel_id=1, source_target_pairs={{0,4},{1,5},{2,6},{3,7},{4,0},{5,1},{6,2},{7,3},{8,12},{9,13},{10,... | collective-permute-start | bytes 589832 | tf_op jit(solution)/shard_map/ppermute | solution.py:27
  100.8 7.6 %collective-permute-start.13 = (bf16[2,64,896]{2,1,0:T(8,128)(2,1)S(1)}, bf16[2,64,896]{2,1,0:T(8,128)(2,1)S(1)}, u32[]{:S(2)}, u32[]{:S(2)}) collective-permute-start(bf16[2,64,896]{2,1,0:T(8,128)(2,1)S(1)} %pad_maximum_fusion.7), channel_id=1, source_target_pairs={{0,16},{1,17},{2,18},{3,19},{4,20},{5,21},{6,22},{7,23},{8,24},{9,... | collective-permute-start | bytes 688136 | tf_op jit(solution)/shard_map/ppermute | solution.py:27
  104.2 10.8 %collective-permute-start.19 = (bf16[2,2,64,768]{3,2,1,0:T(8,128)(2,1)S(1)}, bf16[2,2,64,768]{3,2,1,0:T(8,128)(2,1)S(1)}, u32[]{:S(2)}, u32[]{:S(2)}) collective-permute-start(bf16[2,2,64,768]{3,2,1,0:T(8,128)(2,1)S(1)} %pad_maximum_fusion.6), channel_id=1, source_target_pairs={{0,2},{1,3},{2,0},{3,1},{4,6},{5,7},{6,4},{7,5},{8,10},{9,11},{10,... | collective-permute-start | bytes 1179656 | tf_op jit(solution)/shard_map/ppermute | solution.py:27
  108.5 17.8 %collective-permute-start.14 = (bf16[2,2,64,896]{3,2,1,0:T(8,128)(2,1)S(1)}, bf16[2,2,64,896]{3,2,1,0:T(8,128)(2,1)S(1)}, u32[]{:S(2)}, u32[]{:S(2)}) collective-permute-start(bf16[2,2,64,896]{3,2,1,0:T(8,128)(2,1)S(1)} %pad_maximum_fusion.5), channel_id=1, source_target_pairs={{0,8},{1,9},{2,10},{3,11},{4,12},{5,13},{6,14},{7,15},{8,0},{9,1},... | collective-permute-start | bytes 1376264 | tf_op jit(solution)/shard_map/ppermute | solution.py:27
  115.1 20.6 %collective-permute-start.20 = (bf16[2,2,2,64,768]{4,3,2,1,0:T(8,128)(2,1)S(1)}, bf16[2,2,2,64,768]{4,3,2,1,0:T(8,128)(2,1)S(1)}, u32[]{:S(2)}, u32[]{:S(2)}) collective-permute-start(bf16[2,2,2,64,768]{4,3,2,1,0:T(8,128)(2,1)S(1)} %pad_maximum_fusion.4), channel_id=1, source_target_pairs={{0,8},{1,9},{2,10},{3,11},{4,12},{5,13},{6,14},{7,15},{8,0},{9,1},... | collective-permute-start | bytes 2359304 | tf_op jit(solution)/shard_map/ppermute | solution.py:27
  126.6 13.5 %collective-permute-start.15 = (bf16[2,2,2,64,896]{4,3,2,1,0:T(8,128)(2,1)S(1)}, bf16[2,2,2,64,896]{4,3,2,1,0:T(8,128)(2,1)S(1)}, u32[]{:S(2)}, u32[]{:S(2)}) collective-permute-start(bf16[2,2,2,64,896]{4,3,2,1,0:T(8,128)(2,1)S(1)} %pad_maximum_fusion.3), channel_id=1, source_target_pairs={{0,2},{1,3},{2,0},{3,1},{4,6},{5,7},{6,4},{7,5},{8,10},{9,11},{10,... | collective-permute-start | bytes 2752520 | tf_op jit(solution)/shard_map/ppermute | solution.py:27
  182.7 6.7 %collective-permute-start.22 = (bf16[2,2,2,2,64,768]{5,4,3,2,1,0:T(8,128)(2,1)S(1)}, bf16[2,2,2,2,64,768]{5,4,3,2,1,0:T(8,128)(2,1)S(1)}, u32[]{:S(2)}, u32[]{:S(2)}) collective-permute-start(bf16[2,2,2,2,64,768]{5,4,3,2,1,0:T(8,128)(2,1)S(1)} %bitcast.203), channel_id=1, source_target_pairs={{0,1},{1,0},{2,3},{3,2},{4,5},{5,4},{6,7},{7,6},{8,9},{9,8},{10,11... | collective-permute-start | bytes 4718600 | tf_op jit(solution)/shard_map/ppermute | solution.py:27
  187.4 20.2 %collective-permute-start.28 = (bf16[2,2,2,64,768]{4,3,1,2,0:T(8,128)(2,1)}, bf16[2,2,2,64,768]{4,3,1,2,0:T(8,128)(2,1)}, u32[]{:S(2)}, u32[]{:S(2)}) collective-permute-start(bf16[2,2,2,64,768]{4,3,1,2,0:T(8,128)(2,1)} %fusion.13), channel_id=1, source_target_pairs={{0,8},{1,9},{2,10},{3,11},{4,12},{5,13},{6,14},{7,15},{8,0},{9,1},... | collective-permute-start | bytes 2359304 | tf_op jit(solution)/shard_map/ppermute | solution.py:27
  192.5 20.2 %collective-permute-start.23 = (bf16[2,2,2,64,768]{4,3,2,1,0:T(8,128)(2,1)}, bf16[2,2,2,64,768]{4,3,2,1,0:T(8,128)(2,1)}, u32[]{:S(2)}, u32[]{:S(2)}) collective-permute-start(bf16[2,2,2,64,768]{4,3,2,1,0:T(8,128)(2,1)} %fusion.12), channel_id=1, source_target_pairs={{0,2},{1,3},{2,0},{3,1},{4,6},{5,7},{6,4},{7,5},{8,10},{9,11},{10,... | collective-permute-start | bytes 2359304 | tf_op jit(solution)/shard_map/ppermute | solution.py:27
  209.2 11.2 %collective-permute-start.29 = (bf16[2,2,64,768]{3,2,0,1:T(8,128)(2,1)S(1)}, bf16[2,2,64,768]{3,2,0,1:T(8,128)(2,1)S(1)}, u32[]{:S(2)}, u32[]{:S(2)}) collective-permute-start(bf16[2,2,64,768]{3,2,0,1:T(8,128)(2,1)S(1)} %fusion.35), channel_id=1, source_target_pairs={{0,2},{1,3},{2,0},{3,1},{4,6},{5,7},{6,4},{7,5},{8,10},{9,11},{10,... | collective-permute-start | bytes 1179656 | tf_op jit(solution)/shard_map/ppermute | solution.py:27
  214.3 9.5 %collective-permute-start.24 = (bf16[2,2,64,768]{3,2,1,0:T(8,128)(2,1)S(1)}, bf16[2,2,64,768]{3,2,1,0:T(8,128)(2,1)S(1)}, u32[]{:S(2)}, u32[]{:S(2)}) collective-permute-start(bf16[2,2,64,768]{3,2,1,0:T(8,128)(2,1)S(1)} %fusion.34), channel_id=1, source_target_pairs={{0,8},{1,9},{2,10},{3,11},{4,12},{5,13},{6,14},{7,15},{8,0},{9,1},... | collective-permute-start | bytes 1179656 | tf_op jit(solution)/shard_map/ppermute | solution.py:27
  220.6 7.7 %collective-permute-start.30 = (bf16[2,64,768]{2,1,0:T(8,128)(2,1)S(1)}, bf16[2,64,768]{2,1,0:T(8,128)(2,1)S(1)}, u32[]{:S(2)}, u32[]{:S(2)}) collective-permute-start(bf16[2,64,768]{2,1,0:T(8,128)(2,1)S(1)} %fusion.41), channel_id=1, source_target_pairs={{0,4},{1,5},{2,6},{3,7},{4,0},{5,1},{6,2},{7,3},{8,12},{9,13},{10,... | collective-permute-start | bytes 589832 | tf_op jit(solution)/shard_map/ppermute | solution.py:27
  224.0 7.5 %collective-permute-start.25 = (bf16[2,64,768]{2,1,0:T(8,128)(2,1)S(1)}, bf16[2,64,768]{2,1,0:T(8,128)(2,1)S(1)}, u32[]{:S(2)}, u32[]{:S(2)}) collective-permute-start(bf16[2,64,768]{2,1,0:T(8,128)(2,1)S(1)} %fusion.40), channel_id=1, source_target_pairs={{0,16},{1,17},{2,18},{3,19},{4,20},{5,21},{6,22},{7,23},{8,24},{9,... | collective-permute-start | bytes 589832 | tf_op jit(solution)/shard_map/ppermute | solution.py:27
  (23 other events, 152.4 us)

commit v9 on v8

--- a/solution.py
+++ b/solution.py
@@ -142,7 +142,7 @@
     second_width = second_rows.shape[1]
     model_width = gate_up.shape[1]
     expert_count = gate_up.shape[0]
-    tile = 256
+    tile = 512
     return pl.pallas_call(
         expert_block,
         grid=(row_count // tile,),

time: 241 us -> 240 us (level)
  starting transfers between devices: 47.7 us -> 38.1 us
  waiting for transfers between devices: 107 us -> 113 us
    ppermute x32, starting transfers between devices: 47.7 us -> 38.1 us  [partner(): return lax.ppermute(value, axis, pairs)]
    ppermute x32, waiting for transfers between devices: 107 us -> 113 us  [partner(): return lax.ppermute(value, axis, pairs)]
  transfers between devices with their start and end apart: 32 -> 32, of which waited for: 25 -> 27; matrix products, arithmetic and copies ran while one was open for 14% -> 15% of each run, Pallas kernels for 0% -> 0%
where the time goes in v9:
time: 240 us; the launch traced here: 235 us
  waiting for transfers between devices  113 us (47%)
  starting transfers between devices  38.1 us (16%)
  other arithmetic  27.7 us (12%)
  Pallas kernels  27.1 us (11%)
  local copies, waits for them, and re-layouts  14.7 us (6%)
  loops' own time  7.35 us (3%)
  matrix products  5.44 us (2%)
    ppermute x32, waiting for transfers between devices, partner(): return lax.ppermute(value, axis, pairs)  113 us
    ppermute x32, starting transfers between devices, partner(): return lax.ppermute(value, axis, pairs)  38.1 us
    pallas_call x1, Pallas kernels, dense_experts(): pl.pallas_call(expert_block, grid=(row_count // tile,), in_specs=[pl.Bloc...  27.1 us
    another operation x19, other arithmetic, gather_any(): state = jnp.stack([lower_rows, upper_rows], axis=0)  7.56 us
    another operation x1, loops' own time, on_device(): lax.map(attend, jnp.arange(rows_quarter // block_rows, dtype=jnp.int32))  6.97 us
    unnamed x31, local copies, waits for them, and re-layouts  5.73 us
  transfers between devices with their start and end apart: 32, of which 27 were waited for; matrix products, arithmetic and copies ran while one was open for 15% of the time, Pallas kernels for 0%

profile of v9, /device:TPU:24, one launch (start us, length us, event | category | flops | bytes accessed | tf_op | source)
XLA Modules:
  0.0 235.3 jit_solution(7841046619503130113)
XLA Ops:
  3.6 3.1 %collective-permute-start = (bf16[64,1536]{1,0:T(8,128)(2,1)S(1)}, bf16[64,1536]{1,0:T(8,128)(2,1)S(1)}, u32[]{:S(2)}, u32[]{:S(2)}) collective-permute-start(bf16[64,1536]{1,0:T(8,128)(2,1)S(1)} %fusion.27), channel_id=1, source_target_pairs={{0,4},{1,5},{2,6},{3,7},{4,0},{5,1},{6,2},{7,3},{8,12},{9,13},{10,... | collective-permute-start | bytes 589832 | tf_op jit(solution)/shard_map/ppermute | solution.py:27
  15.2 6.3 %collective-permute-done.1 = bf16[128,1536]{1,0:T(8,128)(2,1)S(1)} collective-permute-done((bf16[128,1536]{1,0:T(8,128)(2,1)S(1)}, bf16[128,1536]{1,0:T(8,128)(2,1)S(1)}, u32[]{:S(2)}, u32[]{:S(2)}) %collective-permute-start.1) | collective-permute-done | bytes 393248 | tf_op jit(solution)/shard_map/ppermute | solution.py:27
  23.4 4.3 %collective-permute-done.4 = bf16[1536,160]{0,1:T(8,128)(2,1)S(1)} collective-permute-done((bf16[1536,160]{0,1:T(8,128)(2,1)S(1)}, bf16[1536,160]{0,1:T(8,128)(2,1)S(1)}, u32[]{:S(2)}, u32[]{:S(2)}) %collective-permute-start.4) | collective-permute-done | bytes 491552 | tf_op jit(solution)/shard_map/ppermute | solution.py:27
  32.6 3.0 %collective-permute-done.5 = bf16[512,128]{0,1:T(8,128)(2,1)S(1)} collective-permute-done((bf16[512,128]{0,1:T(8,128)(2,1)S(1)}, bf16[512,128]{0,1:T(8,128)(2,1)S(1)}, u32[]{:S(2)}, u32[]{:S(2)}) %collective-permute-start.5) | collective-permute-done | bytes 131104 | tf_op jit(solution)/shard_map/ppermute | solution.py:27
  35.7 2.8 %collective-permute-start.6 = (bf16[1024,128]{0,1:T(8,128)(2,1)S(1)}, bf16[1024,128]{0,1:T(8,128)(2,1)S(1)}, u32[]{:S(2)}, u32[]{:S(2)}) collective-permute-start(bf16[1024,128]{0,1:T(8,128)(2,1)S(1)} %maximum_select_fusion.8), channel_id=1, source_target_pairs={{0,16},{1,17},{2,18},{3,19},{4,20},{5,21},{6,22},{7,23},{8,24},{9,... | collective-permute-start | bytes 786440 | tf_op jit(solution)/shard_map/ppermute | solution.py:27
  38.6 6.0 %collective-permute-done.6 = bf16[1024,128]{0,1:T(8,128)(2,1)S(1)} collective-permute-done((bf16[1024,128]{0,1:T(8,128)(2,1)S(1)}, bf16[1024,128]{0,1:T(8,128)(2,1)S(1)}, u32[]{:S(2)}, u32[]{:S(2)}) %collective-permute-start.6) | collective-permute-done | bytes 262176 | tf_op jit(solution)/shard_map/ppermute | solution.py:27
  45.0 18.1 %while.59 = (s32[]{:T(128)}, bf16[2,256,192]{1,2,0:T(8,128)(2,1)S(1)}, s32[2]{0:T(128)S(1)}, s32[]{:T(128)}, s32[2048]{0:T(1024)S(1)}, /*index=5*/bf16[3,512,64]...) while((s32[]{:T(128)}, ...), condition=%wide.region_8.9_spmd, body=%wide.region_3.8_spmd.sunk | while | flops 104007976 | bytes 8950756 | solution.py:293
  49.9 6.1 %while.60 = (s32[]{:T(128)}, f32[768]{0:T(1024)S(1)}, f32[768]{0:T(1024)S(1)}, f32[768,64]{0,1:T(8,128)S(1)}, s32[]{:T(128)}, /*index=5*/s32[256]{0:T(256)S(1)},...) while((s32[]{:T(128)}, f32[768]{0:T(1024)S(1)}, ...), condition=%wide.region_7.7_spmd.clone, body=%wide.region_4.6_spmd.clone.sunk | while | flops 103909632 | bytes 7464147 | solution.py:289
  68.2 10.2 %collective-permute-done.10 = bf16[2,64,1536]{2,1,0:T(8,128)(2,1)S(1)} collective-permute-done((bf16[2,64,1536]{2,1,0:T(8,128)(2,1)S(1)}, bf16[2,64,1536]{2,1,0:T(8,128)(2,1)S(1)}, u32[]{:S(2)}, u32[]{:S(2)}) %collective-permute-start.10) | collective-permute-done | bytes 393248 | tf_op jit(solution)/shard_map/ppermute | solution.py:27
  78.6 2.6 %collective-permute-start.11 = (bf16[64,1536]{1,0:T(8,128)(2,1)S(1)}, bf16[64,1536]{1,0:T(8,128)(2,1)S(1)}, u32[]{:S(2)}, u32[]{:S(2)}) collective-permute-start(bf16[64,1536]{1,0:T(8,128)(2,1)S(1)} %fusion.39), channel_id=1, source_target_pairs={{0,4},{1,5},{2,6},{3,7},{4,0},{5,1},{6,2},{7,3},{8,12},{9,13},{10,... | collective-permute-start | bytes 589832 | tf_op jit(solution)/shard_map/ppermute | solution.py:27
  81.2 5.1 %collective-permute-done.11 = bf16[64,1536]{1,0:T(8,128)(2,1)S(1)} collective-permute-done((bf16[64,1536]{1,0:T(8,128)(2,1)S(1)}, bf16[64,1536]{1,0:T(8,128)(2,1)S(1)}, u32[]{:S(2)}, u32[]{:S(2)}) %collective-permute-start.11) | collective-permute-done | bytes 196640 | tf_op jit(solution)/shard_map/ppermute | solution.py:27
  88.8 4.6 %collective-permute-done.17 = bf16[64,768]{1,0:T(8,128)(2,1)S(1)} collective-permute-done((bf16[64,768]{1,0:T(8,128)(2,1)S(1)}, bf16[64,768]{1,0:T(8,128)(2,1)S(1)}, u32[]{:S(2)}, u32[]{:S(2)}) %collective-permute-start.17) | collective-permute-done | bytes 98336 | tf_op jit(solution)/shard_map/ppermute | solution.py:27
  97.3 3.4 %collective-permute-done.12 = bf16[64,896]{1,0:T(8,128)(2,1)S(1)} collective-permute-done((bf16[64,896]{1,0:T(8,128)(2,1)S(1)}, bf16[64,896]{1,0:T(8,128)(2,1)S(1)}, u32[]{:S(2)}, u32[]{:S(2)}) %collective-permute-start.12) | collective-permute-done | bytes 114720 | tf_op jit(solution)/shard_map/ppermute | solution.py:27
  105.4 5.5 %collective-permute-done.13 = bf16[2,64,896]{2,1,0:T(8,128)(2,1)S(1)} collective-permute-done((bf16[2,64,896]{2,1,0:T(8,128)(2,1)S(1)}, bf16[2,64,896]{2,1,0:T(8,128)(2,1)S(1)}, u32[]{:S(2)}, u32[]{:S(2)}) %collective-permute-start.13) | collective-permute-done | bytes 229408 | tf_op jit(solution)/shard_map/ppermute | solution.py:27
  113.3 10.6 %collective-permute-done.14 = bf16[2,2,64,896]{3,2,1,0:T(8,128)(2,1)S(1)} collective-permute-done((bf16[2,2,64,896]{3,2,1,0:T(8,128)(2,1)S(1)}, bf16[2,2,64,896]{3,2,1,0:T(8,128)(2,1)S(1)}, u32[]{:S(2)}, u32[]{:S(2)}) %collective-permute-start.14) | collective-permute-done | bytes 458784 | tf_op jit(solution)/shard_map/ppermute | solution.py:27
  125.0 7.4 %collective-permute-done.20 = bf16[2,2,2,64,768]{4,3,2,1,0:T(8,128)(2,1)S(1)} collective-permute-done((bf16[2,2,2,64,768]{4,3,2,1,0:T(8,128)(2,1)S(1)}, bf16[2,2,2,64,768]{4,3,2,1,0:T(8,128)(2,1)S(1)}, u32[]{:S(2)}, u32[]{:S(2)}) %collective-permute-start.20) | collective-permute-done | bytes 786464 | tf_op jit(solution)/shard_map/ppermute | solution.py:27
  133.8 3.9 %collective-permute-done.15 = bf16[2,2,2,64,896]{4,3,2,1,0:T(8,128)(2,1)S(1)} collective-permute-done((bf16[2,2,2,64,896]{4,3,2,1,0:T(8,128)(2,1)S(1)}, bf16[2,2,2,64,896]{4,3,2,1,0:T(8,128)(2,1)S(1)}, u32[]{:S(2)}, u32[]{:S(2)}) %collective-permute-start.15) | collective-permute-done | bytes 917536 | tf_op jit(solution)/shard_map/ppermute | solution.py:27
  148.6 27.1 %shard_map.121 = bf16[2048,1536]{1,0:T(8,128)(2,1)} custom-call(bf16[2048,896]{1,0:T(8,128)(2,1)} %bitcast.194, bf16[2048,768]{1,0:T(8,128)(2,1)S(1)} %bitcast.190, f32[2048,5]{1,0:T(8,128)S(1)} %dynamic-slice_convert_fusion.share_ref, bf16[5,1536,256]{2,1,0:T(8,128)(2,1)} %gate_up_ref.1, bf16[5,128,1536]{2,1,0:T(8,128)(2,1)S(1)} %copy-done), custom_call_target="tpu_custom_call" | custom-call | tf_op jit(solution)/shard_map/pallas_call | solution.py:146
  175.6 3.0 %broadcast_select_fusion.2 = (bf16[1024,768]{1,0:T(8,128)(2,1)S(1)}, bf16[1024,768]{1,0:T(8,128)(2,1)S(1)}, bf16[1024,768]{1,0:T(8,128)(2,1)S(1)}, bf16[1024,768]{1,0:T(8,128)(2,1)S(1)}) fusion(pred[]{:T(512)S(6)} %eq.20, bf16[2048,1536]{1,0:T(8,128)(2,1)} %shard_map.121), kind=kLoop, calls=%fused_computation.39 | loop fusion | flops 3145728 | bytes 12582913 | tf_op jit(solution)/shard_map/jit(_where)/select_n | solution.py:99
  179.4 2.9 %collective-permute-done.27 = bf16[2,2,2,2,64,768]{5,4,2,3,0,1:T(8,128)(2,1)S(1)} collective-permute-done((bf16[2,2,2,2,64,768]{5,4,2,3,0,1:T(8,128)(2,1)S(1)}, bf16[2,2,2,2,64,768]{5,4,2,3,0,1:T(8,128)(2,1)S(1)}, u32[]{:S(2)}, u32[]{:S(2)}) %collective-permute-start.27) | collective-permute-done | bytes 1572896 | tf_op jit(solution)/shard_map/ppermute | solution.py:27
  190.0 13.6 %collective-permute-done.28 = bf16[2,2,2,64,768]{4,3,1,2,0:T(8,128)(2,1)} collective-permute-done((bf16[2,2,2,64,768]{4,3,1,2,0:T(8,128)(2,1)}, bf16[2,2,2,64,768]{4,3,1,2,0:T(8,128)(2,1)}, u32[]{:S(2)}, u32[]{:S(2)}) %collective-permute-start.28) | collective-permute-done | bytes 786464 | tf_op jit(solution)/shard_map/ppermute | solution.py:27
  211.0 4.8 %collective-permute-done.29 = bf16[2,2,64,768]{3,2,0,1:T(8,128)(2,1)S(1)} collective-permute-done((bf16[2,2,64,768]{3,2,0,1:T(8,128)(2,1)S(1)}, bf16[2,2,64,768]{3,2,0,1:T(8,128)(2,1)S(1)}, u32[]{:S(2)}, u32[]{:S(2)}) %collective-permute-start.29) | collective-permute-done | bytes 393248 | tf_op jit(solution)/shard_map/ppermute | solution.py:27
  224.8 3.4 %collective-permute-done.25 = bf16[2,64,768]{2,1,0:T(8,128)(2,1)S(1)} collective-permute-done((bf16[2,64,768]{2,1,0:T(8,128)(2,1)S(1)}, bf16[2,64,768]{2,1,0:T(8,128)(2,1)S(1)}, u32[]{:S(2)}, u32[]{:S(2)}) %collective-permute-start.25) | collective-permute-done | bytes 196640 | tf_op jit(solution)/shard_map/ppermute | solution.py:27
  230.7 3.8 %collective-permute-done.26 = bf16[64,768]{1,0:T(8,128)(2,1)S(1)} collective-permute-done((bf16[64,768]{1,0:T(8,128)(2,1)S(1)}, bf16[64,768]{1,0:T(8,128)(2,1)S(1)}, u32[]{:S(2)}, u32[]{:S(2)}) %collective-permute-start.26) | collective-permute-done | bytes 98336 | tf_op jit(solution)/shard_map/ppermute | solution.py:27
  (240 shorter events, 90.5 us)
Async XLA Ops:
  0.6 21.4 %collective-permute-start.7 = (bf16[1536,48]{0,1:T(8,128)(2,1)}, bf16[1536,48]{0,1:T(8,128)(2,1)S(1)}, u32[]{:S(2)}, u32[]{:S(2)}) collective-permute-start(bf16[1536,48]{0,1:T(8,128)(2,1)} %param.20), channel_id=1, source_target_pairs={{0,8},{1,9},{2,10},{3,11},{4,12},{5,13},{6,14},{7,15},{8,0},{9,1},... | collective-permute-start | bytes 442376 | tf_op jit(solution)/shard_map/ppermute | solution.py:27
  3.6 8.0 %collective-permute-start = (bf16[64,1536]{1,0:T(8,128)(2,1)S(1)}, bf16[64,1536]{1,0:T(8,128)(2,1)S(1)}, u32[]{:S(2)}, u32[]{:S(2)}) collective-permute-start(bf16[64,1536]{1,0:T(8,128)(2,1)S(1)} %fusion.27), channel_id=1, source_target_pairs={{0,4},{1,5},{2,6},{3,7},{4,0},{5,1},{6,2},{7,3},{8,12},{9,13},{10,... | collective-permute-start | bytes 589832 | tf_op jit(solution)/shard_map/ppermute | solution.py:27
  6.7 7.3 %collective-permute-start.3 = (bf16[1536,80]{0,1:T(8,128)(2,1)}, bf16[1536,80]{0,1:T(8,128)(2,1)S(1)}, u32[]{:S(2)}, u32[]{:S(2)}) collective-permute-start(bf16[1536,80]{0,1:T(8,128)(2,1)} %param.19), channel_id=1, source_target_pairs={{0,8},{1,9},{2,10},{3,11},{4,12},{5,13},{6,14},{7,15},{8,0},{9,1},... | collective-permute-start | bytes 737288 | tf_op jit(solution)/shard_map/ppermute | solution.py:27
  11.6 9.8 %collective-permute-start.1 = (bf16[128,1536]{1,0:T(8,128)(2,1)S(1)}, bf16[128,1536]{1,0:T(8,128)(2,1)S(1)}, u32[]{:S(2)}, u32[]{:S(2)}) collective-permute-start(bf16[128,1536]{1,0:T(8,128)(2,1)S(1)} %maximum_select_fusion.6), channel_id=1, source_target_pairs={{0,2},{1,3},{2,0},{3,1},{4,6},{5,7},{6,4},{7,5},{8,10},{9,11},{10,... | collective-permute-start | bytes 1179656 | tf_op jit(solution)/shard_map/ppermute | solution.py:27
  14.2 13.6 %collective-permute-start.4 = (bf16[1536,160]{0,1:T(8,128)(2,1)S(1)}, bf16[1536,160]{0,1:T(8,128)(2,1)S(1)}, u32[]{:S(2)}, u32[]{:S(2)}) collective-permute-start(bf16[1536,160]{0,1:T(8,128)(2,1)S(1)} %maximum_select_fusion.5), channel_id=1, source_target_pairs={{0,16},{1,17},{2,18},{3,19},{4,20},{5,21},{6,22},{7,23},{8,24},{9,... | collective-permute-start | bytes 1474568 | tf_op jit(solution)/shard_map/ppermute | solution.py:27
  21.6 6.5 %collective-permute-start.2 = (bf16[256,1536]{1,0:T(8,128)(2,1)S(1)}, bf16[256,1536]{1,0:T(8,128)(2,1)S(1)}, u32[]{:S(2)}, u32[]{:S(2)}) collective-permute-start(bf16[256,1536]{1,0:T(8,128)(2,1)S(1)} %maximum_select_fusion.2), channel_id=1, source_target_pairs={{0,1},{1,0},{2,3},{3,2},{4,5},{5,4},{6,7},{7,6},{8,9},{9,8},{10,11... | collective-permute-start | bytes 2359304 | tf_op jit(solution)/shard_map/ppermute | solution.py:27
  22.1 41.2 %collective-permute-start.8 = (bf16[1536,96]{0,1:T(8,128)(2,1)S(1)}, bf16[1536,96]{0,1:T(8,128)(2,1)S(1)}, u32[]{:S(2)}, u32[]{:S(2)}) collective-permute-start(bf16[1536,96]{0,1:T(8,128)(2,1)S(1)} %maximum_select_fusion.7), channel_id=1, source_target_pairs={{0,16},{1,17},{2,18},{3,19},{4,20},{5,21},{6,22},{7,23},{8,24},{9,... | collective-permute-start | bytes 884744 | tf_op jit(solution)/shard_map/ppermute | solution.py:27
  35.7 8.9 %collective-permute-start.6 = (bf16[1024,128]{0,1:T(8,128)(2,1)S(1)}, bf16[1024,128]{0,1:T(8,128)(2,1)S(1)}, u32[]{:S(2)}, u32[]{:S(2)}) collective-permute-start(bf16[1024,128]{0,1:T(8,128)(2,1)S(1)} %maximum_select_fusion.8), channel_id=1, source_target_pairs={{0,16},{1,17},{2,18},{3,19},{4,20},{5,21},{6,22},{7,23},{8,24},{9,... | collective-permute-start | bytes 786440 | tf_op jit(solution)/shard_map/ppermute | solution.py:27
  67.1 11.2 %collective-permute-start.10 = (bf16[2,64,1536]{2,1,0:T(8,128)(2,1)S(1)}, bf16[2,64,1536]{2,1,0:T(8,128)(2,1)S(1)}, u32[]{:S(2)}, u32[]{:S(2)}) collective-permute-start(bf16[2,64,1536]{2,1,0:T(8,128)(2,1)S(1)} %fusion.33), channel_id=1, source_target_pairs={{0,2},{1,3},{2,0},{3,1},{4,6},{5,7},{6,4},{7,5},{8,10},{9,11},{10,... | collective-permute-start | bytes 1179656 | tf_op jit(solution)/shard_map/ppermute | solution.py:27
  78.6 7.7 %collective-permute-start.11 = (bf16[64,1536]{1,0:T(8,128)(2,1)S(1)}, bf16[64,1536]{1,0:T(8,128)(2,1)S(1)}, u32[]{:S(2)}, u32[]{:S(2)}) collective-permute-start(bf16[64,1536]{1,0:T(8,128)(2,1)S(1)} %fusion.39), channel_id=1, source_target_pairs={{0,4},{1,5},{2,6},{3,7},{4,0},{5,1},{6,2},{7,3},{8,12},{9,13},{10,... | collective-permute-start | bytes 589832 | tf_op jit(solution)/shard_map/ppermute | solution.py:27
  93.5 7.2 %collective-permute-start.12 = (bf16[64,896]{1,0:T(8,128)(2,1)S(1)}, bf16[64,896]{1,0:T(8,128)(2,1)S(1)}, u32[]{:S(2)}, u32[]{:S(2)}) collective-permute-start(bf16[64,896]{1,0:T(8,128)(2,1)S(1)} %maximum_maximum_fusion), channel_id=1, source_target_pairs={{0,4},{1,5},{2,6},{3,7},{4,0},{5,1},{6,2},{7,3},{8,12},{9,13},{10,... | collective-permute-start | bytes 344072 | tf_op jit(solution)/shard_map/ppermute | solution.py:27
  96.2 8.1 %collective-permute-start.18 = (bf16[2,64,768]{2,1,0:T(8,128)(2,1)S(1)}, bf16[2,64,768]{2,1,0:T(8,128)(2,1)S(1)}, u32[]{:S(2)}, u32[]{:S(2)}) collective-permute-start(bf16[2,64,768]{2,1,0:T(8,128)(2,1)S(1)} %pad_maximum_fusion.8), channel_id=1, source_target_pairs={{0,4},{1,5},{2,6},{3,7},{4,0},{5,1},{6,2},{7,3},{8,12},{9,13},{10,... | collective-permute-start | bytes 589832 | tf_op jit(solution)/shard_map/ppermute | solution.py:27
  100.8 10.1 %collective-permute-start.13 = (bf16[2,64,896]{2,1,0:T(8,128)(2,1)S(1)}, bf16[2,64,896]{2,1,0:T(8,128)(2,1)S(1)}, u32[]{:S(2)}, u32[]{:S(2)}) collective-permute-start(bf16[2,64,896]{2,1,0:T(8,128)(2,1)S(1)} %pad_maximum_fusion.7), channel_id=1, source_target_pairs={{0,16},{1,17},{2,18},{3,19},{4,20},{5,21},{6,22},{7,23},{8,24},{9,... | collective-permute-start | bytes 688136 | tf_op jit(solution)/shard_map/ppermute | solution.py:27
  104.3 7.9 %collective-permute-start.19 = (bf16[2,2,64,768]{3,2,1,0:T(8,128)(2,1)S(1)}, bf16[2,2,64,768]{3,2,1,0:T(8,128)(2,1)S(1)}, u32[]{:S(2)}, u32[]{:S(2)}) collective-permute-start(bf16[2,2,64,768]{3,2,1,0:T(8,128)(2,1)S(1)} %pad_maximum_fusion.6), channel_id=1, source_target_pairs={{0,2},{1,3},{2,0},{3,1},{4,6},{5,7},{6,4},{7,5},{8,10},{9,11},{10,... | collective-permute-start | bytes 1179656 | tf_op jit(solution)/shard_map/ppermute | solution.py:27
  111.0 13.0 %collective-permute-start.14 = (bf16[2,2,64,896]{3,2,1,0:T(8,128)(2,1)S(1)}, bf16[2,2,64,896]{3,2,1,0:T(8,128)(2,1)S(1)}, u32[]{:S(2)}, u32[]{:S(2)}) collective-permute-start(bf16[2,2,64,896]{3,2,1,0:T(8,128)(2,1)S(1)} %pad_maximum_fusion.5), channel_id=1, source_target_pairs={{0,8},{1,9},{2,10},{3,11},{4,12},{5,13},{6,14},{7,15},{8,0},{9,1},... | collective-permute-start | bytes 1376264 | tf_op jit(solution)/shard_map/ppermute | solution.py:27
  112.3 20.0 %collective-permute-start.20 = (bf16[2,2,2,64,768]{4,3,2,1,0:T(8,128)(2,1)S(1)}, bf16[2,2,2,64,768]{4,3,2,1,0:T(8,128)(2,1)S(1)}, u32[]{:S(2)}, u32[]{:S(2)}) collective-permute-start(bf16[2,2,2,64,768]{4,3,2,1,0:T(8,128)(2,1)S(1)} %pad_maximum_fusion.4), channel_id=1, source_target_pairs={{0,8},{1,9},{2,10},{3,11},{4,12},{5,13},{6,14},{7,15},{8,0},{9,1},... | collective-permute-start | bytes 2359304 | tf_op jit(solution)/shard_map/ppermute | solution.py:27
  124.2 13.5 %collective-permute-start.15 = (bf16[2,2,2,64,896]{4,3,2,1,0:T(8,128)(2,1)S(1)}, bf16[2,2,2,64,896]{4,3,2,1,0:T(8,128)(2,1)S(1)}, u32[]{:S(2)}, u32[]{:S(2)}) collective-permute-start(bf16[2,2,2,64,896]{4,3,2,1,0:T(8,128)(2,1)S(1)} %pad_maximum_fusion.3), channel_id=1, source_target_pairs={{0,2},{1,3},{2,0},{3,1},{4,6},{5,7},{6,4},{7,5},{8,10},{9,11},{10,... | collective-permute-start | bytes 2752520 | tf_op jit(solution)/shard_map/ppermute | solution.py:27
  183.7 19.9 %collective-permute-start.28 = (bf16[2,2,2,64,768]{4,3,1,2,0:T(8,128)(2,1)}, bf16[2,2,2,64,768]{4,3,1,2,0:T(8,128)(2,1)}, u32[]{:S(2)}, u32[]{:S(2)}) collective-permute-start(bf16[2,2,2,64,768]{4,3,1,2,0:T(8,128)(2,1)} %fusion.13), channel_id=1, source_target_pairs={{0,8},{1,9},{2,10},{3,11},{4,12},{5,13},{6,14},{7,15},{8,0},{9,1},... | collective-permute-start | bytes 2359304 | tf_op jit(solution)/shard_map/ppermute | solution.py:27
  187.6 20.1 %collective-permute-start.23 = (bf16[2,2,2,64,768]{4,3,2,1,0:T(8,128)(2,1)}, bf16[2,2,2,64,768]{4,3,2,1,0:T(8,128)(2,1)}, u32[]{:S(2)}, u32[]{:S(2)}) collective-permute-start(bf16[2,2,2,64,768]{4,3,2,1,0:T(8,128)(2,1)} %fusion.12), channel_id=1, source_target_pairs={{0,2},{1,3},{2,0},{3,1},{4,6},{5,7},{6,4},{7,5},{8,10},{9,11},{10,... | collective-permute-start | bytes 2359304 | tf_op jit(solution)/shard_map/ppermute | solution.py:27
  205.3 10.6 %collective-permute-start.29 = (bf16[2,2,64,768]{3,2,0,1:T(8,128)(2,1)S(1)}, bf16[2,2,64,768]{3,2,0,1:T(8,128)(2,1)S(1)}, u32[]{:S(2)}, u32[]{:S(2)}) collective-permute-start(bf16[2,2,64,768]{3,2,0,1:T(8,128)(2,1)S(1)} %fusion.35), channel_id=1, source_target_pairs={{0,2},{1,3},{2,0},{3,1},{4,6},{5,7},{6,4},{7,5},{8,10},{9,11},{10,... | collective-permute-start | bytes 1179656 | tf_op jit(solution)/shard_map/ppermute | solution.py:27
  209.3 10.7 %collective-permute-start.24 = (bf16[2,2,64,768]{3,2,1,0:T(8,128)(2,1)S(1)}, bf16[2,2,64,768]{3,2,1,0:T(8,128)(2,1)S(1)}, u32[]{:S(2)}, u32[]{:S(2)}) collective-permute-start(bf16[2,2,64,768]{3,2,1,0:T(8,128)(2,1)S(1)} %fusion.34), channel_id=1, source_target_pairs={{0,8},{1,9},{2,10},{3,11},{4,12},{5,13},{6,14},{7,15},{8,0},{9,1},... | collective-permute-start | bytes 1179656 | tf_op jit(solution)/shard_map/ppermute | solution.py:27
  216.0 7.3 %collective-permute-start.30 = (bf16[2,64,768]{2,1,0:T(8,128)(2,1)S(1)}, bf16[2,64,768]{2,1,0:T(8,128)(2,1)S(1)}, u32[]{:S(2)}, u32[]{:S(2)}) collective-permute-start(bf16[2,64,768]{2,1,0:T(8,128)(2,1)S(1)} %fusion.41), channel_id=1, source_target_pairs={{0,4},{1,5},{2,6},{3,7},{4,0},{5,1},{6,2},{7,3},{8,12},{9,13},{10,... | collective-permute-start | bytes 589832 | tf_op jit(solution)/shard_map/ppermute | solution.py:27
  220.2 8.0 %collective-permute-start.25 = (bf16[2,64,768]{2,1,0:T(8,128)(2,1)S(1)}, bf16[2,64,768]{2,1,0:T(8,128)(2,1)S(1)}, u32[]{:S(2)}, u32[]{:S(2)}) collective-permute-start(bf16[2,64,768]{2,1,0:T(8,128)(2,1)S(1)} %fusion.40), channel_id=1, source_target_pairs={{0,16},{1,17},{2,18},{3,19},{4,20},{5,21},{6,22},{7,23},{8,24},{9,... | collective-permute-start | bytes 589832 | tf_op jit(solution)/shard_map/ppermute | solution.py:27
  223.4 7.2 %collective-permute-start.31 = (bf16[64,768]{1,0:T(8,128)(2,1)S(1)}, bf16[64,768]{1,0:T(8,128)(2,1)S(1)}, u32[]{:S(2)}, u32[]{:S(2)}) collective-permute-start(bf16[64,768]{1,0:T(8,128)(2,1)S(1)} %fusion.44), channel_id=1, source_target_pairs={{0,16},{1,17},{2,18},{3,19},{4,20},{5,21},{6,22},{7,23},{8,24},{9,... | collective-permute-start | bytes 294920 | tf_op jit(solution)/shard_map/ppermute | solution.py:27
  (23 other events, 145.2 us)

commit v10 on v9

--- a/solution.py
+++ b/solution.py
@@ -125,15 +125,17 @@
 def expert_block(first_ref, second_ref, share_ref, gate_up_ref, down_ref, out_ref):
     half_width = second_ref.shape[1]
     rows = jnp.concatenate([first_ref[:, :half_width], second_ref[...]], axis=1)
-    inner_width = down_ref.shape[1]
-    total = jnp.zeros(out_ref.shape, jnp.float32)
-    for expert in range(gate_up_ref.shape[0]):
+    expert_count, inner_width, model_width = down_ref.shape
+    scaled = []
+    for expert in range(expert_count):
         both = jnp.dot(rows, gate_up_ref[expert], preferred_element_type=jnp.float32)
         gate_val = both[:, :inner_width]
         up_val = both[:, inner_width:]
-        inner_act = (jax.nn.silu(gate_val) * up_val).astype(jnp.bfloat16)
-        produced = jnp.dot(inner_act, down_ref[expert], preferred_element_type=jnp.float32)
-        total = total + share_ref[:, expert : expert + 1] * produced
+        inner_act = jax.nn.silu(gate_val) * up_val * share_ref[:, expert : expert + 1]
+        scaled.append(inner_act.astype(jnp.bfloat16))
+    joined = jnp.concatenate(scaled, axis=1)
+    down_all = down_ref[...].reshape(expert_count * inner_width, model_width)
+    total = jnp.dot(joined, down_all, preferred_element_type=jnp.float32)
     out_ref[...] = total.astype(out_ref.dtype)
 
 

time: 240 us -> 232 us (0.967)
  Pallas kernels: 27.1 us -> 19.5 us
    pallas_call x1, Pallas kernels: 27.1 us -> 19.5 us  [dense_experts(): pl.pallas_call(expert_block, grid=(row_count // tile,), in_specs=[pl.Bloc...]
where the time goes in v10:
time: 232 us; the launch traced here: 228 us
  waiting for transfers between devices  113 us (49%)
  starting transfers between devices  38.1 us (16%)
  other arithmetic  27.7 us (12%)
  Pallas kernels  19.5 us (8%)
  local copies, waits for them, and re-layouts  14.7 us (6%)
  loops' own time  7.35 us (3%)
  matrix products  5.44 us (2%)
    ppermute x32, waiting for transfers between devices, partner(): return lax.ppermute(value, axis, pairs)  113 us
    ppermute x32, starting transfers between devices, partner(): return lax.ppermute(value, axis, pairs)  38.1 us
    pallas_call x1, Pallas kernels, dense_experts(): pl.pallas_call(expert_block, grid=(row_count // tile,), in_specs=[pl.Bloc...  19.5 us
    another operation x19, other arithmetic, gather_any(): state = jnp.stack([lower_rows, upper_rows], axis=0)  7.56 us
    another operation x1, loops' own time, on_device(): lax.map(attend, jnp.arange(rows_quarter // block_rows, dtype=jnp.int32))  6.97 us
    unnamed x31, local copies, waits for them, and re-layouts  5.73 us
    add x12, other arithmetic, fold_any(): state = kept_rows.astype(jnp.float32) + arrived.astype(jnp.float32)  4.77 us
  transfers between devices with their start and end apart: 32, of which 27 were waited for; matrix products, arithmetic and copies ran while one was open for 15% of the time, Pallas kernels for 0%

profile of v10, /device:TPU:24, one launch (start us, length us, event | category | flops | bytes accessed | tf_op | source)
XLA Modules:
  0.0 227.5 jit_solution(14602111372214832709)
XLA Ops:
  3.6 3.1 %collective-permute-start = (bf16[64,1536]{1,0:T(8,128)(2,1)S(1)}, bf16[64,1536]{1,0:T(8,128)(2,1)S(1)}, u32[]{:S(2)}, u32[]{:S(2)}) collective-permute-start(bf16[64,1536]{1,0:T(8,128)(2,1)S(1)} %fusion.27), channel_id=1, source_target_pairs={{0,4},{1,5},{2,6},{3,7},{4,0},{5,1},{6,2},{7,3},{8,12},{9,13},{10,... | collective-permute-start | bytes 589832 | tf_op jit(solution)/shard_map/ppermute | solution.py:27
  15.2 6.3 %collective-permute-done.1 = bf16[128,1536]{1,0:T(8,128)(2,1)S(1)} collective-permute-done((bf16[128,1536]{1,0:T(8,128)(2,1)S(1)}, bf16[128,1536]{1,0:T(8,128)(2,1)S(1)}, u32[]{:S(2)}, u32[]{:S(2)}) %collective-permute-start.1) | collective-permute-done | bytes 393248 | tf_op jit(solution)/shard_map/ppermute | solution.py:27
  23.4 4.3 %collective-permute-done.4 = bf16[1536,160]{0,1:T(8,128)(2,1)S(1)} collective-permute-done((bf16[1536,160]{0,1:T(8,128)(2,1)S(1)}, bf16[1536,160]{0,1:T(8,128)(2,1)S(1)}, u32[]{:S(2)}, u32[]{:S(2)}) %collective-permute-start.4) | collective-permute-done | bytes 491552 | tf_op jit(solution)/shard_map/ppermute | solution.py:27
  32.6 3.0 %collective-permute-done.5 = bf16[512,128]{0,1:T(8,128)(2,1)S(1)} collective-permute-done((bf16[512,128]{0,1:T(8,128)(2,1)S(1)}, bf16[512,128]{0,1:T(8,128)(2,1)S(1)}, u32[]{:S(2)}, u32[]{:S(2)}) %collective-permute-start.5) | collective-permute-done | bytes 131104 | tf_op jit(solution)/shard_map/ppermute | solution.py:27
  35.7 2.8 %collective-permute-start.6 = (bf16[1024,128]{0,1:T(8,128)(2,1)S(1)}, bf16[1024,128]{0,1:T(8,128)(2,1)S(1)}, u32[]{:S(2)}, u32[]{:S(2)}) collective-permute-start(bf16[1024,128]{0,1:T(8,128)(2,1)S(1)} %maximum_select_fusion.8), channel_id=1, source_target_pairs={{0,16},{1,17},{2,18},{3,19},{4,20},{5,21},{6,22},{7,23},{8,24},{9,... | collective-permute-start | bytes 786440 | tf_op jit(solution)/shard_map/ppermute | solution.py:27
  38.6 6.0 %collective-permute-done.6 = bf16[1024,128]{0,1:T(8,128)(2,1)S(1)} collective-permute-done((bf16[1024,128]{0,1:T(8,128)(2,1)S(1)}, bf16[1024,128]{0,1:T(8,128)(2,1)S(1)}, u32[]{:S(2)}, u32[]{:S(2)}) %collective-permute-start.6) | collective-permute-done | bytes 262176 | tf_op jit(solution)/shard_map/ppermute | solution.py:27
  45.0 18.1 %while.59 = (s32[]{:T(128)}, bf16[2,256,192]{1,2,0:T(8,128)(2,1)S(1)}, s32[2]{0:T(128)S(1)}, s32[]{:T(128)}, s32[2048]{0:T(1024)S(1)}, /*index=5*/bf16[3,512,64]...) while((s32[]{:T(128)}, ...), condition=%wide.region_8.9_spmd, body=%wide.region_3.8_spmd.sunk | while | flops 104007976 | bytes 8950756 | solution.py:295
  49.9 6.1 %while.60 = (s32[]{:T(128)}, f32[768]{0:T(1024)S(1)}, f32[768]{0:T(1024)S(1)}, f32[768,64]{0,1:T(8,128)S(1)}, s32[]{:T(128)}, /*index=5*/s32[256]{0:T(256)S(1)},...) while((s32[]{:T(128)}, f32[768]{0:T(1024)S(1)}, ...), condition=%wide.region_7.7_spmd.clone, body=%wide.region_4.6_spmd.clone.sunk | while | flops 103909632 | bytes 7464147 | solution.py:291
  68.2 10.2 %collective-permute-done.10 = bf16[2,64,1536]{2,1,0:T(8,128)(2,1)S(1)} collective-permute-done((bf16[2,64,1536]{2,1,0:T(8,128)(2,1)S(1)}, bf16[2,64,1536]{2,1,0:T(8,128)(2,1)S(1)}, u32[]{:S(2)}, u32[]{:S(2)}) %collective-permute-start.10) | collective-permute-done | bytes 393248 | tf_op jit(solution)/shard_map/ppermute | solution.py:27
  78.6 2.6 %collective-permute-start.11 = (bf16[64,1536]{1,0:T(8,128)(2,1)S(1)}, bf16[64,1536]{1,0:T(8,128)(2,1)S(1)}, u32[]{:S(2)}, u32[]{:S(2)}) collective-permute-start(bf16[64,1536]{1,0:T(8,128)(2,1)S(1)} %fusion.39), channel_id=1, source_target_pairs={{0,4},{1,5},{2,6},{3,7},{4,0},{5,1},{6,2},{7,3},{8,12},{9,13},{10,... | collective-permute-start | bytes 589832 | tf_op jit(solution)/shard_map/ppermute | solution.py:27
  81.2 5.1 %collective-permute-done.11 = bf16[64,1536]{1,0:T(8,128)(2,1)S(1)} collective-permute-done((bf16[64,1536]{1,0:T(8,128)(2,1)S(1)}, bf16[64,1536]{1,0:T(8,128)(2,1)S(1)}, u32[]{:S(2)}, u32[]{:S(2)}) %collective-permute-start.11) | collective-permute-done | bytes 196640 | tf_op jit(solution)/shard_map/ppermute | solution.py:27
  88.8 4.6 %collective-permute-done.17 = bf16[64,768]{1,0:T(8,128)(2,1)S(1)} collective-permute-done((bf16[64,768]{1,0:T(8,128)(2,1)S(1)}, bf16[64,768]{1,0:T(8,128)(2,1)S(1)}, u32[]{:S(2)}, u32[]{:S(2)}) %collective-permute-start.17) | collective-permute-done | bytes 98336 | tf_op jit(solution)/shard_map/ppermute | solution.py:27
  97.3 3.4 %collective-permute-done.12 = bf16[64,896]{1,0:T(8,128)(2,1)S(1)} collective-permute-done((bf16[64,896]{1,0:T(8,128)(2,1)S(1)}, bf16[64,896]{1,0:T(8,128)(2,1)S(1)}, u32[]{:S(2)}, u32[]{:S(2)}) %collective-permute-start.12) | collective-permute-done | bytes 114720 | tf_op jit(solution)/shard_map/ppermute | solution.py:27
  105.4 5.5 %collective-permute-done.13 = bf16[2,64,896]{2,1,0:T(8,128)(2,1)S(1)} collective-permute-done((bf16[2,64,896]{2,1,0:T(8,128)(2,1)S(1)}, bf16[2,64,896]{2,1,0:T(8,128)(2,1)S(1)}, u32[]{:S(2)}, u32[]{:S(2)}) %collective-permute-start.13) | collective-permute-done | bytes 229408 | tf_op jit(solution)/shard_map/ppermute | solution.py:27
  113.3 10.6 %collective-permute-done.14 = bf16[2,2,64,896]{3,2,1,0:T(8,128)(2,1)S(1)} collective-permute-done((bf16[2,2,64,896]{3,2,1,0:T(8,128)(2,1)S(1)}, bf16[2,2,64,896]{3,2,1,0:T(8,128)(2,1)S(1)}, u32[]{:S(2)}, u32[]{:S(2)}) %collective-permute-start.14) | collective-permute-done | bytes 458784 | tf_op jit(solution)/shard_map/ppermute | solution.py:27
  125.0 7.4 %collective-permute-done.20 = bf16[2,2,2,64,768]{4,3,2,1,0:T(8,128)(2,1)S(1)} collective-permute-done((bf16[2,2,2,64,768]{4,3,2,1,0:T(8,128)(2,1)S(1)}, bf16[2,2,2,64,768]{4,3,2,1,0:T(8,128)(2,1)S(1)}, u32[]{:S(2)}, u32[]{:S(2)}) %collective-permute-start.20) | collective-permute-done | bytes 786464 | tf_op jit(solution)/shard_map/ppermute | solution.py:27
  133.8 3.9 %collective-permute-done.15 = bf16[2,2,2,64,896]{4,3,2,1,0:T(8,128)(2,1)S(1)} collective-permute-done((bf16[2,2,2,64,896]{4,3,2,1,0:T(8,128)(2,1)S(1)}, bf16[2,2,2,64,896]{4,3,2,1,0:T(8,128)(2,1)S(1)}, u32[]{:S(2)}, u32[]{:S(2)}) %collective-permute-start.15) | collective-permute-done | bytes 917536 | tf_op jit(solution)/shard_map/ppermute | solution.py:27
  148.6 19.5 %shard_map.121 = bf16[2048,1536]{1,0:T(8,128)(2,1)} custom-call(bf16[2048,896]{1,0:T(8,128)(2,1)} %bitcast.194, bf16[2048,768]{1,0:T(8,128)(2,1)S(1)} %bitcast.190, f32[2048,5]{1,0:T(8,128)S(1)} %dynamic-slice_convert_fusion.share_ref, bf16[5,1536,256]{2,1,0:T(8,128)(2,1)} %gate_up_ref.1, bf16[5,128,1536]{2,1,0:T(8,128)(2,1)S(1)} %copy-done), custom_call_target="tpu_custom_call" | custom-call | tf_op jit(solution)/shard_map/pallas_call | solution.py:148
  168.1 3.0 %broadcast_select_fusion.2 = (bf16[1024,768]{1,0:T(8,128)(2,1)S(1)}, bf16[1024,768]{1,0:T(8,128)(2,1)S(1)}, bf16[1024,768]{1,0:T(8,128)(2,1)S(1)}, bf16[1024,768]{1,0:T(8,128)(2,1)S(1)}) fusion(pred[]{:T(512)S(6)} %eq.20, bf16[2048,1536]{1,0:T(8,128)(2,1)} %shard_map.121), kind=kLoop, calls=%fused_computation.39 | loop fusion | flops 3145728 | bytes 12582913 | tf_op jit(solution)/shard_map/jit(_where)/select_n | solution.py:99
  171.8 2.9 %collective-permute-done.27 = bf16[2,2,2,2,64,768]{5,4,2,3,0,1:T(8,128)(2,1)S(1)} collective-permute-done((bf16[2,2,2,2,64,768]{5,4,2,3,0,1:T(8,128)(2,1)S(1)}, bf16[2,2,2,2,64,768]{5,4,2,3,0,1:T(8,128)(2,1)S(1)}, u32[]{:S(2)}, u32[]{:S(2)}) %collective-permute-start.27) | collective-permute-done | bytes 1572896 | tf_op jit(solution)/shard_map/ppermute | solution.py:27
  182.5 13.6 %collective-permute-done.28 = bf16[2,2,2,64,768]{4,3,1,2,0:T(8,128)(2,1)} collective-permute-done((bf16[2,2,2,64,768]{4,3,1,2,0:T(8,128)(2,1)}, bf16[2,2,2,64,768]{4,3,1,2,0:T(8,128)(2,1)}, u32[]{:S(2)}, u32[]{:S(2)}) %collective-permute-start.28) | collective-permute-done | bytes 786464 | tf_op jit(solution)/shard_map/ppermute | solution.py:27
  203.2 5.1 %collective-permute-done.29 = bf16[2,2,64,768]{3,2,0,1:T(8,128)(2,1)S(1)} collective-permute-done((bf16[2,2,64,768]{3,2,0,1:T(8,128)(2,1)S(1)}, bf16[2,2,64,768]{3,2,0,1:T(8,128)(2,1)S(1)}, u32[]{:S(2)}, u32[]{:S(2)}) %collective-permute-start.29) | collective-permute-done | bytes 393248 | tf_op jit(solution)/shard_map/ppermute | solution.py:27
  217.2 3.3 %collective-permute-done.25 = bf16[2,64,768]{2,1,0:T(8,128)(2,1)S(1)} collective-permute-done((bf16[2,64,768]{2,1,0:T(8,128)(2,1)S(1)}, bf16[2,64,768]{2,1,0:T(8,128)(2,1)S(1)}, u32[]{:S(2)}, u32[]{:S(2)}) %collective-permute-start.25) | collective-permute-done | bytes 196640 | tf_op jit(solution)/shard_map/ppermute | solution.py:27
  223.1 3.7 %collective-permute-done.26 = bf16[64,768]{1,0:T(8,128)(2,1)S(1)} collective-permute-done((bf16[64,768]{1,0:T(8,128)(2,1)S(1)}, bf16[64,768]{1,0:T(8,128)(2,1)S(1)}, u32[]{:S(2)}, u32[]{:S(2)}) %collective-permute-start.26) | collective-permute-done | bytes 98336 | tf_op jit(solution)/shard_map/ppermute | solution.py:27
  (240 shorter events, 90.4 us)
Async XLA Ops:
  0.6 21.4 %collective-permute-start.7 = (bf16[1536,48]{0,1:T(8,128)(2,1)}, bf16[1536,48]{0,1:T(8,128)(2,1)S(1)}, u32[]{:S(2)}, u32[]{:S(2)}) collective-permute-start(bf16[1536,48]{0,1:T(8,128)(2,1)} %param.20), channel_id=1, source_target_pairs={{0,8},{1,9},{2,10},{3,11},{4,12},{5,13},{6,14},{7,15},{8,0},{9,1},... | collective-permute-start | bytes 442376 | tf_op jit(solution)/shard_map/ppermute | solution.py:27
  3.6 8.0 %collective-permute-start = (bf16[64,1536]{1,0:T(8,128)(2,1)S(1)}, bf16[64,1536]{1,0:T(8,128)(2,1)S(1)}, u32[]{:S(2)}, u32[]{:S(2)}) collective-permute-start(bf16[64,1536]{1,0:T(8,128)(2,1)S(1)} %fusion.27), channel_id=1, source_target_pairs={{0,4},{1,5},{2,6},{3,7},{4,0},{5,1},{6,2},{7,3},{8,12},{9,13},{10,... | collective-permute-start | bytes 589832 | tf_op jit(solution)/shard_map/ppermute | solution.py:27
  6.7 7.3 %collective-permute-start.3 = (bf16[1536,80]{0,1:T(8,128)(2,1)}, bf16[1536,80]{0,1:T(8,128)(2,1)S(1)}, u32[]{:S(2)}, u32[]{:S(2)}) collective-permute-start(bf16[1536,80]{0,1:T(8,128)(2,1)} %param.19), channel_id=1, source_target_pairs={{0,8},{1,9},{2,10},{3,11},{4,12},{5,13},{6,14},{7,15},{8,0},{9,1},... | collective-permute-start | bytes 737288 | tf_op jit(solution)/shard_map/ppermute | solution.py:27
  11.6 9.8 %collective-permute-start.1 = (bf16[128,1536]{1,0:T(8,128)(2,1)S(1)}, bf16[128,1536]{1,0:T(8,128)(2,1)S(1)}, u32[]{:S(2)}, u32[]{:S(2)}) collective-permute-start(bf16[128,1536]{1,0:T(8,128)(2,1)S(1)} %maximum_select_fusion.6), channel_id=1, source_target_pairs={{0,2},{1,3},{2,0},{3,1},{4,6},{5,7},{6,4},{7,5},{8,10},{9,11},{10,... | collective-permute-start | bytes 1179656 | tf_op jit(solution)/shard_map/ppermute | solution.py:27
  14.2 13.6 %collective-permute-start.4 = (bf16[1536,160]{0,1:T(8,128)(2,1)S(1)}, bf16[1536,160]{0,1:T(8,128)(2,1)S(1)}, u32[]{:S(2)}, u32[]{:S(2)}) collective-permute-start(bf16[1536,160]{0,1:T(8,128)(2,1)S(1)} %maximum_select_fusion.5), channel_id=1, source_target_pairs={{0,16},{1,17},{2,18},{3,19},{4,20},{5,21},{6,22},{7,23},{8,24},{9,... | collective-permute-start | bytes 1474568 | tf_op jit(solution)/shard_map/ppermute | solution.py:27
  21.6 6.5 %collective-permute-start.2 = (bf16[256,1536]{1,0:T(8,128)(2,1)S(1)}, bf16[256,1536]{1,0:T(8,128)(2,1)S(1)}, u32[]{:S(2)}, u32[]{:S(2)}) collective-permute-start(bf16[256,1536]{1,0:T(8,128)(2,1)S(1)} %maximum_select_fusion.2), channel_id=1, source_target_pairs={{0,1},{1,0},{2,3},{3,2},{4,5},{5,4},{6,7},{7,6},{8,9},{9,8},{10,11... | collective-permute-start | bytes 2359304 | tf_op jit(solution)/shard_map/ppermute | solution.py:27
  22.1 41.2 %collective-permute-start.8 = (bf16[1536,96]{0,1:T(8,128)(2,1)S(1)}, bf16[1536,96]{0,1:T(8,128)(2,1)S(1)}, u32[]{:S(2)}, u32[]{:S(2)}) collective-permute-start(bf16[1536,96]{0,1:T(8,128)(2,1)S(1)} %maximum_select_fusion.7), channel_id=1, source_target_pairs={{0,16},{1,17},{2,18},{3,19},{4,20},{5,21},{6,22},{7,23},{8,24},{9,... | collective-permute-start | bytes 884744 | tf_op jit(solution)/shard_map/ppermute | solution.py:27
  35.7 8.9 %collective-permute-start.6 = (bf16[1024,128]{0,1:T(8,128)(2,1)S(1)}, bf16[1024,128]{0,1:T(8,128)(2,1)S(1)}, u32[]{:S(2)}, u32[]{:S(2)}) collective-permute-start(bf16[1024,128]{0,1:T(8,128)(2,1)S(1)} %maximum_select_fusion.8), channel_id=1, source_target_pairs={{0,16},{1,17},{2,18},{3,19},{4,20},{5,21},{6,22},{7,23},{8,24},{9,... | collective-permute-start | bytes 786440 | tf_op jit(solution)/shard_map/ppermute | solution.py:27
  67.1 11.2 %collective-permute-start.10 = (bf16[2,64,1536]{2,1,0:T(8,128)(2,1)S(1)}, bf16[2,64,1536]{2,1,0:T(8,128)(2,1)S(1)}, u32[]{:S(2)}, u32[]{:S(2)}) collective-permute-start(bf16[2,64,1536]{2,1,0:T(8,128)(2,1)S(1)} %fusion.33), channel_id=1, source_target_pairs={{0,2},{1,3},{2,0},{3,1},{4,6},{5,7},{6,4},{7,5},{8,10},{9,11},{10,... | collective-permute-start | bytes 1179656 | tf_op jit(solution)/shard_map/ppermute | solution.py:27
  78.6 7.7 %collective-permute-start.11 = (bf16[64,1536]{1,0:T(8,128)(2,1)S(1)}, bf16[64,1536]{1,0:T(8,128)(2,1)S(1)}, u32[]{:S(2)}, u32[]{:S(2)}) collective-permute-start(bf16[64,1536]{1,0:T(8,128)(2,1)S(1)} %fusion.39), channel_id=1, source_target_pairs={{0,4},{1,5},{2,6},{3,7},{4,0},{5,1},{6,2},{7,3},{8,12},{9,13},{10,... | collective-permute-start | bytes 589832 | tf_op jit(solution)/shard_map/ppermute | solution.py:27
  93.5 7.2 %collective-permute-start.12 = (bf16[64,896]{1,0:T(8,128)(2,1)S(1)}, bf16[64,896]{1,0:T(8,128)(2,1)S(1)}, u32[]{:S(2)}, u32[]{:S(2)}) collective-permute-start(bf16[64,896]{1,0:T(8,128)(2,1)S(1)} %maximum_maximum_fusion), channel_id=1, source_target_pairs={{0,4},{1,5},{2,6},{3,7},{4,0},{5,1},{6,2},{7,3},{8,12},{9,13},{10,... | collective-permute-start | bytes 344072 | tf_op jit(solution)/shard_map/ppermute | solution.py:27
  96.2 8.1 %collective-permute-start.18 = (bf16[2,64,768]{2,1,0:T(8,128)(2,1)S(1)}, bf16[2,64,768]{2,1,0:T(8,128)(2,1)S(1)}, u32[]{:S(2)}, u32[]{:S(2)}) collective-permute-start(bf16[2,64,768]{2,1,0:T(8,128)(2,1)S(1)} %pad_maximum_fusion.8), channel_id=1, source_target_pairs={{0,4},{1,5},{2,6},{3,7},{4,0},{5,1},{6,2},{7,3},{8,12},{9,13},{10,... | collective-permute-start | bytes 589832 | tf_op jit(solution)/shard_map/ppermute | solution.py:27
  100.8 10.1 %collective-permute-start.13 = (bf16[2,64,896]{2,1,0:T(8,128)(2,1)S(1)}, bf16[2,64,896]{2,1,0:T(8,128)(2,1)S(1)}, u32[]{:S(2)}, u32[]{:S(2)}) collective-permute-start(bf16[2,64,896]{2,1,0:T(8,128)(2,1)S(1)} %pad_maximum_fusion.7), channel_id=1, source_target_pairs={{0,16},{1,17},{2,18},{3,19},{4,20},{5,21},{6,22},{7,23},{8,24},{9,... | collective-permute-start | bytes 688136 | tf_op jit(solution)/shard_map/ppermute | solution.py:27
  104.3 7.9 %collective-permute-start.19 = (bf16[2,2,64,768]{3,2,1,0:T(8,128)(2,1)S(1)}, bf16[2,2,64,768]{3,2,1,0:T(8,128)(2,1)S(1)}, u32[]{:S(2)}, u32[]{:S(2)}) collective-permute-start(bf16[2,2,64,768]{3,2,1,0:T(8,128)(2,1)S(1)} %pad_maximum_fusion.6), channel_id=1, source_target_pairs={{0,2},{1,3},{2,0},{3,1},{4,6},{5,7},{6,4},{7,5},{8,10},{9,11},{10,... | collective-permute-start | bytes 1179656 | tf_op jit(solution)/shard_map/ppermute | solution.py:27
  111.0 13.0 %collective-permute-start.14 = (bf16[2,2,64,896]{3,2,1,0:T(8,128)(2,1)S(1)}, bf16[2,2,64,896]{3,2,1,0:T(8,128)(2,1)S(1)}, u32[]{:S(2)}, u32[]{:S(2)}) collective-permute-start(bf16[2,2,64,896]{3,2,1,0:T(8,128)(2,1)S(1)} %pad_maximum_fusion.5), channel_id=1, source_target_pairs={{0,8},{1,9},{2,10},{3,11},{4,12},{5,13},{6,14},{7,15},{8,0},{9,1},... | collective-permute-start | bytes 1376264 | tf_op jit(solution)/shard_map/ppermute | solution.py:27
  112.3 20.0 %collective-permute-start.20 = (bf16[2,2,2,64,768]{4,3,2,1,0:T(8,128)(2,1)S(1)}, bf16[2,2,2,64,768]{4,3,2,1,0:T(8,128)(2,1)S(1)}, u32[]{:S(2)}, u32[]{:S(2)}) collective-permute-start(bf16[2,2,2,64,768]{4,3,2,1,0:T(8,128)(2,1)S(1)} %pad_maximum_fusion.4), channel_id=1, source_target_pairs={{0,8},{1,9},{2,10},{3,11},{4,12},{5,13},{6,14},{7,15},{8,0},{9,1},... | collective-permute-start | bytes 2359304 | tf_op jit(solution)/shard_map/ppermute | solution.py:27
  124.2 13.5 %collective-permute-start.15 = (bf16[2,2,2,64,896]{4,3,2,1,0:T(8,128)(2,1)S(1)}, bf16[2,2,2,64,896]{4,3,2,1,0:T(8,128)(2,1)S(1)}, u32[]{:S(2)}, u32[]{:S(2)}) collective-permute-start(bf16[2,2,2,64,896]{4,3,2,1,0:T(8,128)(2,1)S(1)} %pad_maximum_fusion.3), channel_id=1, source_target_pairs={{0,2},{1,3},{2,0},{3,1},{4,6},{5,7},{6,4},{7,5},{8,10},{9,11},{10,... | collective-permute-start | bytes 2752520 | tf_op jit(solution)/shard_map/ppermute | solution.py:27
  176.1 19.9 %collective-permute-start.28 = (bf16[2,2,2,64,768]{4,3,1,2,0:T(8,128)(2,1)}, bf16[2,2,2,64,768]{4,3,1,2,0:T(8,128)(2,1)}, u32[]{:S(2)}, u32[]{:S(2)}) collective-permute-start(bf16[2,2,2,64,768]{4,3,1,2,0:T(8,128)(2,1)} %fusion.13), channel_id=1, source_target_pairs={{0,8},{1,9},{2,10},{3,11},{4,12},{5,13},{6,14},{7,15},{8,0},{9,1},... | collective-permute-start | bytes 2359304 | tf_op jit(solution)/shard_map/ppermute | solution.py:27
  180.1 20.1 %collective-permute-start.23 = (bf16[2,2,2,64,768]{4,3,2,1,0:T(8,128)(2,1)}, bf16[2,2,2,64,768]{4,3,2,1,0:T(8,128)(2,1)}, u32[]{:S(2)}, u32[]{:S(2)}) collective-permute-start(bf16[2,2,2,64,768]{4,3,2,1,0:T(8,128)(2,1)} %fusion.12), channel_id=1, source_target_pairs={{0,2},{1,3},{2,0},{3,1},{4,6},{5,7},{6,4},{7,5},{8,10},{9,11},{10,... | collective-permute-start | bytes 2359304 | tf_op jit(solution)/shard_map/ppermute | solution.py:27
  197.7 10.6 %collective-permute-start.29 = (bf16[2,2,64,768]{3,2,0,1:T(8,128)(2,1)S(1)}, bf16[2,2,64,768]{3,2,0,1:T(8,128)(2,1)S(1)}, u32[]{:S(2)}, u32[]{:S(2)}) collective-permute-start(bf16[2,2,64,768]{3,2,0,1:T(8,128)(2,1)S(1)} %fusion.35), channel_id=1, source_target_pairs={{0,2},{1,3},{2,0},{3,1},{4,6},{5,7},{6,4},{7,5},{8,10},{9,11},{10,... | collective-permute-start | bytes 1179656 | tf_op jit(solution)/shard_map/ppermute | solution.py:27
  201.7 10.3 %collective-permute-start.24 = (bf16[2,2,64,768]{3,2,1,0:T(8,128)(2,1)S(1)}, bf16[2,2,64,768]{3,2,1,0:T(8,128)(2,1)S(1)}, u32[]{:S(2)}, u32[]{:S(2)}) collective-permute-start(bf16[2,2,64,768]{3,2,1,0:T(8,128)(2,1)S(1)} %fusion.34), channel_id=1, source_target_pairs={{0,8},{1,9},{2,10},{3,11},{4,12},{5,13},{6,14},{7,15},{8,0},{9,1},... | collective-permute-start | bytes 1179656 | tf_op jit(solution)/shard_map/ppermute | solution.py:27
  208.4 7.3 %collective-permute-start.30 = (bf16[2,64,768]{2,1,0:T(8,128)(2,1)S(1)}, bf16[2,64,768]{2,1,0:T(8,128)(2,1)S(1)}, u32[]{:S(2)}, u32[]{:S(2)}) collective-permute-start(bf16[2,64,768]{2,1,0:T(8,128)(2,1)S(1)} %fusion.41), channel_id=1, source_target_pairs={{0,4},{1,5},{2,6},{3,7},{4,0},{5,1},{6,2},{7,3},{8,12},{9,13},{10,... | collective-permute-start | bytes 589832 | tf_op jit(solution)/shard_map/ppermute | solution.py:27
  212.2 8.3 %collective-permute-start.25 = (bf16[2,64,768]{2,1,0:T(8,128)(2,1)S(1)}, bf16[2,64,768]{2,1,0:T(8,128)(2,1)S(1)}, u32[]{:S(2)}, u32[]{:S(2)}) collective-permute-start(bf16[2,64,768]{2,1,0:T(8,128)(2,1)S(1)} %fusion.40), channel_id=1, source_target_pairs={{0,16},{1,17},{2,18},{3,19},{4,20},{5,21},{6,22},{7,23},{8,24},{9,... | collective-permute-start | bytes 589832 | tf_op jit(solution)/shard_map/ppermute | solution.py:27
  215.8 7.2 %collective-permute-start.31 = (bf16[64,768]{1,0:T(8,128)(2,1)S(1)}, bf16[64,768]{1,0:T(8,128)(2,1)S(1)}, u32[]{:S(2)}, u32[]{:S(2)}) collective-permute-start(bf16[64,768]{1,0:T(8,128)(2,1)S(1)} %fusion.44), channel_id=1, source_target_pairs={{0,16},{1,17},{2,18},{3,19},{4,20},{5,21},{6,22},{7,23},{8,24},{9,... | collective-permute-start | bytes 294920 | tf_op jit(solution)/shard_map/ppermute | solution.py:27
  (23 other events, 145.0 us)

commit v11 on v10

--- a/solution.py
+++ b/solution.py
@@ -144,7 +144,7 @@
     second_width = second_rows.shape[1]
     model_width = gate_up.shape[1]
     expert_count = gate_up.shape[0]
-    tile = 512
+    tile = 1024
     return pl.pallas_call(
         expert_block,
         grid=(row_count // tile,),

time: 232 us -> 232 us (level); the launches traced: 228 us -> 232 us
  starting transfers between devices: 38.1 us -> 34.1 us
  waiting for transfers between devices: 113 us -> 117 us
    ppermute x32, waiting for transfers between devices: 113 us -> 117 us  [partner(): return lax.ppermute(value, axis, pairs)]
    ppermute x32, starting transfers between devices: 38.1 us -> 34.1 us  [partner(): return lax.ppermute(value, axis, pairs)]
  transfers between devices with their start and end apart: 32 -> 32, of which waited for: 27 -> 27; matrix products, arithmetic and copies ran while one was open for 15% -> 17% of each run, Pallas kernels for 0% -> 0%
where the time goes in v11:
time: 232 us
  waiting for transfers between devices  117 us (50%)
  starting transfers between devices  34.1 us (15%)
  other arithmetic  28.6 us (12%)
  Pallas kernels  19.6 us (8%)
  local copies, waits for them, and re-layouts  15.8 us (7%)
  loops' own time  7.53 us (3%)
  matrix products  7.21 us (3%)
    ppermute x32, waiting for transfers between devices, partner(): return lax.ppermute(value, axis, pairs)  117 us
    ppermute x32, starting transfers between devices, partner(): return lax.ppermute(value, axis, pairs)  34.1 us
    pallas_call x1, Pallas kernels, dense_experts(): pl.pallas_call(expert_block, grid=(row_count // tile,), in_specs=[pl.Bloc...  19.6 us
    another operation x19, other arithmetic, gather_any(): state = jnp.stack([lower_rows, upper_rows], axis=0)  7.56 us
    another operation x1, loops' own time, on_device(): lax.map(attend, jnp.arange(rows_quarter // block_rows, dtype=jnp.int32))  6.97 us
    unnamed x31, local copies, waits for them, and re-layouts  5.73 us
    add x12, other arithmetic, fold_any(): state = kept_rows.astype(jnp.float32) + arrived.astype(jnp.float32)  4.77 us
  transfers between devices with their start and end apart: 32, of which 27 were waited for; matrix products, arithmetic and copies ran while one was open for 17% of the time, Pallas kernels for 0%

profile of v11, /device:TPU:24, one launch (start us, length us, event | category | flops | bytes accessed | tf_op | source)
XLA Modules:
  0.0 231.8 jit_solution(11717982133296259196)
XLA Ops:
  3.6 3.1 %collective-permute-start = (bf16[64,1536]{1,0:T(8,128)(2,1)S(1)}, bf16[64,1536]{1,0:T(8,128)(2,1)S(1)}, u32[]{:S(2)}, u32[]{:S(2)}) collective-permute-start(bf16[64,1536]{1,0:T(8,128)(2,1)S(1)} %fusion.27), channel_id=1, source_target_pairs={{0,4},{1,5},{2,6},{3,7},{4,0},{5,1},{6,2},{7,3},{8,12},{9,13},{10,... | collective-permute-start | bytes 589832 | tf_op jit(solution)/shard_map/ppermute | solution.py:27
  15.2 6.3 %collective-permute-done.1 = bf16[128,1536]{1,0:T(8,128)(2,1)S(1)} collective-permute-done((bf16[128,1536]{1,0:T(8,128)(2,1)S(1)}, bf16[128,1536]{1,0:T(8,128)(2,1)S(1)}, u32[]{:S(2)}, u32[]{:S(2)}) %collective-permute-start.1) | collective-permute-done | bytes 393248 | tf_op jit(solution)/shard_map/ppermute | solution.py:27
  23.4 4.3 %collective-permute-done.4 = bf16[1536,160]{0,1:T(8,128)(2,1)S(1)} collective-permute-done((bf16[1536,160]{0,1:T(8,128)(2,1)S(1)}, bf16[1536,160]{0,1:T(8,128)(2,1)S(1)}, u32[]{:S(2)}, u32[]{:S(2)}) %collective-permute-start.4) | collective-permute-done | bytes 491552 | tf_op jit(solution)/shard_map/ppermute | solution.py:27
  32.6 3.0 %collective-permute-done.5 = bf16[512,128]{0,1:T(8,128)(2,1)S(1)} collective-permute-done((bf16[512,128]{0,1:T(8,128)(2,1)S(1)}, bf16[512,128]{0,1:T(8,128)(2,1)S(1)}, u32[]{:S(2)}, u32[]{:S(2)}) %collective-permute-start.5) | collective-permute-done | bytes 131104 | tf_op jit(solution)/shard_map/ppermute | solution.py:27
  38.6 6.0 %collective-permute-done.6 = bf16[1024,128]{0,1:T(8,128)(2,1)S(1)} collective-permute-done((bf16[1024,128]{0,1:T(8,128)(2,1)S(1)}, bf16[1024,128]{0,1:T(8,128)(2,1)S(1)}, u32[]{:S(2)}, u32[]{:S(2)}) %collective-permute-start.6) | collective-permute-done | bytes 262176 | tf_op jit(solution)/shard_map/ppermute | solution.py:27
  45.0 22.2 %while.59 = (s32[]{:T(128)}, bf16[2,256,192]{1,2,0:T(8,128)(2,1)S(1)}, s32[2]{0:T(128)S(1)}, s32[]{:T(128)}, s32[2048]{0:T(1024)S(1)}, /*index=5*/bf16[3,512,64]...) while((s32[]{:T(128)}, ...), condition=%wide.region_8.9_spmd, body=%wide.region_3.8_spmd.sunk | while | flops 104007976 | bytes 8950756 | solution.py:295
  49.9 6.1 %while.60 = (s32[]{:T(128)}, f32[768]{0:T(1024)S(1)}, f32[768]{0:T(1024)S(1)}, f32[768,64]{0,1:T(8,128)S(1)}, s32[]{:T(128)}, /*index=5*/s32[256]{0:T(256)S(1)},...) while((s32[]{:T(128)}, f32[768]{0:T(1024)S(1)}, ...), condition=%wide.region_7.7_spmd.clone, body=%wide.region_4.6_spmd.clone.sunk | while | flops 103909632 | bytes 7464147 | solution.py:291
  61.0 6.1 %while.60 = (s32[]{:T(128)}, f32[768]{0:T(1024)S(1)}, f32[768]{0:T(1024)S(1)}, f32[768,64]{0,1:T(8,128)S(1)}, s32[]{:T(128)}, /*index=5*/s32[256]{0:T(256)S(1)},...) while((s32[]{:T(128)}, f32[768]{0:T(1024)S(1)}, ...), condition=%wide.region_7.7_spmd.clone, body=%wide.region_4.6_spmd.clone.sunk | while | flops 103909632 | bytes 7464147 | solution.py:291
  72.2 10.2 %collective-permute-done.10 = bf16[2,64,1536]{2,1,0:T(8,128)(2,1)S(1)} collective-permute-done((bf16[2,64,1536]{2,1,0:T(8,128)(2,1)S(1)}, bf16[2,64,1536]{2,1,0:T(8,128)(2,1)S(1)}, u32[]{:S(2)}, u32[]{:S(2)}) %collective-permute-start.10) | collective-permute-done | bytes 393248 | tf_op jit(solution)/shard_map/ppermute | solution.py:27
  85.2 5.1 %collective-permute-done.11 = bf16[64,1536]{1,0:T(8,128)(2,1)S(1)} collective-permute-done((bf16[64,1536]{1,0:T(8,128)(2,1)S(1)}, bf16[64,1536]{1,0:T(8,128)(2,1)S(1)}, u32[]{:S(2)}, u32[]{:S(2)}) %collective-permute-start.11) | collective-permute-done | bytes 196640 | tf_op jit(solution)/shard_map/ppermute | solution.py:27
  91.7 5.8 %collective-permute-done.17 = bf16[64,768]{1,0:T(8,128)(2,1)S(1)} collective-permute-done((bf16[64,768]{1,0:T(8,128)(2,1)S(1)}, bf16[64,768]{1,0:T(8,128)(2,1)S(1)}, u32[]{:S(2)}, u32[]{:S(2)}) %collective-permute-start.17) | collective-permute-done | bytes 98336 | tf_op jit(solution)/shard_map/ppermute | solution.py:27
  101.3 3.4 %collective-permute-done.12 = bf16[64,896]{1,0:T(8,128)(2,1)S(1)} collective-permute-done((bf16[64,896]{1,0:T(8,128)(2,1)S(1)}, bf16[64,896]{1,0:T(8,128)(2,1)S(1)}, u32[]{:S(2)}, u32[]{:S(2)}) %collective-permute-start.12) | collective-permute-done | bytes 114720 | tf_op jit(solution)/shard_map/ppermute | solution.py:27
  105.2 3.1 %collective-permute-done.18 = bf16[2,64,768]{2,1,0:T(8,128)(2,1)S(1)} collective-permute-done((bf16[2,64,768]{2,1,0:T(8,128)(2,1)S(1)}, bf16[2,64,768]{2,1,0:T(8,128)(2,1)S(1)}, u32[]{:S(2)}, u32[]{:S(2)}) %collective-permute-start.18) | collective-permute-done | bytes 196640 | tf_op jit(solution)/shard_map/ppermute | solution.py:27
  109.4 5.5 %collective-permute-done.13 = bf16[2,64,896]{2,1,0:T(8,128)(2,1)S(1)} collective-permute-done((bf16[2,64,896]{2,1,0:T(8,128)(2,1)S(1)}, bf16[2,64,896]{2,1,0:T(8,128)(2,1)S(1)}, u32[]{:S(2)}, u32[]{:S(2)}) %collective-permute-start.13) | collective-permute-done | bytes 229408 | tf_op jit(solution)/shard_map/ppermute | solution.py:27
  117.3 10.6 %collective-permute-done.14 = bf16[2,2,64,896]{3,2,1,0:T(8,128)(2,1)S(1)} collective-permute-done((bf16[2,2,64,896]{3,2,1,0:T(8,128)(2,1)S(1)}, bf16[2,2,64,896]{3,2,1,0:T(8,128)(2,1)S(1)}, u32[]{:S(2)}, u32[]{:S(2)}) %collective-permute-start.14) | collective-permute-done | bytes 458784 | tf_op jit(solution)/shard_map/ppermute | solution.py:27
  129.0 7.4 %collective-permute-done.20 = bf16[2,2,2,64,768]{4,3,2,1,0:T(8,128)(2,1)S(1)} collective-permute-done((bf16[2,2,2,64,768]{4,3,2,1,0:T(8,128)(2,1)S(1)}, bf16[2,2,2,64,768]{4,3,2,1,0:T(8,128)(2,1)S(1)}, u32[]{:S(2)}, u32[]{:S(2)}) %collective-permute-start.20) | collective-permute-done | bytes 786464 | tf_op jit(solution)/shard_map/ppermute | solution.py:27
  137.8 3.9 %collective-permute-done.15 = bf16[2,2,2,64,896]{4,3,2,1,0:T(8,128)(2,1)S(1)} collective-permute-done((bf16[2,2,2,64,896]{4,3,2,1,0:T(8,128)(2,1)S(1)}, bf16[2,2,2,64,896]{4,3,2,1,0:T(8,128)(2,1)S(1)}, u32[]{:S(2)}, u32[]{:S(2)}) %collective-permute-start.15) | collective-permute-done | bytes 917536 | tf_op jit(solution)/shard_map/ppermute | solution.py:27
  152.6 19.6 %shard_map.121 = bf16[2048,1536]{1,0:T(8,128)(2,1)} custom-call(bf16[2048,896]{1,0:T(8,128)(2,1)} %bitcast.194, bf16[2048,768]{1,0:T(8,128)(2,1)S(1)} %bitcast.190, f32[2048,5]{1,0:T(8,128)S(1)} %dynamic-slice_convert_fusion.share_ref, bf16[5,1536,256]{2,1,0:T(8,128)(2,1)} %gate_up_ref.1, bf16[5,128,1536]{2,1,0:T(8,128)(2,1)S(1)} %copy-done), custom_call_target="tpu_custom_call" | custom-call | tf_op jit(solution)/shard_map/pallas_call | solution.py:148
  172.2 3.0 %broadcast_select_fusion.2 = (bf16[1024,768]{1,0:T(8,128)(2,1)S(1)}, bf16[1024,768]{1,0:T(8,128)(2,1)S(1)}, bf16[1024,768]{1,0:T(8,128)(2,1)S(1)}, bf16[1024,768]{1,0:T(8,128)(2,1)S(1)}) fusion(pred[]{:T(512)S(6)} %eq.20, bf16[2048,1536]{1,0:T(8,128)(2,1)} %shard_map.121), kind=kLoop, calls=%fused_computation.39 | loop fusion | flops 3145728 | bytes 12582913 | tf_op jit(solution)/shard_map/jit(_where)/select_n | solution.py:99
  186.6 13.6 %collective-permute-done.28 = bf16[2,2,2,64,768]{4,3,1,2,0:T(8,128)(2,1)} collective-permute-done((bf16[2,2,2,64,768]{4,3,1,2,0:T(8,128)(2,1)}, bf16[2,2,2,64,768]{4,3,1,2,0:T(8,128)(2,1)}, u32[]{:S(2)}, u32[]{:S(2)}) %collective-permute-start.28) | collective-permute-done | bytes 786464 | tf_op jit(solution)/shard_map/ppermute | solution.py:27
  207.6 4.8 %collective-permute-done.29 = bf16[2,2,64,768]{3,2,0,1:T(8,128)(2,1)S(1)} collective-permute-done((bf16[2,2,64,768]{3,2,0,1:T(8,128)(2,1)S(1)}, bf16[2,2,64,768]{3,2,0,1:T(8,128)(2,1)S(1)}, u32[]{:S(2)}, u32[]{:S(2)}) %collective-permute-start.29) | collective-permute-done | bytes 393248 | tf_op jit(solution)/shard_map/ppermute | solution.py:27
  216.9 2.9 %collective-permute-done.30 = bf16[2,64,768]{2,1,0:T(8,128)(2,1)S(1)} collective-permute-done((bf16[2,64,768]{2,1,0:T(8,128)(2,1)S(1)}, bf16[2,64,768]{2,1,0:T(8,128)(2,1)S(1)}, u32[]{:S(2)}, u32[]{:S(2)}) %collective-permute-start.30) | collective-permute-done | bytes 196640 | tf_op jit(solution)/shard_map/ppermute | solution.py:27
  220.6 4.1 %collective-permute-done.25 = bf16[2,64,768]{2,1,0:T(8,128)(2,1)S(1)} collective-permute-done((bf16[2,64,768]{2,1,0:T(8,128)(2,1)S(1)}, bf16[2,64,768]{2,1,0:T(8,128)(2,1)S(1)}, u32[]{:S(2)}, u32[]{:S(2)}) %collective-permute-start.25) | collective-permute-done | bytes 196640 | tf_op jit(solution)/shard_map/ppermute | solution.py:27
  227.2 3.8 %collective-permute-done.26 = bf16[64,768]{1,0:T(8,128)(2,1)S(1)} collective-permute-done((bf16[64,768]{1,0:T(8,128)(2,1)S(1)}, bf16[64,768]{1,0:T(8,128)(2,1)S(1)}, u32[]{:S(2)}, u32[]{:S(2)}) %collective-permute-start.26) | collective-permute-done | bytes 98336 | tf_op jit(solution)/shard_map/ppermute | solution.py:27
  (262 shorter events, 92.6 us)
Async XLA Ops:
  0.6 21.4 %collective-permute-start.7 = (bf16[1536,48]{0,1:T(8,128)(2,1)}, bf16[1536,48]{0,1:T(8,128)(2,1)S(1)}, u32[]{:S(2)}, u32[]{:S(2)}) collective-permute-start(bf16[1536,48]{0,1:T(8,128)(2,1)} %param.20), channel_id=1, source_target_pairs={{0,8},{1,9},{2,10},{3,11},{4,12},{5,13},{6,14},{7,15},{8,0},{9,1},... | collective-permute-start | bytes 442376 | tf_op jit(solution)/shard_map/ppermute | solution.py:27
  3.6 8.0 %collective-permute-start = (bf16[64,1536]{1,0:T(8,128)(2,1)S(1)}, bf16[64,1536]{1,0:T(8,128)(2,1)S(1)}, u32[]{:S(2)}, u32[]{:S(2)}) collective-permute-start(bf16[64,1536]{1,0:T(8,128)(2,1)S(1)} %fusion.27), channel_id=1, source_target_pairs={{0,4},{1,5},{2,6},{3,7},{4,0},{5,1},{6,2},{7,3},{8,12},{9,13},{10,... | collective-permute-start | bytes 589832 | tf_op jit(solution)/shard_map/ppermute | solution.py:27
  6.7 7.3 %collective-permute-start.3 = (bf16[1536,80]{0,1:T(8,128)(2,1)}, bf16[1536,80]{0,1:T(8,128)(2,1)S(1)}, u32[]{:S(2)}, u32[]{:S(2)}) collective-permute-start(bf16[1536,80]{0,1:T(8,128)(2,1)} %param.19), channel_id=1, source_target_pairs={{0,8},{1,9},{2,10},{3,11},{4,12},{5,13},{6,14},{7,15},{8,0},{9,1},... | collective-permute-start | bytes 737288 | tf_op jit(solution)/shard_map/ppermute | solution.py:27
  11.6 9.8 %collective-permute-start.1 = (bf16[128,1536]{1,0:T(8,128)(2,1)S(1)}, bf16[128,1536]{1,0:T(8,128)(2,1)S(1)}, u32[]{:S(2)}, u32[]{:S(2)}) collective-permute-start(bf16[128,1536]{1,0:T(8,128)(2,1)S(1)} %maximum_select_fusion.6), channel_id=1, source_target_pairs={{0,2},{1,3},{2,0},{3,1},{4,6},{5,7},{6,4},{7,5},{8,10},{9,11},{10,... | collective-permute-start | bytes 1179656 | tf_op jit(solution)/shard_map/ppermute | solution.py:27
  14.2 13.6 %collective-permute-start.4 = (bf16[1536,160]{0,1:T(8,128)(2,1)S(1)}, bf16[1536,160]{0,1:T(8,128)(2,1)S(1)}, u32[]{:S(2)}, u32[]{:S(2)}) collective-permute-start(bf16[1536,160]{0,1:T(8,128)(2,1)S(1)} %maximum_select_fusion.5), channel_id=1, source_target_pairs={{0,16},{1,17},{2,18},{3,19},{4,20},{5,21},{6,22},{7,23},{8,24},{9,... | collective-permute-start | bytes 1474568 | tf_op jit(solution)/shard_map/ppermute | solution.py:27
  21.6 6.5 %collective-permute-start.2 = (bf16[256,1536]{1,0:T(8,128)(2,1)S(1)}, bf16[256,1536]{1,0:T(8,128)(2,1)S(1)}, u32[]{:S(2)}, u32[]{:S(2)}) collective-permute-start(bf16[256,1536]{1,0:T(8,128)(2,1)S(1)} %maximum_select_fusion.2), channel_id=1, source_target_pairs={{0,1},{1,0},{2,3},{3,2},{4,5},{5,4},{6,7},{7,6},{8,9},{9,8},{10,11... | collective-permute-start | bytes 2359304 | tf_op jit(solution)/shard_map/ppermute | solution.py:27
  22.1 45.2 %collective-permute-start.8 = (bf16[1536,96]{0,1:T(8,128)(2,1)S(1)}, bf16[1536,96]{0,1:T(8,128)(2,1)S(1)}, u32[]{:S(2)}, u32[]{:S(2)}) collective-permute-start(bf16[1536,96]{0,1:T(8,128)(2,1)S(1)} %maximum_select_fusion.7), channel_id=1, source_target_pairs={{0,16},{1,17},{2,18},{3,19},{4,20},{5,21},{6,22},{7,23},{8,24},{9,... | collective-permute-start | bytes 884744 | tf_op jit(solution)/shard_map/ppermute | solution.py:27
  35.7 8.9 %collective-permute-start.6 = (bf16[1024,128]{0,1:T(8,128)(2,1)S(1)}, bf16[1024,128]{0,1:T(8,128)(2,1)S(1)}, u32[]{:S(2)}, u32[]{:S(2)}) collective-permute-start(bf16[1024,128]{0,1:T(8,128)(2,1)S(1)} %maximum_select_fusion.8), channel_id=1, source_target_pairs={{0,16},{1,17},{2,18},{3,19},{4,20},{5,21},{6,22},{7,23},{8,24},{9,... | collective-permute-start | bytes 786440 | tf_op jit(solution)/shard_map/ppermute | solution.py:27
  71.1 11.2 %collective-permute-start.10 = (bf16[2,64,1536]{2,1,0:T(8,128)(2,1)S(1)}, bf16[2,64,1536]{2,1,0:T(8,128)(2,1)S(1)}, u32[]{:S(2)}, u32[]{:S(2)}) collective-permute-start(bf16[2,64,1536]{2,1,0:T(8,128)(2,1)S(1)} %fusion.33), channel_id=1, source_target_pairs={{0,2},{1,3},{2,0},{3,1},{4,6},{5,7},{6,4},{7,5},{8,10},{9,11},{10,... | collective-permute-start | bytes 1179656 | tf_op jit(solution)/shard_map/ppermute | solution.py:27
  82.6 7.7 %collective-permute-start.11 = (bf16[64,1536]{1,0:T(8,128)(2,1)S(1)}, bf16[64,1536]{1,0:T(8,128)(2,1)S(1)}, u32[]{:S(2)}, u32[]{:S(2)}) collective-permute-start(bf16[64,1536]{1,0:T(8,128)(2,1)S(1)} %fusion.39), channel_id=1, source_target_pairs={{0,4},{1,5},{2,6},{3,7},{4,0},{5,1},{6,2},{7,3},{8,12},{9,13},{10,... | collective-permute-start | bytes 589832 | tf_op jit(solution)/shard_map/ppermute | solution.py:27
  97.6 7.2 %collective-permute-start.12 = (bf16[64,896]{1,0:T(8,128)(2,1)S(1)}, bf16[64,896]{1,0:T(8,128)(2,1)S(1)}, u32[]{:S(2)}, u32[]{:S(2)}) collective-permute-start(bf16[64,896]{1,0:T(8,128)(2,1)S(1)} %maximum_maximum_fusion), channel_id=1, source_target_pairs={{0,4},{1,5},{2,6},{3,7},{4,0},{5,1},{6,2},{7,3},{8,12},{9,13},{10,... | collective-permute-start | bytes 344072 | tf_op jit(solution)/shard_map/ppermute | solution.py:27
  100.2 8.1 %collective-permute-start.18 = (bf16[2,64,768]{2,1,0:T(8,128)(2,1)S(1)}, bf16[2,64,768]{2,1,0:T(8,128)(2,1)S(1)}, u32[]{:S(2)}, u32[]{:S(2)}) collective-permute-start(bf16[2,64,768]{2,1,0:T(8,128)(2,1)S(1)} %pad_maximum_fusion.8), channel_id=1, source_target_pairs={{0,4},{1,5},{2,6},{3,7},{4,0},{5,1},{6,2},{7,3},{8,12},{9,13},{10,... | collective-permute-start | bytes 589832 | tf_op jit(solution)/shard_map/ppermute | solution.py:27
  104.8 10.1 %collective-permute-start.13 = (bf16[2,64,896]{2,1,0:T(8,128)(2,1)S(1)}, bf16[2,64,896]{2,1,0:T(8,128)(2,1)S(1)}, u32[]{:S(2)}, u32[]{:S(2)}) collective-permute-start(bf16[2,64,896]{2,1,0:T(8,128)(2,1)S(1)} %pad_maximum_fusion.7), channel_id=1, source_target_pairs={{0,16},{1,17},{2,18},{3,19},{4,20},{5,21},{6,22},{7,23},{8,24},{9,... | collective-permute-start | bytes 688136 | tf_op jit(solution)/shard_map/ppermute | solution.py:27
  108.4 7.9 %collective-permute-start.19 = (bf16[2,2,64,768]{3,2,1,0:T(8,128)(2,1)S(1)}, bf16[2,2,64,768]{3,2,1,0:T(8,128)(2,1)S(1)}, u32[]{:S(2)}, u32[]{:S(2)}) collective-permute-start(bf16[2,2,64,768]{3,2,1,0:T(8,128)(2,1)S(1)} %pad_maximum_fusion.6), channel_id=1, source_target_pairs={{0,2},{1,3},{2,0},{3,1},{4,6},{5,7},{6,4},{7,5},{8,10},{9,11},{10,... | collective-permute-start | bytes 1179656 | tf_op jit(solution)/shard_map/ppermute | solution.py:27
  115.0 13.0 %collective-permute-start.14 = (bf16[2,2,64,896]{3,2,1,0:T(8,128)(2,1)S(1)}, bf16[2,2,64,896]{3,2,1,0:T(8,128)(2,1)S(1)}, u32[]{:S(2)}, u32[]{:S(2)}) collective-permute-start(bf16[2,2,64,896]{3,2,1,0:T(8,128)(2,1)S(1)} %pad_maximum_fusion.5), channel_id=1, source_target_pairs={{0,8},{1,9},{2,10},{3,11},{4,12},{5,13},{6,14},{7,15},{8,0},{9,1},... | collective-permute-start | bytes 1376264 | tf_op jit(solution)/shard_map/ppermute | solution.py:27
  116.4 20.0 %collective-permute-start.20 = (bf16[2,2,2,64,768]{4,3,2,1,0:T(8,128)(2,1)S(1)}, bf16[2,2,2,64,768]{4,3,2,1,0:T(8,128)(2,1)S(1)}, u32[]{:S(2)}, u32[]{:S(2)}) collective-permute-start(bf16[2,2,2,64,768]{4,3,2,1,0:T(8,128)(2,1)S(1)} %pad_maximum_fusion.4), channel_id=1, source_target_pairs={{0,8},{1,9},{2,10},{3,11},{4,12},{5,13},{6,14},{7,15},{8,0},{9,1},... | collective-permute-start | bytes 2359304 | tf_op jit(solution)/shard_map/ppermute | solution.py:27
  128.2 13.5 %collective-permute-start.15 = (bf16[2,2,2,64,896]{4,3,2,1,0:T(8,128)(2,1)S(1)}, bf16[2,2,2,64,896]{4,3,2,1,0:T(8,128)(2,1)S(1)}, u32[]{:S(2)}, u32[]{:S(2)}) collective-permute-start(bf16[2,2,2,64,896]{4,3,2,1,0:T(8,128)(2,1)S(1)} %pad_maximum_fusion.3), channel_id=1, source_target_pairs={{0,2},{1,3},{2,0},{3,1},{4,6},{5,7},{6,4},{7,5},{8,10},{9,11},{10,... | collective-permute-start | bytes 2752520 | tf_op jit(solution)/shard_map/ppermute | solution.py:27
  180.3 19.9 %collective-permute-start.28 = (bf16[2,2,2,64,768]{4,3,1,2,0:T(8,128)(2,1)}, bf16[2,2,2,64,768]{4,3,1,2,0:T(8,128)(2,1)}, u32[]{:S(2)}, u32[]{:S(2)}) collective-permute-start(bf16[2,2,2,64,768]{4,3,1,2,0:T(8,128)(2,1)} %fusion.13), channel_id=1, source_target_pairs={{0,8},{1,9},{2,10},{3,11},{4,12},{5,13},{6,14},{7,15},{8,0},{9,1},... | collective-permute-start | bytes 2359304 | tf_op jit(solution)/shard_map/ppermute | solution.py:27
  184.2 20.1 %collective-permute-start.23 = (bf16[2,2,2,64,768]{4,3,2,1,0:T(8,128)(2,1)}, bf16[2,2,2,64,768]{4,3,2,1,0:T(8,128)(2,1)}, u32[]{:S(2)}, u32[]{:S(2)}) collective-permute-start(bf16[2,2,2,64,768]{4,3,2,1,0:T(8,128)(2,1)} %fusion.12), channel_id=1, source_target_pairs={{0,2},{1,3},{2,0},{3,1},{4,6},{5,7},{6,4},{7,5},{8,10},{9,11},{10,... | collective-permute-start | bytes 2359304 | tf_op jit(solution)/shard_map/ppermute | solution.py:27
  201.8 10.6 %collective-permute-start.29 = (bf16[2,2,64,768]{3,2,0,1:T(8,128)(2,1)S(1)}, bf16[2,2,64,768]{3,2,0,1:T(8,128)(2,1)S(1)}, u32[]{:S(2)}, u32[]{:S(2)}) collective-permute-start(bf16[2,2,64,768]{3,2,0,1:T(8,128)(2,1)S(1)} %fusion.35), channel_id=1, source_target_pairs={{0,2},{1,3},{2,0},{3,1},{4,6},{5,7},{6,4},{7,5},{8,10},{9,11},{10,... | collective-permute-start | bytes 1179656 | tf_op jit(solution)/shard_map/ppermute | solution.py:27
  205.9 10.8 %collective-permute-start.24 = (bf16[2,2,64,768]{3,2,1,0:T(8,128)(2,1)S(1)}, bf16[2,2,64,768]{3,2,1,0:T(8,128)(2,1)S(1)}, u32[]{:S(2)}, u32[]{:S(2)}) collective-permute-start(bf16[2,2,64,768]{3,2,1,0:T(8,128)(2,1)S(1)} %fusion.34), channel_id=1, source_target_pairs={{0,8},{1,9},{2,10},{3,11},{4,12},{5,13},{6,14},{7,15},{8,0},{9,1},... | collective-permute-start | bytes 1179656 | tf_op jit(solution)/shard_map/ppermute | solution.py:27
  212.6 7.3 %collective-permute-start.30 = (bf16[2,64,768]{2,1,0:T(8,128)(2,1)S(1)}, bf16[2,64,768]{2,1,0:T(8,128)(2,1)S(1)}, u32[]{:S(2)}, u32[]{:S(2)}) collective-permute-start(bf16[2,64,768]{2,1,0:T(8,128)(2,1)S(1)} %fusion.41), channel_id=1, source_target_pairs={{0,4},{1,5},{2,6},{3,7},{4,0},{5,1},{6,2},{7,3},{8,12},{9,13},{10,... | collective-permute-start | bytes 589832 | tf_op jit(solution)/shard_map/ppermute | solution.py:27
  216.8 8.0 %collective-permute-start.25 = (bf16[2,64,768]{2,1,0:T(8,128)(2,1)S(1)}, bf16[2,64,768]{2,1,0:T(8,128)(2,1)S(1)}, u32[]{:S(2)}, u32[]{:S(2)}) collective-permute-start(bf16[2,64,768]{2,1,0:T(8,128)(2,1)S(1)} %fusion.40), channel_id=1, source_target_pairs={{0,16},{1,17},{2,18},{3,19},{4,20},{5,21},{6,22},{7,23},{8,24},{9,... | collective-permute-start | bytes 589832 | tf_op jit(solution)/shard_map/ppermute | solution.py:27
  219.9 7.2 %collective-permute-start.31 = (bf16[64,768]{1,0:T(8,128)(2,1)S(1)}, bf16[64,768]{1,0:T(8,128)(2,1)S(1)}, u32[]{:S(2)}, u32[]{:S(2)}) collective-permute-start(bf16[64,768]{1,0:T(8,128)(2,1)S(1)} %fusion.44), channel_id=1, source_target_pairs={{0,16},{1,17},{2,18},{3,19},{4,20},{5,21},{6,22},{7,23},{8,24},{9,... | collective-permute-start | bytes 294920 | tf_op jit(solution)/shard_map/ppermute | solution.py:27
  (23 other events, 142.8 us)

commit v12 on v10

--- a/solution.py
+++ b/solution.py
@@ -332,11 +332,16 @@
         1,
     ).astype(jnp.float32)
     expert_part = dense_experts(first_rows, second_rows, local_shares, w_gate_up, w_down)
-    flat_part = expert_part
+    half_rows = expert_part.shape[0] // 2
+    core_upper = lax.axis_index(TENSOR) & 1 == 1
+    kept_rows = jnp.where(core_upper, expert_part[half_rows:], expert_part[:half_rows])
+    sent_rows = jnp.where(core_upper, expert_part[:half_rows], expert_part[half_rows:])
+    flat_part = kept_rows.astype(jnp.float32) + partner(sent_rows, TENSOR, 0).astype(jnp.float32)
+    rest = layout[1:]
     expert_sum = jnp.concatenate(
         [
-            fold_any(flat_part[:, :half_width], layout, (0, 1, 3, 4, 2)),
-            fold_any(flat_part[:, half_width:], layout, (0, 3, 1, 2, 4)),
+            fold_any(flat_part[:, :half_width], rest, (1, 3, 4, 2)),
+            fold_any(flat_part[:, half_width:], rest, (3, 1, 2, 4)),
         ],
         axis=1,
     )

time: 232 us -> 234 us (level)
  waiting for transfers between devices: 113 us -> 116 us
    add x0 -> x1, other arithmetic: none -> 4.08 us  [on_device(): kept_rows.astype(jnp.float32)]
    add x12 -> x10, other arithmetic: 4.77 us -> 1.37 us  [fold_any(): state = kept_rows.astype(jnp.float32) + arrived.astype(jnp.float32)]
    ppermute x32 -> x31, waiting for transfers between devices: 113 us -> 116 us  [partner(): return lax.ppermute(value, axis, pairs)]
    select_n x1 -> x2, other arithmetic: 3.02 us -> 5.19 us  [the longest x1 4.89 us: on_device(): jnp.where(core_upper, expert_part[:half_rows], expert_part[half_rows:])]
    unnamed x31 -> x27, local copies, waits for them, and re-layouts: 5.73 us -> 4.09 us
    ppermute x32 -> x31, starting transfers between devices: 38.1 us -> 38.2 us  [partner(): return lax.ppermute(value, axis, pairs)]
  transfers between devices with their start and end apart: 32 -> 31, of which waited for: 27 -> 25; matrix products, arithmetic and copies ran while one was open for 15% -> 13% of each run, Pallas kernels for 0% -> 0%
where the time goes in v12:
time: 234 us; the launch traced here: 230 us
  waiting for transfers between devices  116 us (50%)
  starting transfers between devices  38.2 us (16%)
  other arithmetic  28.8 us (12%)
  Pallas kernels  19.5 us (8%)
  local copies, waits for them, and re-layouts  13.4 us (6%)
  loops' own time  6.58 us (3%)
  matrix products  5.43 us (2%)
    ppermute x31, waiting for transfers between devices, partner(): return lax.ppermute(value, axis, pairs)  116 us
    ppermute x31, starting transfers between devices, partner(): return lax.ppermute(value, axis, pairs)  38.2 us
    pallas_call x1, Pallas kernels, dense_experts(): pl.pallas_call(expert_block, grid=(row_count // tile,), in_specs=[pl.Bloc...  19.5 us
    another operation x19, other arithmetic, gather_any(): state = jnp.stack([lower_rows, upper_rows], axis=0)  7.56 us
    another operation x1, loops' own time, on_device(): lax.map(attend, jnp.arange(rows_quarter // block_rows, dtype=jnp.int32))  6.2 us
    select_n x1, other arithmetic, on_device(): jnp.where(core_upper, expert_part[:half_rows], expert_part[half_rows:])  4.89 us
  transfers between devices with their start and end apart: 31, of which 25 were waited for; matrix products, arithmetic and copies ran while one was open for 13% of the time, Pallas kernels for 0%

profile of v12, /device:TPU:24, one launch (start us, length us, event | category | flops | bytes accessed | tf_op | source)
XLA Modules:
  0.0 229.7 jit_solution(1464898351782196910)
XLA Ops:
  3.6 3.1 %collective-permute-start = (bf16[64,1536]{1,0:T(8,128)(2,1)S(1)}, bf16[64,1536]{1,0:T(8,128)(2,1)S(1)}, u32[]{:S(2)}, u32[]{:S(2)}) collective-permute-start(bf16[64,1536]{1,0:T(8,128)(2,1)S(1)} %fusion.26), channel_id=1, source_target_pairs={{0,4},{1,5},{2,6},{3,7},{4,0},{5,1},{6,2},{7,3},{8,12},{9,13},{10,... | collective-permute-start | bytes 589832 | tf_op jit(solution)/shard_map/ppermute | solution.py:27
  15.2 6.3 %collective-permute-done.1 = bf16[128,1536]{1,0:T(8,128)(2,1)S(1)} collective-permute-done((bf16[128,1536]{1,0:T(8,128)(2,1)S(1)}, bf16[128,1536]{1,0:T(8,128)(2,1)S(1)}, u32[]{:S(2)}, u32[]{:S(2)}) %collective-permute-start.1) | collective-permute-done | bytes 393248 | tf_op jit(solution)/shard_map/ppermute | solution.py:27
  23.4 4.3 %collective-permute-done.4 = bf16[1536,160]{0,1:T(8,128)(2,1)S(1)} collective-permute-done((bf16[1536,160]{0,1:T(8,128)(2,1)S(1)}, bf16[1536,160]{0,1:T(8,128)(2,1)S(1)}, u32[]{:S(2)}, u32[]{:S(2)}) %collective-permute-start.4) | collective-permute-done | bytes 491552 | tf_op jit(solution)/shard_map/ppermute | solution.py:27
  32.6 3.0 %collective-permute-done.5 = bf16[512,128]{0,1:T(8,128)(2,1)S(1)} collective-permute-done((bf16[512,128]{0,1:T(8,128)(2,1)S(1)}, bf16[512,128]{0,1:T(8,128)(2,1)S(1)}, u32[]{:S(2)}, u32[]{:S(2)}) %collective-permute-start.5) | collective-permute-done | bytes 131104 | tf_op jit(solution)/shard_map/ppermute | solution.py:27
  35.7 2.8 %collective-permute-start.6 = (bf16[1024,128]{0,1:T(8,128)(2,1)S(1)}, bf16[1024,128]{0,1:T(8,128)(2,1)S(1)}, u32[]{:S(2)}, u32[]{:S(2)}) collective-permute-start(bf16[1024,128]{0,1:T(8,128)(2,1)S(1)} %maximum_select_fusion.8), channel_id=1, source_target_pairs={{0,16},{1,17},{2,18},{3,19},{4,20},{5,21},{6,22},{7,23},{8,24},{9,... | collective-permute-start | bytes 786440 | tf_op jit(solution)/shard_map/ppermute | solution.py:27
  38.6 6.0 %collective-permute-done.6 = bf16[1024,128]{0,1:T(8,128)(2,1)S(1)} collective-permute-done((bf16[1024,128]{0,1:T(8,128)(2,1)S(1)}, bf16[1024,128]{0,1:T(8,128)(2,1)S(1)}, u32[]{:S(2)}, u32[]{:S(2)}) %collective-permute-start.6) | collective-permute-done | bytes 262176 | tf_op jit(solution)/shard_map/ppermute | solution.py:27
  45.0 17.2 %while.59 = (s32[]{:T(128)}, bf16[2,256,192]{1,2,0:T(8,128)(2,1)S(1)}, s32[2]{0:T(128)S(1)}, s32[]{:T(128)}, s32[2048]{0:T(1024)S(1)}, /*index=5*/bf16[3,512,64]...) while((s32[]{:T(128)}, ...), condition=%wide.region_8.9_spmd, body=%wide.region_3.8_spmd.sunk | while | flops 104007976 | bytes 8950756 | solution.py:295
  49.5 4.0 %while.60 = (s32[]{:T(128)}, f32[768]{0:T(1024)S(1)}, f32[768]{0:T(1024)S(1)}, f32[768,64]{0,1:T(8,128)S(1)}, s32[]{:T(128)}, /*index=5*/s32[256]{0:T(256)S(1)},...) while((s32[]{:T(128)}, f32[768]{0:T(1024)S(1)}, ...), condition=%wide.region_7.7_spmd.clone, body=%wide.region_4.6_spmd.clone.sunk | while | flops 103909632 | bytes 7464147 | solution.py:291
  58.1 4.0 %while.60 = (s32[]{:T(128)}, f32[768]{0:T(1024)S(1)}, f32[768]{0:T(1024)S(1)}, f32[768,64]{0,1:T(8,128)S(1)}, s32[]{:T(128)}, /*index=5*/s32[256]{0:T(256)S(1)},...) while((s32[]{:T(128)}, f32[768]{0:T(1024)S(1)}, ...), condition=%wide.region_7.7_spmd.clone, body=%wide.region_4.6_spmd.clone.sunk | while | flops 103909632 | bytes 7464147 | solution.py:291
  67.3 10.2 %collective-permute-done.10 = bf16[2,64,1536]{2,1,0:T(8,128)(2,1)S(1)} collective-permute-done((bf16[2,64,1536]{2,1,0:T(8,128)(2,1)S(1)}, bf16[2,64,1536]{2,1,0:T(8,128)(2,1)S(1)}, u32[]{:S(2)}, u32[]{:S(2)}) %collective-permute-start.10) | collective-permute-done | bytes 393248 | tf_op jit(solution)/shard_map/ppermute | solution.py:27
  80.3 5.1 %collective-permute-done.11 = bf16[64,1536]{1,0:T(8,128)(2,1)S(1)} collective-permute-done((bf16[64,1536]{1,0:T(8,128)(2,1)S(1)}, bf16[64,1536]{1,0:T(8,128)(2,1)S(1)}, u32[]{:S(2)}, u32[]{:S(2)}) %collective-permute-start.11) | collective-permute-done | bytes 196640 | tf_op jit(solution)/shard_map/ppermute | solution.py:27
  87.9 4.6 %collective-permute-done.17 = bf16[64,768]{1,0:T(8,128)(2,1)S(1)} collective-permute-done((bf16[64,768]{1,0:T(8,128)(2,1)S(1)}, bf16[64,768]{1,0:T(8,128)(2,1)S(1)}, u32[]{:S(2)}, u32[]{:S(2)}) %collective-permute-start.17) | collective-permute-done | bytes 98336 | tf_op jit(solution)/shard_map/ppermute | solution.py:27
  96.4 3.4 %collective-permute-done.12 = bf16[64,896]{1,0:T(8,128)(2,1)S(1)} collective-permute-done((bf16[64,896]{1,0:T(8,128)(2,1)S(1)}, bf16[64,896]{1,0:T(8,128)(2,1)S(1)}, u32[]{:S(2)}, u32[]{:S(2)}) %collective-permute-start.12) | collective-permute-done | bytes 114720 | tf_op jit(solution)/shard_map/ppermute | solution.py:27
  104.5 5.5 %collective-permute-done.13 = bf16[2,64,896]{2,1,0:T(8,128)(2,1)S(1)} collective-permute-done((bf16[2,64,896]{2,1,0:T(8,128)(2,1)S(1)}, bf16[2,64,896]{2,1,0:T(8,128)(2,1)S(1)}, u32[]{:S(2)}, u32[]{:S(2)}) %collective-permute-start.13) | collective-permute-done | bytes 229408 | tf_op jit(solution)/shard_map/ppermute | solution.py:27
  112.4 10.6 %collective-permute-done.14 = bf16[2,2,64,896]{3,2,1,0:T(8,128)(2,1)S(1)} collective-permute-done((bf16[2,2,64,896]{3,2,1,0:T(8,128)(2,1)S(1)}, bf16[2,2,64,896]{3,2,1,0:T(8,128)(2,1)S(1)}, u32[]{:S(2)}, u32[]{:S(2)}) %collective-permute-start.14) | collective-permute-done | bytes 458784 | tf_op jit(solution)/shard_map/ppermute | solution.py:27
  124.1 7.4 %collective-permute-done.20 = bf16[2,2,2,64,768]{4,3,2,1,0:T(8,128)(2,1)S(1)} collective-permute-done((bf16[2,2,2,64,768]{4,3,2,1,0:T(8,128)(2,1)S(1)}, bf16[2,2,2,64,768]{4,3,2,1,0:T(8,128)(2,1)S(1)}, u32[]{:S(2)}, u32[]{:S(2)}) %collective-permute-start.20) | collective-permute-done | bytes 786464 | tf_op jit(solution)/shard_map/ppermute | solution.py:27
  132.9 3.9 %collective-permute-done.15 = bf16[2,2,2,64,896]{4,3,2,1,0:T(8,128)(2,1)S(1)} collective-permute-done((bf16[2,2,2,64,896]{4,3,2,1,0:T(8,128)(2,1)S(1)}, bf16[2,2,2,64,896]{4,3,2,1,0:T(8,128)(2,1)S(1)}, u32[]{:S(2)}, u32[]{:S(2)}) %collective-permute-start.15) | collective-permute-done | bytes 917536 | tf_op jit(solution)/shard_map/ppermute | solution.py:27
  147.7 19.5 %shard_map.121 = bf16[2048,1536]{1,0:T(8,128)(2,1)} custom-call(bf16[2048,896]{1,0:T(8,128)(2,1)} %bitcast.187, bf16[2048,768]{1,0:T(8,128)(2,1)S(1)} %bitcast.183, f32[2048,5]{1,0:T(8,128)S(1)} %dynamic-slice_convert_fusion.share_ref, bf16[5,1536,256]{2,1,0:T(8,128)(2,1)} %gate_up_ref.1, bf16[5,128,1536]{2,1,0:T(8,128)(2,1)S(1)} %copy-done), custom_call_target="tpu_custom_call" | custom-call | tf_op jit(solution)/shard_map/pallas_call | solution.py:148
  167.2 4.9 %broadcast_select_fusion = bf16[1024,1536]{1,0:T(8,128)(2,1)} fusion(pred[]{:T(512)S(6)} %eq.25, bf16[2048,1536]{1,0:T(8,128)(2,1)} %shard_map.121), kind=kLoop, calls=%fused_computation.21 | loop fusion | flops 1572864 | bytes 9437185 | tf_op jit(solution)/shard_map/jit(_where)/select_n | solution.py:338
  173.9 4.0 %collective-permute-done.22 = bf16[1024,1536]{1,0:T(8,128)(2,1)S(1)} collective-permute-done((bf16[1024,1536]{1,0:T(8,128)(2,1)}, bf16[1024,1536]{1,0:T(8,128)(2,1)S(1)}, u32[]{:S(2)}, u32[]{:S(2)}) %collective-permute-start.22) | collective-permute-done | bytes 3145760 | tf_op jit(solution)/shard_map/ppermute | solution.py:27
  178.0 4.1 %convert_add_fusion = f32[1024,1536]{1,0:T(8,128)S(1)} fusion(bf16[1024,1536]{1,0:T(8,128)(2,1)S(1)} %collective-permute-done.22, pred[]{:T(512)S(6)} %eq.25, bf16[2048,1536]{1,0:T(8,128)(2,1)} %shard_map.121), kind=kLoop, calls=%fused_computation.18 | loop fusion | flops 6291456 | bytes 15728641 | tf_op jit(solution)/shard_map/add | solution.py:339
  184.5 17.6 %collective-permute-done.23 = bf16[2,2,2,64,768]{4,3,2,1,0:T(8,128)(2,1)S(1)} collective-permute-done((bf16[2,2,2,64,768]{4,3,2,1,0:T(8,128)(2,1)S(1)}, bf16[2,2,2,64,768]{4,3,2,1,0:T(8,128)(2,1)S(1)}, u32[]{:S(2)}, u32[]{:S(2)}) %collective-permute-start.23) | collective-permute-done | bytes 786464 | tf_op jit(solution)/shard_map/ppermute | solution.py:27
  204.9 7.9 %collective-permute-done.24 = bf16[2,2,64,768]{3,2,1,0:T(8,128)(2,1)S(1)} collective-permute-done((bf16[2,2,64,768]{3,2,1,0:T(8,128)(2,1)S(1)}, bf16[2,2,64,768]{3,2,1,0:T(8,128)(2,1)S(1)}, u32[]{:S(2)}, u32[]{:S(2)}) %collective-permute-start.24) | collective-permute-done | bytes 393248 | tf_op jit(solution)/shard_map/ppermute | solution.py:27
  216.5 3.7 %collective-permute-done.25 = bf16[2,64,768]{2,1,0:T(8,128)(2,1)S(1)} collective-permute-done((bf16[2,64,768]{2,1,0:T(8,128)(2,1)S(1)}, bf16[2,64,768]{2,1,0:T(8,128)(2,1)S(1)}, u32[]{:S(2)}, u32[]{:S(2)}) %collective-permute-start.25) | collective-permute-done | bytes 196640 | tf_op jit(solution)/shard_map/ppermute | solution.py:27
  (235 shorter events, 83.3 us)
Async XLA Ops:
  0.6 21.4 %collective-permute-start.7 = (bf16[1536,48]{0,1:T(8,128)(2,1)}, bf16[1536,48]{0,1:T(8,128)(2,1)S(1)}, u32[]{:S(2)}, u32[]{:S(2)}) collective-permute-start(bf16[1536,48]{0,1:T(8,128)(2,1)} %param.20), channel_id=1, source_target_pairs={{0,8},{1,9},{2,10},{3,11},{4,12},{5,13},{6,14},{7,15},{8,0},{9,1},... | collective-permute-start | bytes 442376 | tf_op jit(solution)/shard_map/ppermute | solution.py:27
  3.6 8.0 %collective-permute-start = (bf16[64,1536]{1,0:T(8,128)(2,1)S(1)}, bf16[64,1536]{1,0:T(8,128)(2,1)S(1)}, u32[]{:S(2)}, u32[]{:S(2)}) collective-permute-start(bf16[64,1536]{1,0:T(8,128)(2,1)S(1)} %fusion.26), channel_id=1, source_target_pairs={{0,4},{1,5},{2,6},{3,7},{4,0},{5,1},{6,2},{7,3},{8,12},{9,13},{10,... | collective-permute-start | bytes 589832 | tf_op jit(solution)/shard_map/ppermute | solution.py:27
  6.7 7.3 %collective-permute-start.3 = (bf16[1536,80]{0,1:T(8,128)(2,1)}, bf16[1536,80]{0,1:T(8,128)(2,1)S(1)}, u32[]{:S(2)}, u32[]{:S(2)}) collective-permute-start(bf16[1536,80]{0,1:T(8,128)(2,1)} %param.19), channel_id=1, source_target_pairs={{0,8},{1,9},{2,10},{3,11},{4,12},{5,13},{6,14},{7,15},{8,0},{9,1},... | collective-permute-start | bytes 737288 | tf_op jit(solution)/shard_map/ppermute | solution.py:27
  11.6 9.8 %collective-permute-start.1 = (bf16[128,1536]{1,0:T(8,128)(2,1)S(1)}, bf16[128,1536]{1,0:T(8,128)(2,1)S(1)}, u32[]{:S(2)}, u32[]{:S(2)}) collective-permute-start(bf16[128,1536]{1,0:T(8,128)(2,1)S(1)} %maximum_select_fusion.6), channel_id=1, source_target_pairs={{0,2},{1,3},{2,0},{3,1},{4,6},{5,7},{6,4},{7,5},{8,10},{9,11},{10,... | collective-permute-start | bytes 1179656 | tf_op jit(solution)/shard_map/ppermute | solution.py:27
  14.2 13.6 %collective-permute-start.4 = (bf16[1536,160]{0,1:T(8,128)(2,1)S(1)}, bf16[1536,160]{0,1:T(8,128)(2,1)S(1)}, u32[]{:S(2)}, u32[]{:S(2)}) collective-permute-start(bf16[1536,160]{0,1:T(8,128)(2,1)S(1)} %maximum_select_fusion.5), channel_id=1, source_target_pairs={{0,16},{1,17},{2,18},{3,19},{4,20},{5,21},{6,22},{7,23},{8,24},{9,... | collective-permute-start | bytes 1474568 | tf_op jit(solution)/shard_map/ppermute | solution.py:27
  21.6 6.5 %collective-permute-start.2 = (bf16[256,1536]{1,0:T(8,128)(2,1)S(1)}, bf16[256,1536]{1,0:T(8,128)(2,1)S(1)}, u32[]{:S(2)}, u32[]{:S(2)}) collective-permute-start(bf16[256,1536]{1,0:T(8,128)(2,1)S(1)} %maximum_select_fusion.2), channel_id=1, source_target_pairs={{0,1},{1,0},{2,3},{3,2},{4,5},{5,4},{6,7},{7,6},{8,9},{9,8},{10,11... | collective-permute-start | bytes 2359304 | tf_op jit(solution)/shard_map/ppermute | solution.py:27
  22.1 40.3 %collective-permute-start.8 = (bf16[1536,96]{0,1:T(8,128)(2,1)S(1)}, bf16[1536,96]{0,1:T(8,128)(2,1)S(1)}, u32[]{:S(2)}, u32[]{:S(2)}) collective-permute-start(bf16[1536,96]{0,1:T(8,128)(2,1)S(1)} %maximum_select_fusion.7), channel_id=1, source_target_pairs={{0,16},{1,17},{2,18},{3,19},{4,20},{5,21},{6,22},{7,23},{8,24},{9,... | collective-permute-start | bytes 884744 | tf_op jit(solution)/shard_map/ppermute | solution.py:27
  35.7 8.9 %collective-permute-start.6 = (bf16[1024,128]{0,1:T(8,128)(2,1)S(1)}, bf16[1024,128]{0,1:T(8,128)(2,1)S(1)}, u32[]{:S(2)}, u32[]{:S(2)}) collective-permute-start(bf16[1024,128]{0,1:T(8,128)(2,1)S(1)} %maximum_select_fusion.8), channel_id=1, source_target_pairs={{0,16},{1,17},{2,18},{3,19},{4,20},{5,21},{6,22},{7,23},{8,24},{9,... | collective-permute-start | bytes 786440 | tf_op jit(solution)/shard_map/ppermute | solution.py:27
  66.2 11.2 %collective-permute-start.10 = (bf16[2,64,1536]{2,1,0:T(8,128)(2,1)S(1)}, bf16[2,64,1536]{2,1,0:T(8,128)(2,1)S(1)}, u32[]{:S(2)}, u32[]{:S(2)}) collective-permute-start(bf16[2,64,1536]{2,1,0:T(8,128)(2,1)S(1)} %fusion.32), channel_id=1, source_target_pairs={{0,2},{1,3},{2,0},{3,1},{4,6},{5,7},{6,4},{7,5},{8,10},{9,11},{10,... | collective-permute-start | bytes 1179656 | tf_op jit(solution)/shard_map/ppermute | solution.py:27
  77.7 7.7 %collective-permute-start.11 = (bf16[64,1536]{1,0:T(8,128)(2,1)S(1)}, bf16[64,1536]{1,0:T(8,128)(2,1)S(1)}, u32[]{:S(2)}, u32[]{:S(2)}) collective-permute-start(bf16[64,1536]{1,0:T(8,128)(2,1)S(1)} %fusion.38), channel_id=1, source_target_pairs={{0,4},{1,5},{2,6},{3,7},{4,0},{5,1},{6,2},{7,3},{8,12},{9,13},{10,... | collective-permute-start | bytes 589832 | tf_op jit(solution)/shard_map/ppermute | solution.py:27
  92.6 7.2 %collective-permute-start.12 = (bf16[64,896]{1,0:T(8,128)(2,1)S(1)}, bf16[64,896]{1,0:T(8,128)(2,1)S(1)}, u32[]{:S(2)}, u32[]{:S(2)}) collective-permute-start(bf16[64,896]{1,0:T(8,128)(2,1)S(1)} %maximum_maximum_fusion), channel_id=1, source_target_pairs={{0,4},{1,5},{2,6},{3,7},{4,0},{5,1},{6,2},{7,3},{8,12},{9,13},{10,... | collective-permute-start | bytes 344072 | tf_op jit(solution)/shard_map/ppermute | solution.py:27
  95.3 8.1 %collective-permute-start.18 = (bf16[2,64,768]{2,1,0:T(8,128)(2,1)S(1)}, bf16[2,64,768]{2,1,0:T(8,128)(2,1)S(1)}, u32[]{:S(2)}, u32[]{:S(2)}) collective-permute-start(bf16[2,64,768]{2,1,0:T(8,128)(2,1)S(1)} %pad_maximum_fusion.8), channel_id=1, source_target_pairs={{0,4},{1,5},{2,6},{3,7},{4,0},{5,1},{6,2},{7,3},{8,12},{9,13},{10,... | collective-permute-start | bytes 589832 | tf_op jit(solution)/shard_map/ppermute | solution.py:27
  99.9 10.1 %collective-permute-start.13 = (bf16[2,64,896]{2,1,0:T(8,128)(2,1)S(1)}, bf16[2,64,896]{2,1,0:T(8,128)(2,1)S(1)}, u32[]{:S(2)}, u32[]{:S(2)}) collective-permute-start(bf16[2,64,896]{2,1,0:T(8,128)(2,1)S(1)} %pad_maximum_fusion.7), channel_id=1, source_target_pairs={{0,16},{1,17},{2,18},{3,19},{4,20},{5,21},{6,22},{7,23},{8,24},{9,... | collective-permute-start | bytes 688136 | tf_op jit(solution)/shard_map/ppermute | solution.py:27
  103.4 7.9 %collective-permute-start.19 = (bf16[2,2,64,768]{3,2,1,0:T(8,128)(2,1)S(1)}, bf16[2,2,64,768]{3,2,1,0:T(8,128)(2,1)S(1)}, u32[]{:S(2)}, u32[]{:S(2)}) collective-permute-start(bf16[2,2,64,768]{3,2,1,0:T(8,128)(2,1)S(1)} %pad_maximum_fusion.6), channel_id=1, source_target_pairs={{0,2},{1,3},{2,0},{3,1},{4,6},{5,7},{6,4},{7,5},{8,10},{9,11},{10,... | collective-permute-start | bytes 1179656 | tf_op jit(solution)/shard_map/ppermute | solution.py:27
  110.1 13.0 %collective-permute-start.14 = (bf16[2,2,64,896]{3,2,1,0:T(8,128)(2,1)S(1)}, bf16[2,2,64,896]{3,2,1,0:T(8,128)(2,1)S(1)}, u32[]{:S(2)}, u32[]{:S(2)}) collective-permute-start(bf16[2,2,64,896]{3,2,1,0:T(8,128)(2,1)S(1)} %pad_maximum_fusion.5), channel_id=1, source_target_pairs={{0,8},{1,9},{2,10},{3,11},{4,12},{5,13},{6,14},{7,15},{8,0},{9,1},... | collective-permute-start | bytes 1376264 | tf_op jit(solution)/shard_map/ppermute | solution.py:27
  111.5 20.0 %collective-permute-start.20 = (bf16[2,2,2,64,768]{4,3,2,1,0:T(8,128)(2,1)S(1)}, bf16[2,2,2,64,768]{4,3,2,1,0:T(8,128)(2,1)S(1)}, u32[]{:S(2)}, u32[]{:S(2)}) collective-permute-start(bf16[2,2,2,64,768]{4,3,2,1,0:T(8,128)(2,1)S(1)} %pad_maximum_fusion.4), channel_id=1, source_target_pairs={{0,8},{1,9},{2,10},{3,11},{4,12},{5,13},{6,14},{7,15},{8,0},{9,1},... | collective-permute-start | bytes 2359304 | tf_op jit(solution)/shard_map/ppermute | solution.py:27
  123.3 13.5 %collective-permute-start.15 = (bf16[2,2,2,64,896]{4,3,2,1,0:T(8,128)(2,1)S(1)}, bf16[2,2,2,64,896]{4,3,2,1,0:T(8,128)(2,1)S(1)}, u32[]{:S(2)}, u32[]{:S(2)}) collective-permute-start(bf16[2,2,2,64,896]{4,3,2,1,0:T(8,128)(2,1)S(1)} %pad_maximum_fusion.3), channel_id=1, source_target_pairs={{0,2},{1,3},{2,0},{3,1},{4,6},{5,7},{6,4},{7,5},{8,10},{9,11},{10,... | collective-permute-start | bytes 2752520 | tf_op jit(solution)/shard_map/ppermute | solution.py:27
  182.4 19.7 %collective-permute-start.23 = (bf16[2,2,2,64,768]{4,3,2,1,0:T(8,128)(2,1)S(1)}, bf16[2,2,2,64,768]{4,3,2,1,0:T(8,128)(2,1)S(1)}, u32[]{:S(2)}, u32[]{:S(2)}) collective-permute-start(bf16[2,2,2,64,768]{4,3,2,1,0:T(8,128)(2,1)S(1)} %bitcast.196), channel_id=1, source_target_pairs={{0,2},{1,3},{2,0},{3,1},{4,6},{5,7},{6,4},{7,5},{8,10},{9,11},{10,... | collective-permute-start | bytes 2359304 | tf_op jit(solution)/shard_map/ppermute | solution.py:27
  183.7 19.4 %collective-permute-start.27 = (bf16[2,2,2,64,768]{4,3,1,2,0:T(8,128)(2,1)S(1)}, bf16[2,2,2,64,768]{4,3,1,2,0:T(8,128)(2,1)S(1)}, u32[]{:S(2)}, u32[]{:S(2)}) collective-permute-start(bf16[2,2,2,64,768]{4,3,1,2,0:T(8,128)(2,1)S(1)} %fusion.12), channel_id=1, source_target_pairs={{0,8},{1,9},{2,10},{3,11},{4,12},{5,13},{6,14},{7,15},{8,0},{9,1},... | collective-permute-start | bytes 2359304 | tf_op jit(solution)/shard_map/ppermute | solution.py:27
  202.4 10.4 %collective-permute-start.24 = (bf16[2,2,64,768]{3,2,1,0:T(8,128)(2,1)S(1)}, bf16[2,2,64,768]{3,2,1,0:T(8,128)(2,1)S(1)}, u32[]{:S(2)}, u32[]{:S(2)}) collective-permute-start(bf16[2,2,64,768]{3,2,1,0:T(8,128)(2,1)S(1)} %fusion.33), channel_id=1, source_target_pairs={{0,8},{1,9},{2,10},{3,11},{4,12},{5,13},{6,14},{7,15},{8,0},{9,1},... | collective-permute-start | bytes 1179656 | tf_op jit(solution)/shard_map/ppermute | solution.py:27
  203.4 10.8 %collective-permute-start.28 = (bf16[2,2,64,768]{3,2,0,1:T(8,128)(2,1)S(1)}, bf16[2,2,64,768]{3,2,0,1:T(8,128)(2,1)S(1)}, u32[]{:S(2)}, u32[]{:S(2)}) collective-permute-start(bf16[2,2,64,768]{3,2,0,1:T(8,128)(2,1)S(1)} %fusion.34), channel_id=1, source_target_pairs={{0,2},{1,3},{2,0},{3,1},{4,6},{5,7},{6,4},{7,5},{8,10},{9,11},{10,... | collective-permute-start | bytes 1179656 | tf_op jit(solution)/shard_map/ppermute | solution.py:27
  212.9 7.3 %collective-permute-start.25 = (bf16[2,64,768]{2,1,0:T(8,128)(2,1)S(1)}, bf16[2,64,768]{2,1,0:T(8,128)(2,1)S(1)}, u32[]{:S(2)}, u32[]{:S(2)}) collective-permute-start(bf16[2,64,768]{2,1,0:T(8,128)(2,1)S(1)} %fusion.39), channel_id=1, source_target_pairs={{0,16},{1,17},{2,18},{3,19},{4,20},{5,21},{6,22},{7,23},{8,24},{9,... | collective-permute-start | bytes 589832 | tf_op jit(solution)/shard_map/ppermute | solution.py:27
  214.4 8.2 %collective-permute-start.29 = (bf16[2,64,768]{2,1,0:T(8,128)(2,1)S(1)}, bf16[2,64,768]{2,1,0:T(8,128)(2,1)S(1)}, u32[]{:S(2)}, u32[]{:S(2)}) collective-permute-start(bf16[2,64,768]{2,1,0:T(8,128)(2,1)S(1)} %fusion.40), channel_id=1, source_target_pairs={{0,4},{1,5},{2,6},{3,7},{4,0},{5,1},{6,2},{7,3},{8,12},{9,13},{10,... | collective-permute-start | bytes 589832 | tf_op jit(solution)/shard_map/ppermute | solution.py:27
  220.3 6.2 %collective-permute-start.26 = (bf16[64,768]{1,0:T(8,128)(2,1)S(1)}, bf16[64,768]{1,0:T(8,128)(2,1)S(1)}, u32[]{:S(2)}, u32[]{:S(2)}) collective-permute-start(bf16[64,768]{1,0:T(8,128)(2,1)S(1)} %fusion.42), channel_id=1, source_target_pairs={{0,4},{1,5},{2,6},{3,7},{4,0},{5,1},{6,2},{7,3},{8,12},{9,13},{10,... | collective-permute-start | bytes 294920 | tf_op jit(solution)/shard_map/ppermute | solution.py:27
  (20 other events, 137.1 us)
